TPU v7x, 768 devices: a whole 4x8x12 slice. The times are simulated.
768 devices in a mesh: branch: 2 (over y_lo), hidden: 48 (over x, z), width: 8 (over y_hi, core).
Axes of the slice: x: 4, y: 8 (y_hi: 4, y_lo: 2; y = y_hi * 2 + y_lo), z: 12, core: 2. Of those that a mesh axis runs over, the one named last changes fastest.
Arguments:
- rows: bfloat16 [2, 288, 4096], P(None, ('branch', 'hidden'), 'width'), may hold values from -6 to 6
- cotangent: bfloat16 [2, 288, 4096], P(None, ('branch', 'hidden'), 'width'), may hold values from -6 to 6
- labels: int32 [2, 288], P(None, ('branch', 'hidden')), may hold values from 0 to 1, as said below
- counts: int32 [2, 96], P(None, ('branch', 'hidden')), may hold values from 1 to 3, as said below
- gate_weight: bfloat16 [2, 4096, 12288], P('branch', 'width', 'hidden'), may hold values from -0.09375 to 0.09375
- up_weight: bfloat16 [2, 4096, 12288], P('branch', 'width', 'hidden'), may hold values from -0.09375 to 0.09375
- down_weight: bfloat16 [2, 12288, 4096], P('branch', 'hidden', 'width'), may hold values from -0.0546875 to 0.0546875
Outputs:
- output: bfloat16 [2, 288, 4096], P(None, ('branch', 'hidden'), 'width')
- grad_rows: bfloat16 [2, 288, 4096], P(None, ('branch', 'hidden'), 'width')
- grad_gate: float32 [2, 4096, 12288], P('branch', 'width', 'hidden')
- grad_up: float32 [2, 4096, 12288], P('branch', 'width', 'hidden')
- grad_down: float32 [2, 12288, 4096], P('branch', 'hidden', 'width')
Inputs may be any that keep to these rules, and one draw needn't show every extreme that they name: The first counts rows of an owner are used; one owner in each microbatch uses all 3. `labels`: among the used rows of one owner in one microbatch at most 2 carry the same label; some owner in each microbatch has exactly 2 text rows.
All inputs are finite; a program needn't handle non-finite values.
Results may differ from a plain program's by a relative error of at most 0.0049.
Values may be sent and summed in bfloat16 or wider, within the bound.
No kernel may reach another device: no remote copies, remote signals or barrier semaphores. Data moves between devices by JAX's collectives and lax.ppermute only.
A program may use at most 32 MiB of HBM per device.

v0:
```python
import jax
import jax.numpy as jnp
from jax import lax
from jax.sharding import PartitionSpec as P

CAP = 2


def slot_table(labels, counts):
    groups_now, rows_dev = labels.shape
    position = lax.broadcasted_iota(jnp.int32, (groups_now, rows_dev), 1)
    valid = position < counts
    slot_index = lax.broadcasted_iota(jnp.int32, (groups_now, CAP, rows_dev), 1)
    tables = []
    for label_value in (0, 1):
        chosen = valid & (labels == label_value)
        ranking = jnp.cumsum(chosen.astype(jnp.int32), axis=1) - 1
        tables.append(
            (chosen[:, None, :] & (ranking[:, None, :] == slot_index)).astype(jnp.bfloat16)
        )
    return jnp.stack(tables, axis=1)


def contract_rows(left, right):
    return lax.dot_general(
        left, right, (((0,), (0,)), ((), ())), preferred_element_type=jnp.float32
    )


def contract_cols(left, right):
    return lax.dot_general(
        left, right, (((1,), (1,)), ((), ())), preferred_element_type=jnp.float32
    )


def activate(gate, up_value, dhid):
    sigma = jax.nn.sigmoid(gate)
    silu = gate * sigma
    hidden = (silu * up_value).astype(jnp.bfloat16)
    dgate = (dhid * up_value * sigma * (1.0 + gate * (1.0 - sigma))).astype(jnp.bfloat16)
    dup = (dhid * silu).astype(jnp.bfloat16)
    return (hidden, dgate, dup)


def process(rows, cotangent, labels, counts, gate_weight, up_weight, down_weight):
    groups_now = rows.shape[0]
    width_part = rows.shape[2]
    table = slot_table(labels, counts)
    send_rows = jnp.einsum(
        "glsp,gpd->glsd", table, rows, preferred_element_type=jnp.float32
    ).astype(jnp.bfloat16)
    send_cot = jnp.einsum(
        "glsp,gpd->glsd", table, cotangent, preferred_element_type=jnp.float32
    ).astype(jnp.bfloat16)
    routed_rows, routed_cot = (
        lax.all_to_all(send_rows, "branch", split_axis=1, concat_axis=1, tiled=True),
        lax.all_to_all(send_cot, "branch", split_axis=1, concat_axis=1, tiled=True),
    )
    all_rows, all_cot = (
        lax.all_gather(routed_rows, "hidden", axis=1, tiled=True),
        lax.all_gather(routed_cot, "hidden", axis=1, tiled=True),
    )
    slot_count = all_rows.shape[1]
    flat_rows = all_rows.reshape(-1, width_part)
    flat_cot = all_cot.reshape(-1, width_part)
    gate_part = jnp.dot(flat_rows, gate_weight[0], preferred_element_type=jnp.float32)
    up_part = jnp.dot(flat_rows, up_weight[0], preferred_element_type=jnp.float32)
    dhid_part = contract_cols(flat_cot, down_weight[0])
    gate_share, up_share, dhid_share = (
        lax.psum_scatter(gate_part, "width", scatter_dimension=1, tiled=True),
        lax.psum_scatter(up_part, "width", scatter_dimension=1, tiled=True),
        lax.psum_scatter(dhid_part, "width", scatter_dimension=1, tiled=True),
    )
    hidden_share, dgate_share, dup_share = activate(gate_share, up_share, dhid_share)
    hidden, dgate, dup = (
        lax.all_gather(hidden_share, "width", axis=1, tiled=True),
        lax.all_gather(dgate_share, "width", axis=1, tiled=True),
        lax.all_gather(dup_share, "width", axis=1, tiled=True),
    )
    out_part = jnp.dot(hidden, down_weight[0], preferred_element_type=jnp.float32)
    back_part = contract_cols(dgate, gate_weight[0]) + contract_cols(dup, up_weight[0])
    grad_gate = contract_rows(flat_rows, dgate)
    grad_up = contract_rows(flat_rows, dup)
    grad_down = contract_rows(hidden, flat_cot)
    summed_out, summed_back = (
        lax.psum_scatter(
            out_part.reshape(groups_now, slot_count, CAP, width_part),
            "hidden",
            scatter_dimension=1,
            tiled=True,
        ),
        lax.psum_scatter(
            back_part.reshape(groups_now, slot_count, CAP, width_part),
            "hidden",
            scatter_dimension=1,
            tiled=True,
        ),
    )
    result_out, result_back = (
        lax.all_to_all(
            summed_out.astype(jnp.bfloat16), "branch", split_axis=1, concat_axis=1, tiled=True
        ),
        lax.all_to_all(
            summed_back.astype(jnp.bfloat16), "branch", split_axis=1, concat_axis=1, tiled=True
        ),
    )
    output = jnp.einsum(
        "glsp,glsd->gpd", table, result_out, preferred_element_type=jnp.float32
    ).astype(jnp.bfloat16)
    grad_rows = jnp.einsum(
        "glsp,glsd->gpd", table, result_back, preferred_element_type=jnp.float32
    ).astype(jnp.bfloat16)
    return (output, grad_rows, grad_gate, grad_up, grad_down)


def shards(rows, cotangent, labels, counts, gate_weight, up_weight, down_weight):
    outputs = []
    row_grads = []
    grad_gate = None
    for micro in range(rows.shape[0]):
        pieces = process(
            rows[micro : micro + 1],
            cotangent[micro : micro + 1],
            labels[micro : micro + 1],
            counts[micro : micro + 1],
            gate_weight,
            up_weight,
            down_weight,
        )
        outputs.append(pieces[0])
        row_grads.append(pieces[1])
        if grad_gate is None:
            grad_gate, grad_up, grad_down = (pieces[2], pieces[3], pieces[4])
        else:
            grad_gate = grad_gate + pieces[2]
            grad_up = grad_up + pieces[3]
            grad_down = grad_down + pieces[4]
    output = jnp.concatenate(outputs, axis=0)
    grad_rows = jnp.concatenate(row_grads, axis=0)
    return (output, grad_rows, grad_gate[None], grad_up[None], grad_down[None])


def solution(mesh):
    return jax.shard_map(
        shards,
        mesh=mesh,
        in_specs=(
            P(None, ("branch", "hidden"), "width"),
            P(None, ("branch", "hidden"), "width"),
            P(None, ("branch", "hidden")),
            P(None, ("branch", "hidden")),
            P("branch", "width", "hidden"),
            P("branch", "width", "hidden"),
            P("branch", "hidden", "width"),
        ),
        out_specs=(
            P(None, ("branch", "hidden"), "width"),
            P(None, ("branch", "hidden"), "width"),
            P("branch", "width", "hidden"),
            P("branch", "width", "hidden"),
            P("branch", "hidden", "width"),
        ),
        check_vma=False,
    )
```

profile of v0, /device:TPU:8, one launch (start us, length us, event | category | flops | bytes accessed | tf_op | source)
XLA Modules:
  0.0 682.0 jit_solution(14340571845701187524)
XLA Ops:
  7.2 1.3 fusion.47
  9.2 1.3 convert_bitcast_fusion.3
  11.9 12.8 %all-to-all-start = ((bf16[1,2,2,512]{3,2,0,1:T(2,128)(2,1)}), bf16[1,2,2,512]{3,2,0,1:T(2,128)(2,1)S(1)}, u32[]{:S(2)}, u32[]{:S(2)}) async-start(bf16[1,2,2,512]{3,2,0,1:T(2,128)(2,1)} %fusion.11), calls=%async_computation | async-start | bytes 8192 | tf_op jit(solution)/shard_map/all_to_all | solution.py:56
  26.5 5.2 all-to-all-start.4
  31.7 63.4 %all_gather.30 = bf16[1,96,2,512]{3,2,0,1:T(2,128)(2,1)S(1)} all-gather(bf16[1,2,2,512]{3,2,0,1:T(2,128)(2,1)S(1)} %all-to-all-done), channel_id=1, replica_groups=mesh['branch'=2,'hidden'=48,'width'=8] {'hidden'}, dimensions={1}, use_global_device_ids=true | all-gather | bytes 200704 | tf_op jit(solution)/shard_map/all_gather | solution.py:60
  98.2 61.9 %all_gather.34 = bf16[1,96,2,512]{3,2,0,1:T(2,128)(2,1)S(1)} all-gather(bf16[1,2,2,512]{3,2,0,1:T(2,128)(2,1)S(1)} %all-to-all-done.4), channel_id=1, replica_groups=mesh['branch'=2,'hidden'=48,'width'=8] {'hidden'}, dimensions={1}, use_global_device_ids=true | all-gather | bytes 200704 | tf_op jit(solution)/shard_map/all_gather | solution.py:61
  161.4 4.8 all_to_all.40
  166.2 60.2 %all_gather.32 = bf16[1,96,2,512]{3,2,0,1:T(2,128)(2,1)S(1)} all-gather(bf16[1,2,2,512]{3,2,0,1:T(2,128)(2,1)S(1)} %all_to_all.40), channel_id=1, replica_groups=mesh['branch'=2,'hidden'=48,'width'=8] {'hidden'}, dimensions={1}, use_global_device_ids=true | all-gather | bytes 200704 | tf_op jit(solution)/shard_map/all_gather | solution.py:60
  229.3 5.2 all-to-all-start.6
  234.6 1.3 dynamic-slice
  236.5 61.9 %all_gather.37 = bf16[1,96,2,512]{3,2,0,1:T(2,128)(2,1)S(1)} all-gather(bf16[1,2,2,512]{3,2,0,1:T(2,128)(2,1)S(1)} %all-to-all-done.6), channel_id=1, replica_groups=mesh['branch'=2,'hidden'=48,'width'=8] {'hidden'}, dimensions={1}, use_global_device_ids=true | all-gather | bytes 200704 | tf_op jit(solution)/shard_map/all_gather | solution.py:61
  300.4 16.7 %all_gather.35 = bf16[192,256]{0,1:T(8,128)(2,1)S(1)} all-gather(bf16[192,32]{0,1:T(8,128)(2,1)S(1)} %get-tuple-element.33), channel_id=1, replica_groups=mesh['branch'=2,'hidden'=48,'width'=8] {'width'}, dimensions={1}, use_global_device_ids=true | all-gather | bytes 110592 | tf_op jit(solution)/shard_map/all_gather | solution.py:77
  317.3 14.6 %all_gather.36 = bf16[192,256]{0,1:T(8,128)(2,1)S(1)} all-gather(bf16[192,32]{0,1:T(8,128)(2,1)S(1)} %get-tuple-element.32), channel_id=1, replica_groups=mesh['branch'=2,'hidden'=48,'width'=8] {'width'}, dimensions={1}, use_global_device_ids=true | all-gather | bytes 110592 | tf_op jit(solution)/shard_map/all_gather | solution.py:78
  332.7 14.6 %all_gather.31 = bf16[192,256]{0,1:T(8,128)(2,1)S(1)} all-gather(bf16[192,32]{0,1:T(8,128)(2,1)S(1)} %get-tuple-element.34), channel_id=1, replica_groups=mesh['branch'=2,'hidden'=48,'width'=8] {'width'}, dimensions={1}, use_global_device_ids=true | all-gather | bytes 110592 | tf_op jit(solution)/shard_map/all_gather | solution.py:76
  349.4 6.2 reduce-scatter.21.cloned.1.call-done
  356.4 14.6 %all_gather.38 = bf16[192,256]{0,1:T(8,128)(2,1)S(1)} all-gather(bf16[192,32]{0,1:T(8,128)(2,1)S(1)} %get-tuple-element.36), channel_id=1, replica_groups=mesh['branch'=2,'hidden'=48,'width'=8] {'width'}, dimensions={1}, use_global_device_ids=true | all-gather | bytes 110592 | tf_op jit(solution)/shard_map/all_gather | solution.py:77
  371.6 14.5 %all_gather.39 = bf16[192,256]{0,1:T(8,128)(2,1)S(1)} all-gather(bf16[192,32]{0,1:T(8,128)(2,1)S(1)} %get-tuple-element.35), channel_id=1, replica_groups=mesh['branch'=2,'hidden'=48,'width'=8] {'width'}, dimensions={1}, use_global_device_ids=true | all-gather | bytes 110592 | tf_op jit(solution)/shard_map/all_gather | solution.py:78
  388.4 1.6 reshape.541
  389.9 1.9 convolution_bitcast_fusion.1
  391.8 15.6 %all_gather.33 = bf16[192,256]{0,1:T(8,128)(2,1)} all-gather(bf16[192,32]{0,1:T(8,128)(2,1)S(1)} %get-tuple-element.37), channel_id=1, replica_groups=mesh['branch'=2,'hidden'=48,'width'=8] {'width'}, dimensions={1}, use_global_device_ids=true | all-gather | bytes 110592 | tf_op jit(solution)/shard_map/all_gather | solution.py:76
  407.4 1.6 copy.41
  409.1 1.6 reshape.548
  410.6 1.8 convolution_bitcast_fusion
  412.5 230.7 %all-reduce.6 = (bf16[1,96,2,512]{3,1,2,0:T(8,128)(2,1)S(1)}, bf16[1,96,2,512]{3,1,2,0:T(8,128)(2,1)}, bf16[1,96,2,512]{3,2,1,0:T(2,128)(2,1)}, bf16[1,96,2,512]{3,2,1,0:T(2,128)(2,1)}) all-reduce(f32[1,96,2,512]{3,1,2,0:T(8,128)} %convolution_bitcast_fusion, ...), channel_id=7, replica_groups=mesh['branch'=2,'hidden'=48,'width'=8] {'hidden'}, use_global_device_ids=true, to_apply=%region_9.10.clone | all-reduce | flops 393216 | bytes 2359296
  643.2 1.3 fusion.39
  644.5 4.5 all-to-all-start.5
  648.9 1.3 fusion.40
  655.3 3.3 all-to-all-start.7
  658.8 1.6 all-to-all-done.7
  660.4 5.2 all-to-all-start.1
  665.8 1.6 all-to-all-done.1
  667.4 5.2 all-to-all-start.3
  (95 shorter events, 27.8 us)
Async XLA Ops:
  7.2 88.0 %copy-start = (bf16[1,512,256]{2,1,0:T(8,128)(2,1)S(1)}, bf16[1,512,256]{2,1,0:T(8,128)(2,1)}, u32[]{:S(2)}) copy-start(bf16[1,512,256]{2,1,0:T(8,128)(2,1)} %param.11) | copy-start | bytes 786436
  8.5 0.7 copy-start.9
  10.5 0.7 copy-start.7
  11.9 12.8 %copy-start.8 = (bf16[2,3,512]{2,0,1:T(2,128)(2,1)S(1)}, bf16[2,3,512]{2,0,1:T(2,128)(2,1)}, u32[]{:S(2)}) copy-start(bf16[2,3,512]{2,0,1:T(2,128)(2,1)} %param.8) | copy-start | bytes 18436
  11.9 14.6 %all-to-all-start = ((bf16[1,2,2,512]{3,2,0,1:T(2,128)(2,1)}), bf16[1,2,2,512]{3,2,0,1:T(2,128)(2,1)S(1)}, u32[]{:S(2)}, u32[]{:S(2)}) async-start(bf16[1,2,2,512]{3,2,0,1:T(2,128)(2,1)} %fusion.11), calls=%async_computation | async-start | bytes 8192 | tf_op jit(solution)/shard_map/all_to_all | solution.py:56
  26.5 71.7 %all-to-all-start.4 = ((bf16[1,2,2,512]{3,2,0,1:T(2,128)(2,1)}), bf16[1,2,2,512]{3,2,0,1:T(2,128)(2,1)S(1)}, u32[]{:S(2)}, u32[]{:S(2)}) async-start(bf16[1,2,2,512]{3,2,0,1:T(2,128)(2,1)} %fusion.13), calls=%async_computation.8 | async-start | bytes 8192 | tf_op jit(solution)/shard_map/all_to_all | solution.py:57
  31.7 267.8 %reduce-scatter.11.cloned.1.call-start = ((), (), s32[]{:S(2)}) async-start(), calls=%async_computation.14 | async-start | bytes 294912 | tf_op jit(solution)/shard_map/reduce_scatter | solution.py:70
  96.2 0.9 copy-start.2
  96.2 203.3 %reduce-scatter.13.cloned.1.call-start = ((), (), s32[]{:S(2)}) async-start(), calls=%async_computation.15 | async-start | bytes 294912 | tf_op jit(solution)/shard_map/reduce_scatter | solution.py:71
  98.1 201.4 %reduce-scatter.19.cloned.1.call-start = ((), (), s32[]{:S(2)}) async-start(), calls=%async_computation.18 | async-start | bytes 294912 | tf_op jit(solution)/shard_map/reduce_scatter | solution.py:72
  98.2 62.0 %copy-start.1 = (bf16[1,256,512]{2,1,0:T(8,128)(2,1)S(1)}, bf16[1,256,512]{2,1,0:T(8,128)(2,1)}, u32[]{:S(2)}) copy-start(bf16[1,256,512]{2,1,0:T(8,128)(2,1)} %param.13) | copy-start | bytes 786436
  161.2 188.1 %reduce-scatter.15.cloned.1.call-start = ((), (), s32[]{:S(2)}) async-start(), calls=%async_computation.16 | async-start | bytes 294912 | tf_op jit(solution)/shard_map/reduce_scatter | solution.py:70
  227.5 121.8 %reduce-scatter.17.cloned.1.call-start = ((), (), s32[]{:S(2)}) async-start(), calls=%async_computation.17 | async-start | bytes 294912 | tf_op jit(solution)/shard_map/reduce_scatter | solution.py:71
  229.3 7.2 %all-to-all-start.6 = ((bf16[1,2,2,512]{3,2,0,1:T(2,128)(2,1)}), bf16[1,2,2,512]{3,2,0,1:T(2,128)(2,1)S(1)}, u32[]{:S(2)}, u32[]{:S(2)}) async-start(bf16[1,2,2,512]{3,2,0,1:T(2,128)(2,1)} %fusion.14), calls=%async_computation.11 | async-start | bytes 8192 | tf_op jit(solution)/shard_map/all_to_all | solution.py:57
  234.6 121.0 %reduce-scatter.21.cloned.1.call-start = ((), (), s32[]{:S(2)}) async-start(), calls=%async_computation.19 | async-start | bytes 294912 | tf_op jit(solution)/shard_map/reduce_scatter | solution.py:72
  347.2 0.7 copy-start.3
  371.0 0.6 copy-start.5
  644.5 10.8 %all-to-all-start.5 = ((bf16[1,2,2,512]{3,2,0,1:T(2,128)(2,1)}), bf16[1,2,2,512]{3,2,0,1:T(2,128)(2,1)S(1)}, u32[]{:S(2)}, u32[]{:S(2)}) async-start(bf16[1,2,2,512]{3,2,0,1:T(2,128)(2,1)} %fusion.39), calls=%async_computation.10 | async-start | bytes 8192 | tf_op jit(solution)/shard_map/all_to_all | solution.py:103
  650.9 1.1 copy-start.6
  652.0 1.1 copy-start.4
  655.3 5.1 all-to-all-start.7
  660.4 7.0 %all-to-all-start.1 = ((bf16[1,2,2,512]{3,2,0,1:T(2,128)(2,1)}), bf16[1,2,2,512]{3,2,0,1:T(2,128)(2,1)S(1)}, u32[]{:S(2)}, u32[]{:S(2)}) async-start(bf16[1,2,2,512]{3,2,0,1:T(2,128)(2,1)} %copy.38), calls=%async_computation.3 | async-start | bytes 8192 | tf_op jit(solution)/shard_map/all_to_all | solution.py:100
  667.4 7.0 %all-to-all-start.3 = ((bf16[1,2,2,512]{3,2,0,1:T(2,128)(2,1)}), bf16[1,2,2,512]{3,2,0,1:T(2,128)(2,1)S(1)}, u32[]{:S(2)}, u32[]{:S(2)}) async-start(bf16[1,2,2,512]{3,2,0,1:T(2,128)(2,1)} %copy.43), calls=%async_computation.7 | async-start | bytes 8192 | tf_op jit(solution)/shard_map/all_to_all | solution.py:100
Sparse Core Ops, SparseCore 0:
  96.3 36.7 reduce-scatter.10
  136.2 41.0 reduce-scatter.12
  180.4 41.0 reduce-scatter.18
  227.7 38.4 reduce-scatter.14
  269.6 41.1 reduce-scatter.16
  314.4 41.1 reduce-scatter.20
where the time goes:
time: 683 us; the launch traced here: 682 us
  blocking collectives  573 us (84%)
  starting transfers between devices  41.6 us (6%)
  matrix products  19.1 us (3%)
  local copies, waits for them, and re-layouts  17.9 us (3%)
  between operations  15 us (2%)
  waiting for transfers between devices  11.2 us (2%)
    unnamed x1, blocking collectives  231 us
    all_gather x2, blocking collectives, process(): lax.all_gather(routed_cot, 'hidden', axis=1, tiled=True)  124 us
    all_gather x2, blocking collectives, process(): lax.all_gather(routed_rows, 'hidden', axis=1, tiled=True)  124 us
    all_gather x2, blocking collectives, process(): lax.all_gather(dgate_share, 'width', axis=1, tiled=True)  31.2 us
    all_gather x2, blocking collectives, process(): lax.all_gather(hidden_share, 'width', axis=1, tiled=True)  30.2 us
    all_gather x2, blocking collectives, process(): lax.all_gather(dup_share, 'width', axis=1, tiled=True)  29.1 us
  transfers between devices with their start and end apart: 13, of which 5 were waited for; matrix products, arithmetic and copies ran while one was open for 3% of the time, Pallas kernels for 0%

commit v1 on v0

v1 whole, which is shorter than its diff:
```python
import jax
import jax.numpy as jnp
from jax import lax
from jax.sharding import PartitionSpec as P

CAP = 2
BF16 = jnp.bfloat16
F32 = jnp.float32
OWNERS = ("branch", "hidden")


def slot_masks(labels, counts):
    masks = []
    for branch in (0, 1):
        chosen = [
            (counts[:, 0:1] > p) & (labels[:, p : p + 1] == branch)
            for p in range(labels.shape[1])
        ]
        slots = []
        for s in range(CAP):
            picks = []
            for p in range(labels.shape[1]):
                rank = sum((c.astype(jnp.int32) for c in chosen[:p]), jnp.int32(0))
                picks.append(chosen[p] & (rank == s))
            slots.append(picks)
        masks.append(slots)
    return masks


def contract(left, right, left_dim, right_dim):
    return lax.dot_general(
        left, right, (((left_dim,), (right_dim,)), ((), ())), preferred_element_type=F32
    )


def shards(rows, cotangent, labels, counts, gate_weight, up_weight, down_weight):
    gate_weight, up_weight, down_weight = gate_weight[0], up_weight[0], down_weight[0]
    mb, row_dev, width_part = rows.shape
    hidden_size = lax.axis_size("hidden")
    width_size = lax.axis_size("width")
    owners = 2 * hidden_size
    per_owner = mb * CAP
    slots = owners * per_owner
    units = gate_weight.shape[1]
    masks = slot_masks(labels, counts)

    zero = jnp.zeros((), BF16)
    packed = []
    for branch in (0, 1):
        for source in (rows, cotangent):
            for s in range(CAP):
                value = zero
                for p in range(row_dev):
                    value = jnp.where(masks[branch][s][p], source[:, p, :], value)
                packed.append(value)
    packed = jnp.stack(packed).reshape(2, 1, 2 * CAP * mb, width_part)
    send = jnp.broadcast_to(packed, (2, hidden_size, 2 * CAP * mb, width_part))
    recv = lax.all_to_all(
        send.reshape(owners, 2 * per_owner, width_part), OWNERS, 0, 0, tiled=True
    )
    flat_rows = recv[:, :per_owner].reshape(slots, width_part)
    flat_cot = recv[:, per_owner:].reshape(slots, width_part)

    parts = jnp.stack(
        [
            contract(gate_weight, flat_rows, 0, 1),
            contract(up_weight, flat_rows, 0, 1),
            contract(down_weight, flat_cot, 1, 1),
        ]
    ).astype(BF16)
    parts = parts.reshape(3, width_size, units // width_size, slots).transpose(1, 0, 2, 3)
    parts = lax.all_to_all(parts, "width", 0, 0, tiled=True)
    gate, up_value, dhid = jnp.sum(parts.astype(F32), axis=0)
    sigma = jax.nn.sigmoid(gate)
    silu = gate * sigma
    share = jnp.stack(
        [
            (silu * up_value).astype(BF16),
            (dhid * up_value * sigma * (1.0 + gate * (1.0 - sigma))).astype(BF16),
            (dhid * silu).astype(BF16),
        ]
    )
    every = lax.all_gather(share, "width", axis=0, tiled=False)
    hidden = every[:, 0].reshape(units, slots)
    dgate = every[:, 1].reshape(units, slots)
    dup = every[:, 2].reshape(units, slots)

    out_part = contract(hidden, down_weight, 0, 0)
    back_part = contract(dgate, gate_weight, 0, 1) + contract(dup, up_weight, 0, 1)
    result = jnp.stack(
        [
            out_part.astype(BF16).reshape(owners, per_owner, width_part),
            back_part.astype(BF16).reshape(owners, per_owner, width_part),
        ],
        axis=1,
    ).reshape(owners, 2 * per_owner, width_part)
    result = lax.all_to_all(result, OWNERS, 0, 0, tiled=True)
    grad_gate = contract(flat_rows, dgate, 0, 1)
    grad_up = contract(flat_rows, dup, 0, 1)
    grad_down = contract(hidden, flat_cot, 1, 0)
    result = jnp.sum(
        result.reshape(2, hidden_size, 2, CAP, mb, width_part).astype(F32), axis=1
    )
    result = lax.optimization_barrier(result).astype(BF16)
    finals = []
    for which in (0, 1):
        per_row = []
        for p in range(row_dev):
            value = zero
            for branch in (0, 1):
                for s in range(CAP):
                    value = jnp.where(masks[branch][s][p], result[branch, which, s], value)
            per_row.append(value)
        finals.append(jnp.stack(per_row, axis=1))
    return (finals[0], finals[1], grad_gate[None], grad_up[None], grad_down[None])


def solution(mesh):
    owner_rows = P(None, OWNERS, "width")
    return jax.shard_map(
        shards,
        mesh=mesh,
        in_specs=(
            owner_rows,
            owner_rows,
            P(None, OWNERS),
            P(None, OWNERS),
            P("branch", "width", "hidden"),
            P("branch", "width", "hidden"),
            P("branch", "hidden", "width"),
        ),
        out_specs=(
            owner_rows,
            owner_rows,
            P("branch", "width", "hidden"),
            P("branch", "width", "hidden"),
            P("branch", "hidden", "width"),
        ),
        check_vma=False,
    )
```

time: 683 us -> 153 us (0.22)
  blocking collectives: 573 us -> 93.8 us
  starting transfers between devices: 41.6 us -> 8.13 us
  waiting for transfers between devices: 11.2 us -> 31.5 us
  between operations: 15 us -> 0.83 us
  matrix products: 19.1 us -> 5.26 us
  local copies, waits for them, and re-layouts: 17.9 us -> 4.4 us
    all_gather x10 -> x1, blocking collectives: 338 us -> 15.1 us  [shards(): every = lax.all_gather(share, 'width', axis=0, tiled=False)]
    unnamed x1 -> x0, blocking collectives: 231 us -> none
    all_to_all x1 -> x2, blocking collectives: 4.85 us -> 78.7 us  [the longest x1 54.1 us: shards(): lax.all_to_all(send.reshape(owners, 2 * per_owner, width_part), OWNERS, 0...]
    all_to_all x7 -> x1, starting transfers between devices: 41.5 us -> 8.13 us  [shards(): result = lax.all_to_all(result, OWNERS, 0, 0, tiled=True)]
    all_to_all x7 -> x1, waiting for transfers between devices: 4.82 us -> 31.5 us  [shards(): result = lax.all_to_all(result, OWNERS, 0, 0, tiled=True)]
    dot_general x26 -> x9, matrix products: 19.1 us -> 5.26 us  [contract(): lax.dot_general(left, right, (((left_dim,), (right_dim,)), ((), ())), pre...]
  transfers between devices with their start and end apart: 13 -> 1, of which waited for: 5 -> 1; matrix products, arithmetic and copies ran while one was open for 3% -> 2% of each run, Pallas kernels for 0% -> 0%
where the time goes in v1:
time: 153 us
  blocking collectives  93.8 us (61%)
  waiting for transfers between devices  31.5 us (21%)
  other arithmetic  8.73 us (6%)
  starting transfers between devices  8.13 us (5%)
  matrix products  5.26 us (3%)
  local copies, waits for them, and re-layouts  4.4 us (3%)
    all_to_all x1, blocking collectives, shards(): lax.all_to_all(send.reshape(owners, 2 * per_owner, width_part), OWNERS, 0...  54.1 us
    all_to_all x1, waiting for transfers between devices, shards(): result = lax.all_to_all(result, OWNERS, 0, 0, tiled=True)  31.5 us
    all_to_all x1, blocking collectives, shards(): parts = lax.all_to_all(parts, 'width', 0, 0, tiled=True)  24.6 us
    all_gather x1, blocking collectives, shards(): every = lax.all_gather(share, 'width', axis=0, tiled=False)  15.1 us
    all_to_all x1, starting transfers between devices, shards(): result = lax.all_to_all(result, OWNERS, 0, 0, tiled=True)  8.13 us
    unnamed x8, other arithmetic  5.62 us
    dot_general x9, matrix products, contract(): lax.dot_general(left, right, (((left_dim,), (right_dim,)), ((), ())), pre...  5.26 us
  transfers between devices with their start and end apart: 1, of which 1 were waited for; matrix products, arithmetic and copies ran while one was open for 2% of the time, Pallas kernels for 0%

profile of v1, /device:TPU:8, one launch (start us, length us, event | category | flops | bytes accessed | tf_op | source)
XLA Modules:
  0.0 152.6 jit_solution(16795581792489276773)
XLA Ops:
  0.6 0.9 fusion.12
  1.8 0.7 and_bitcast_fusion.4
  2.5 0.7 and_bitcast_fusion.3
  3.1 0.8 constant_dynamic-update-slice_fusion.7
  3.9 0.8 constant_dynamic-update-slice_fusion.6
  4.7 0.8 constant_dynamic-update-slice_fusion.5
  5.5 0.8 constant_dynamic-update-slice_fusion.4
  6.3 0.8 constant_dynamic-update-slice_fusion.3
  7.1 0.8 constant_dynamic-update-slice_fusion.2
  7.8 0.8 constant_dynamic-update-slice_fusion.1
  8.6 0.8 constant_dynamic-update-slice_fusion
  9.5 54.1 %all_to_all.15 = bf16[96,8,512]{2,1,0:T(8,128)(2,1)S(1)} all-to-all(bf16[96,8,512]{2,1,0:T(8,128)(2,1)S(1)} %bitcast.158), channel_id=1, replica_groups=mesh['branch'=2,'hidden'=48,'width'=8] {'branch','hidden'}, dimensions={0} | all-to-all | bytes 1572864 | tf_op jit(solution)/shard_map/all_to_all | solution.py:58
  63.6 0.3 fusion.9
  64.0 0.3 convolution_convert_fusion.3
  64.3 0.5 copy-done.1
  64.8 0.3 convolution_convert_fusion.2
  65.3 0.5 copy-done.2
  65.8 0.3 convolution_convert_fusion.1
  66.2 24.6 %all_to_all.16 = bf16[8,3,32,384]{3,2,1,0:T(8,128)(2,1)S(1)} all-to-all(bf16[8,3,32,384]{3,2,1,0:T(8,128)(2,1)S(1)} %maximum_bitcast_fusion), channel_id=1, replica_groups=mesh['branch'=2,'hidden'=48,'width'=8] {'width'}, dimensions={0} | all-to-all | bytes 1179648 | tf_op jit(solution)/shard_map/all_to_all | solution.py:72
  90.9 15.1 %all-gather = bf16[24,32,384]{2,1,0:T(8,128)(2,1)S(1)} all-gather(bf16[3,32,384]{2,1,0:T(8,128)(2,1)S(1)} %pad_maximum_fusion.1), channel_id=2, replica_groups=mesh['branch'=2,'hidden'=48,'width'=8] {'width'}, dimensions={0}, use_global_device_ids=true | all-gather | bytes 663552 | tf_op jit(solution)/shard_map/all_gather | solution.py:83
  106.0 0.3 fusion.5
  106.4 0.3 fusion
  106.8 0.3 convolution_convert_fusion
  107.4 1.3 copy.136
  108.7 8.1 %all-to-all-start.2 = ((bf16[96,8,512]{2,1,0:T(8,128)(2,1)}), bf16[96,8,512]{2,1,0:T(8,128)(2,1)S(1)}, u32[]{:S(2)}, u32[]{:S(2)}) async-start(bf16[96,8,512]{2,1,0:T(8,128)(2,1)} %copy.136), calls=%async_computation.2 | async-start | bytes 1572864 | tf_op jit(solution)/shard_map/all_to_all | solution.py:97
  116.9 1.1 convolution_bitcast_fusion
  118.0 1.1 convolution_bitcast_fusion.1
  119.1 1.1 convolution_bitcast_fusion.2
  120.2 31.5 %all-to-all-done.2 = bf16[96,8,512]{2,1,0:T(8,128)(2,1)S(1)} async-done(((bf16[96,8,512]{2,1,0:T(8,128)(2,1)}), bf16[96,8,512]{2,1,0:T(8,128)(2,1)S(1)}, u32[]{:S(2)}, u32[]{:S(2)}) %all-to-all-start.2) | async-done | bytes 786464 | tf_op jit(solution)/shard_map/all_to_all | solution.py:97
  151.7 0.1 convert_reduce_fusion
  151.9 0.1 broadcast_select_fusion.11
  152.0 0.6 pad_maximum_fusion.2
  (23 shorter events, 1.3 us)
Async XLA Ops:
  0.6 63.3 %copy-start = (bf16[1,512,256]{2,1,0:T(8,128)(2,1)S(1)}, bf16[1,512,256]{2,1,0:T(8,128)(2,1)}, u32[]{:S(2)}) copy-start(bf16[1,512,256]{2,1,0:T(8,128)(2,1)} %param.11) | copy-start | bytes 786436
  63.9 1.0 copy-start.1
  64.8 0.9 copy-start.2
  108.7 43.0 %all-to-all-start.2 = ((bf16[96,8,512]{2,1,0:T(8,128)(2,1)}), bf16[96,8,512]{2,1,0:T(8,128)(2,1)S(1)}, u32[]{:S(2)}, u32[]{:S(2)}) async-start(bf16[96,8,512]{2,1,0:T(8,128)(2,1)} %copy.136), calls=%async_computation.2 | async-start | bytes 1572864 | tf_op jit(solution)/shard_map/all_to_all | solution.py:97

commit v2 on v1

v2 whole, which is shorter than its diff:
```python
import jax
import jax.numpy as jnp
from jax import lax
from jax.sharding import Mesh, PartitionSpec as P

CAP = 2
BF16 = jnp.bfloat16
F32 = jnp.float32
SUB = (4, 12, 4, 2)
NAMES = ("branch", "hidden_x", "hidden_z", "width_y", "width_core")
HIDDEN = ("hidden_x", "hidden_z")
WIDTH = ("width_y", "width_core")
OWNERS = ("branch",) + HIDDEN
NEAR = ("branch", "hidden_z")


def slot_table(labels, counts):
    mb, row_dev = labels.shape
    shape = (2, mb, row_dev, row_dev)
    branch, _, here, other = (lax.broadcasted_iota(jnp.int32, shape, d) for d in range(4))
    counted = (other < counts[None, :, :, None]) & (labels[None, :, None, :] == branch)
    rank = jnp.sum(jnp.where(counted & (other < here), 1, 0), axis=3)
    own = jnp.sum(jnp.where(counted & (other == here), 1, 0), axis=3)
    rank = jnp.where(own == 1, rank, -1)
    slot = lax.broadcasted_iota(jnp.int32, (2, CAP, mb, row_dev), 1)
    return rank[:, None] == slot


def contract(left, right, left_dim, right_dim):
    return lax.dot_general(
        left, right, (((left_dim,), (right_dim,)), ((), ())), preferred_element_type=F32
    )


def own_kept(own, received, axis):
    place = lax.broadcasted_iota(jnp.int32, own.shape, 0)
    mine = place == lax.axis_index(axis)
    return jnp.sum(jnp.where(mine, own, received.astype(F32)), axis=0)


def shards(rows, cotangent, labels, counts, gate_weight, up_weight, down_weight):
    gate_weight, up_weight, down_weight = gate_weight[0], up_weight[0], down_weight[0]
    mb, row_dev, width = rows.shape
    size_x, size_z = lax.axis_size("hidden_x"), lax.axis_size("hidden_z")
    size_y, size_c = lax.axis_size("width_y"), lax.axis_size("width_core")
    near = 2 * size_z
    per_owner = mb * CAP
    block = near * per_owner
    slots = size_x * block
    units = gate_weight.shape[1]
    share_units = units // (size_y * size_c)
    table = slot_table(labels, counts)

    source = jnp.stack([rows, cotangent])
    packed = jnp.sum(
        jnp.where(
            table[:, None, :, :, :, None], source[None, :, None].astype(F32), 0.0
        ),
        axis=4,
    ).astype(BF16)
    packed = packed.reshape(2, 1, 2 * per_owner, width)
    send = jnp.broadcast_to(packed, (2, size_z, 2 * per_owner, width))
    recv = lax.all_to_all(
        send.reshape(near, 2 * per_owner, width), NEAR, 0, 0, tiled=True
    )
    recv = recv.reshape(near, 2, per_owner, width).transpose(1, 0, 2, 3)
    every = lax.all_gather(recv.reshape(2, block, width), "hidden_x", axis=0, tiled=False)
    flat_rows = every[:, 0].reshape(slots, width)
    flat_cot = every[:, 1].reshape(slots, width)

    parts = jnp.stack(
        [
            contract(gate_weight, flat_rows, 0, 1),
            contract(up_weight, flat_rows, 0, 1),
            contract(down_weight, flat_cot, 1, 1),
        ]
    )
    parts = parts.reshape(3, size_y, size_c, share_units, slots).transpose(2, 1, 0, 3, 4)
    pair = lax.all_to_all(parts, "width_core", 0, 0, tiled=True)
    pair = pair[0] + pair[1]
    sent = lax.all_to_all(pair.astype(BF16), "width_y", 0, 0, tiled=True)
    gate, up_value, dhid = own_kept(pair, sent, "width_y")
    sigma = jax.nn.sigmoid(gate)
    silu = gate * sigma
    share = jnp.stack(
        [
            (silu * up_value).astype(BF16),
            (dhid * up_value * sigma * (1.0 + gate * (1.0 - sigma))).astype(BF16),
            (dhid * silu).astype(BF16),
        ]
    )
    acts = lax.all_gather(share, WIDTH, axis=0, tiled=False)
    hidden = acts[:, 0].reshape(units, slots)
    dgate = acts[:, 1].reshape(units, slots)
    dup = acts[:, 2].reshape(units, slots)

    out_part = contract(hidden, down_weight, 0, 0)
    back_part = contract(dgate, gate_weight, 0, 1) + contract(dup, up_weight, 0, 1)
    result = jnp.stack(
        [out_part.reshape(size_x, block, width), back_part.reshape(size_x, block, width)],
        axis=1,
    )
    sent = lax.all_to_all(result.astype(BF16), "hidden_x", 0, 0, tiled=True)
    grad_gate = contract(flat_rows, dgate, 0, 1)
    grad_up = contract(flat_rows, dup, 0, 1)
    grad_down = contract(hidden, flat_cot, 1, 0)
    result = own_kept(result, sent, "hidden_x").astype(BF16)
    result = result.reshape(2, near, per_owner, width).transpose(1, 0, 2, 3)
    result = lax.all_to_all(
        result.reshape(near, 2 * per_owner, width), NEAR, 0, 0, tiled=True
    )
    result = jnp.sum(
        result.reshape(2, size_z, 2, CAP, mb, width).astype(F32), axis=1
    )
    result = lax.optimization_barrier(result).astype(BF16)
    finals = []
    for which in (0, 1):
        per_row = []
        for p in range(row_dev):
            value = jnp.zeros((), BF16)
            for branch in (0, 1):
                for s in range(CAP):
                    value = jnp.where(
                        table[branch, s, :, p : p + 1], result[branch, which, s], value
                    )
            per_row.append(value)
        finals.append(jnp.stack(per_row, axis=1))
    return (finals[0], finals[1], grad_gate[None], grad_up[None], grad_down[None])


def solution(mesh):
    mesh = Mesh(mesh.devices.reshape((2,) + SUB), NAMES)
    owner_rows = P(None, OWNERS, WIDTH)
    return jax.shard_map(
        shards,
        mesh=mesh,
        in_specs=(
            owner_rows,
            owner_rows,
            P(None, OWNERS),
            P(None, OWNERS),
            P("branch", WIDTH, HIDDEN),
            P("branch", WIDTH, HIDDEN),
            P("branch", HIDDEN, WIDTH),
        ),
        out_specs=(
            owner_rows,
            owner_rows,
            P("branch", WIDTH, HIDDEN),
            P("branch", WIDTH, HIDDEN),
            P("branch", HIDDEN, WIDTH),
        ),
        check_vma=False,
    )
```

time: 153 us -> 132 us (0.86)
  blocking collectives: 93.8 us -> 64.4 us
  starting transfers between devices: 8.13 us -> 15.8 us
  other arithmetic: 8.73 us -> 3.66 us
  waiting for transfers between devices: 31.5 us -> 33.6 us
  matrix products: 5.26 us -> 7.2 us
    all_to_all x2, blocking collectives: 78.7 us -> 34.4 us  [the longest x1 29.8 us: shards(): lax.all_to_all(send.reshape(near, 2 * per_owner, width), NEAR, 0, 0, tile...]
    all_gather x1 -> x2, blocking collectives: 15.1 us -> 29.9 us  [the longest x1 15.7 us: shards(): acts = lax.all_gather(share, WIDTH, axis=0, tiled=False)]
    all_to_all x1 -> x3, starting transfers between devices: 8.13 us -> 15.8 us  [the longest x1 6.2 us: shards(): sent = lax.all_to_all(pair.astype(BF16), 'width_y', 0, 0, tiled=True)]
    unnamed x8 -> x0, other arithmetic: 5.62 us -> none
    convert_element_type x0 -> x5, local copies, waits for them, and re-layouts: none -> 2.2 us  [the longest x1 0.98 us: shards(): sent = lax.all_to_all(result.astype(BF16), 'hidden_x', 0, 0, tiled=True)]
    all_to_all x1 -> x3, waiting for transfers between devices: 31.5 us -> 33.6 us  [the longest x1 13 us: shards(): sent = lax.all_to_all(result.astype(BF16), 'hidden_x', 0, 0, tiled=True)]
    dot_general x9, matrix products: 5.26 us -> 7.2 us  [contract(): lax.dot_general(left, right, (((left_dim,), (right_dim,)), ((), ())), pre...]
    reduce_sum x1 -> x5, other arithmetic: 0.08 us -> 1.74 us  [the longest x1 1.04 us: slot_table(): own = jnp.sum(jnp.where(counted & (other == here), 1, 0), axis=3)]
  transfers between devices with their start and end apart: 1 -> 3, of which waited for: 1 -> 3; matrix products, arithmetic and copies ran while one was open for 2% -> 3% of each run, Pallas kernels for 0% -> 0%
where the time goes in v2:
time: 132 us; the launch traced here: 131 us
  blocking collectives  64.4 us (49%)
  waiting for transfers between devices  33.6 us (25%)
  starting transfers between devices  15.8 us (12%)
  matrix products  7.2 us (5%)
  local copies, waits for them, and re-layouts  5.49 us (4%)
  other arithmetic  3.66 us (3%)
    all_to_all x1, blocking collectives, shards(): lax.all_to_all(send.reshape(near, 2 * per_owner, width), NEAR, 0, 0, tile...  29.8 us
    all_gather x1, blocking collectives, shards(): acts = lax.all_gather(share, WIDTH, axis=0, tiled=False)  15.7 us
    all_gather x1, blocking collectives, shards(): lax.all_gather(recv.reshape(2, block, width), 'hidden_x', axis=0, tiled=F...  14.3 us
    all_to_all x1, waiting for transfers between devices, shards(): sent = lax.all_to_all(result.astype(BF16), 'hidden_x', 0, 0, tiled=True)  13 us
    all_to_all x1, waiting for transfers between devices, shards(): sent = lax.all_to_all(pair.astype(BF16), 'width_y', 0, 0, tiled=True)  11 us
    all_to_all x1, waiting for transfers between devices, shards(): lax.all_to_all(result.reshape(near, 2 * per_owner, width), NEAR, 0, 0, ti...  9.53 us
    dot_general x9, matrix products, contract(): lax.dot_general(left, right, (((left_dim,), (right_dim,)), ((), ())), pre...  7.2 us
    all_to_all x1, starting transfers between devices, shards(): sent = lax.all_to_all(pair.astype(BF16), 'width_y', 0, 0, tiled=True)  6.2 us
  transfers between devices with their start and end apart: 3, of which 3 were waited for; matrix products, arithmetic and copies ran while one was open for 3% of the time, Pallas kernels for 0%

profile of v2, /device:TPU:8, one launch (start us, length us, event | category | flops | bytes accessed | tf_op | source)
XLA Modules:
  0.0 131.0 jit_solution(539716233680960698)
XLA Ops:
  0.6 1.0 fusion.14
  1.7 0.7 maximum_convert_fusion
  2.6 29.8 %all_to_all.25 = bf16[24,8,512]{2,1,0:T(8,128)(2,1)S(1)} all-to-all(bf16[24,8,512]{2,1,0:T(8,128)(2,1)S(1)} %bitcast.186), channel_id=1, replica_groups=mesh['branch'=2,'hidden_x'=4,'hidden_z'=12,'width_y'=4,'width_core'=2] {..., dimensions={0} | all-to-all | bytes 393216 | tf_op jit(solution)/shard_map/all_to_all | solution.py:63
  32.4 0.2 copy.49
  32.7 14.3 %all_gather.9 = bf16[4,2,96,512]{3,2,1,0:T(8,128)(2,1)S(1)} all-gather(bf16[1,2,96,512]{3,2,1,0:T(8,128)(2,1)S(1)} %copy.50), channel_id=1, replica_groups=mesh['branch'=2,'hidden_x'=4,'hidden_z'=12,'width_y'=4,'width_core'=2] {..., dimensions={0}, use_global_device_ids=true | all-gather | bytes 983040 | tf_op jit(solution)/shard_map/all_gather | solution.py:67
  47.1 0.3 fusion.10
  47.4 0.5 copy-done.8
  47.9 0.3 fusion.6
  48.3 0.3 fusion.3
  48.7 4.7 %all_to_all.26 = f32[2,4,3,32,384]{4,3,1,2,0:T(8,128)S(1)} all-to-all(f32[2,4,3,32,384]{4,3,1,2,0:T(8,128)S(1)} %copy_bitcast_fusion), channel_id=1, replica_groups=mesh['branch'=2,'hidden_x'=4,'hidden_z'=12,'width_y'=4,'width_core'=2] {..., dimensions={0} | all-to-all | bytes 2359296 | tf_op jit(solution)/shard_map/all_to_all | solution.py:79
  53.4 0.7 copy.56
  54.2 6.2 %all-to-all-start.2 = ((bf16[4,3,32,384]{3,2,1,0:T(8,128)(2,1)}), bf16[4,3,32,384]{3,2,1,0:T(8,128)(2,1)S(1)}, u32[]{:S(2)}, u32[]{:S(2)}) async-start(bf16[4,3,32,384]{3,2,1,0:T(8,128)(2,1)} %copy.56), calls=%async_computation.2 | async-start | bytes 589824 | tf_op jit(solution)/shard_map/all_to_all | solution.py:81
  60.4 11.0 %all-to-all-done.2 = bf16[4,3,32,384]{3,2,1,0:T(8,128)(2,1)S(1)} async-done(((bf16[4,3,32,384]{3,2,1,0:T(8,128)(2,1)}), bf16[4,3,32,384]{3,2,1,0:T(8,128)(2,1)S(1)}, u32[]{:S(2)}, u32[]{:S(2)}) %all-to-all-start.2) | async-done | bytes 294944 | tf_op jit(solution)/shard_map/all_to_all | solution.py:81
  71.6 15.7 %all-gather = bf16[24,32,384]{2,1,0:T(8,128)(2,1)S(1)} all-gather(bf16[3,32,384]{2,1,0:T(8,128)(2,1)S(1)} %pad_maximum_fusion.2), channel_id=2, replica_groups=mesh['branch'=2,'hidden_x'=4,'hidden_z'=12,'width_y'=4,'width_core'=2] {..., dimensions={0}, use_global_device_ids=true | all-gather | bytes 663552 | tf_op jit(solution)/shard_map/all_gather | solution.py:92
  87.3 0.7 fusion.17
  88.0 0.3 fusion.8
  88.3 0.8 copy.58
  89.2 1.2 convolution_bitcast_fusion
  90.4 1.4 %convolution_add_fusion = f32[384,512]{1,0:T(8,128)S(1)} fusion(f32[384,512]{1,0:T(8,128)S(1)} %fusion.8, bf16[256,384]{1,0:T(8,128)(2,1)} %bitcast.180, bf16[1,512,256]{2,1,0:T(8,128)(2,1)} %param.12), kind=kOutput, calls=%fused_computation.2 | convolution fusion | flops 100859904 | bytes 2031616 | tf_op jit(solution)/shard_map/dot_general | solution.py:30
  91.8 1.0 copy.59
  92.8 3.5 %all-to-all-start.3 = ((bf16[4,2,96,512]{3,2,1,0:T(8,128)(2,1)}), bf16[4,2,96,512]{3,2,1,0:T(8,128)(2,1)S(1)}, u32[]{:S(2)}, u32[]{:S(2)}) async-start(bf16[4,2,96,512]{3,2,1,0:T(8,128)(2,1)} %copy.59), calls=%async_computation.3 | async-start | bytes 1572864 | tf_op jit(solution)/shard_map/all_to_all | solution.py:103
  96.3 13.0 %all-to-all-done.3 = bf16[4,2,96,512]{3,2,1,0:T(8,128)(2,1)S(1)} async-done(((bf16[4,2,96,512]{3,2,1,0:T(8,128)(2,1)}), bf16[4,2,96,512]{3,2,1,0:T(8,128)(2,1)S(1)}, u32[]{:S(2)}, u32[]{:S(2)}) %all-to-all-start.3) | async-done | bytes 786464 | tf_op jit(solution)/shard_map/all_to_all | solution.py:103
  109.4 0.3 select_reduce_fusion
  109.7 0.2 copy.61
  110.0 0.7 copy.63
  110.7 6.1 %all-to-all-start.4 = ((bf16[24,8,512]{2,1,0:T(8,128)(2,1)}), bf16[24,8,512]{2,1,0:T(8,128)(2,1)S(1)}, u32[]{:S(2)}, u32[]{:S(2)}) async-start(bf16[24,8,512]{2,1,0:T(8,128)(2,1)} %copy.63), calls=%async_computation.4 | async-start | bytes 393216 | tf_op jit(solution)/shard_map/all_to_all | solution.py:109
  116.9 1.1 convolution_bitcast_fusion.1
  117.9 1.1 convolution_bitcast_fusion.2
  119.1 1.1 convolution_bitcast_fusion.3
  120.2 9.5 %all-to-all-done.4 = bf16[24,8,512]{2,1,0:T(8,128)(2,1)S(1)} async-done(((bf16[24,8,512]{2,1,0:T(8,128)(2,1)}), bf16[24,8,512]{2,1,0:T(8,128)(2,1)S(1)}, u32[]{:S(2)}, u32[]{:S(2)}) %all-to-all-start.4) | async-done | bytes 196640 | tf_op jit(solution)/shard_map/all_to_all | solution.py:109
  129.8 0.3 reshape.1004
  130.4 0.6 pad_maximum_fusion.3
  (39 shorter events, 1.3 us)
Async XLA Ops:
  0.6 46.4 %copy-start = (bf16[1,512,256]{2,1,0:T(8,128)(2,1)S(1)}, bf16[1,512,256]{2,1,0:T(8,128)(2,1)}, u32[]{:S(2)}) copy-start(bf16[1,512,256]{2,1,0:T(8,128)(2,1)} %param.11) | copy-start | bytes 786436
  46.9 1.0 copy-start.8
  47.0 1.2 copy-start.6
  54.2 17.2 %all-to-all-start.2 = ((bf16[4,3,32,384]{3,2,1,0:T(8,128)(2,1)}), bf16[4,3,32,384]{3,2,1,0:T(8,128)(2,1)S(1)}, u32[]{:S(2)}, u32[]{:S(2)}) async-start(bf16[4,3,32,384]{3,2,1,0:T(8,128)(2,1)} %copy.56), calls=%async_computation.2 | async-start | bytes 589824 | tf_op jit(solution)/shard_map/all_to_all | solution.py:81
  87.3 1.9 %copy-start.7 = (bf16[1,256,512]{2,1,0:T(8,128)(2,1)S(1)}, bf16[1,256,512]{2,1,0:T(8,128)(2,1)}, u32[]{:S(2)}) copy-start(bf16[1,256,512]{2,1,0:T(8,128)(2,1)} %param.13) | copy-start | bytes 786436
  88.0 1.1 copy-start.1
  88.0 1.1 copy-start.3
  92.8 16.5 %all-to-all-start.3 = ((bf16[4,2,96,512]{3,2,1,0:T(8,128)(2,1)}), bf16[4,2,96,512]{3,2,1,0:T(8,128)(2,1)S(1)}, u32[]{:S(2)}, u32[]{:S(2)}) async-start(bf16[4,2,96,512]{3,2,1,0:T(8,128)(2,1)} %copy.59), calls=%async_computation.3 | async-start | bytes 1572864 | tf_op jit(solution)/shard_map/all_to_all | solution.py:103
  109.7 7.2 %copy-start.4 = (bf16[8,1,32,384]{3,2,1,0:T(8,128)(2,1)S(1)}, bf16[8,1,32,384]{3,2,1,0:T(8,128)(2,1)}, u32[]{:S(2)}) copy-start(bf16[8,1,32,384]{3,2,1,0:T(8,128)(2,1)} %copy-done.3) | copy-start | bytes 589828
  109.9 8.1 %copy-start.5 = (bf16[8,1,32,384]{3,2,1,0:T(8,128)(2,1)S(1)}, bf16[8,1,32,384]{3,2,1,0:T(8,128)(2,1)}, u32[]{:S(2)}) copy-start(bf16[8,1,32,384]{3,2,1,0:T(8,128)(2,1)} %get-tuple-element.10) | copy-start | bytes 589828
  110.7 19.1 %all-to-all-start.4 = ((bf16[24,8,512]{2,1,0:T(8,128)(2,1)}), bf16[24,8,512]{2,1,0:T(8,128)(2,1)S(1)}, u32[]{:S(2)}, u32[]{:S(2)}) async-start(bf16[24,8,512]{2,1,0:T(8,128)(2,1)} %copy.63), calls=%async_computation.4 | async-start | bytes 393216 | tf_op jit(solution)/shard_map/all_to_all | solution.py:109
  116.8 2.3 %copy-start.2 = (bf16[8,1,32,384]{3,2,1,0:T(8,128)(2,1)S(1)}, bf16[8,1,32,384]{3,2,1,0:T(8,128)(2,1)}, u32[]{:S(2)}) copy-start(bf16[8,1,32,384]{3,2,1,0:T(8,128)(2,1)} %copy-done.1) | copy-start | bytes 589828

commit v3 on v2

--- a/solution.py
+++ b/solution.py
@@ -1,6 +1,9 @@
 import jax
 import jax.numpy as jnp
 from jax import lax
+from jax.experimental import pallas as pl
+from jax.experimental.layout import Layout, with_layout_constraint
+from jax.experimental.pallas import tpu as pltpu
 from jax.sharding import Mesh, PartitionSpec as P
 
 CAP = 2
@@ -36,6 +39,57 @@
     place = lax.broadcasted_iota(jnp.int32, own.shape, 0)
     mine = place == lax.axis_index(axis)
     return jnp.sum(jnp.where(mine, own, received.astype(F32)), axis=0)
+
+
+def full(shape):
+    return pl.BlockSpec(shape, lambda: (0,) * len(shape))
+
+
+def second_kernel(place_ref, acts_ref, gate_ref, up_ref, down_ref, sent_ref, own_ref, scratch):
+    parts, kinds, share_units, slots = acts_ref.shape
+    units = parts * share_units
+    width = down_ref.shape[1]
+    hidden = acts_ref[:, 0].reshape(units, slots)
+    dgate = acts_ref[:, 1].reshape(units, slots)
+    dup = acts_ref[:, 2].reshape(units, slots)
+    out = contract(hidden, down_ref[...], 0, 0)
+    back = contract(dgate, gate_ref[...], 0, 1) + contract(dup, up_ref[...], 0, 1)
+    tiles = slots // 8
+    out = out.reshape(tiles, 8, width)
+    back = back.reshape(tiles, 8, width)
+    first = lax.broadcasted_iota(jnp.int32, out.shape, 1) < 4
+    even = jnp.where(first, out, pltpu.roll(back, 4, 1))
+    odd = jnp.where(first, pltpu.roll(out, 4, 1), back)
+    sent_ref[:, 0] = even.astype(BF16)
+    sent_ref[:, 1] = odd.astype(BF16)
+    scratch[:, 0] = even
+    scratch[:, 1] = odd
+    own_tiles = own_ref.shape[0]
+    own_ref[...] = scratch[pl.ds(place_ref[0] * own_tiles, own_tiles)]
+
+
+def second_products(place, acts, gate_weight, up_weight, down_weight, size_x):
+    slots = acts.shape[3]
+    width = down_weight.shape[1]
+    shape = (slots // 8, 2, 8, width)
+    own_shape = (slots // 8 // size_x, 2, 8, width)
+    return pl.pallas_call(
+        second_kernel,
+        out_shape=(
+            jax.ShapeDtypeStruct(shape, BF16),
+            jax.ShapeDtypeStruct(own_shape, F32),
+        ),
+        in_specs=[
+            pl.BlockSpec(memory_space=pltpu.SMEM),
+            full(acts.shape),
+            full(gate_weight.shape),
+            full(up_weight.shape),
+            full(down_weight.shape),
+        ],
+        out_specs=(full(shape), full(own_shape)),
+        scratch_shapes=[pltpu.VMEM(shape, F32)],
+        name="second_products",
+    )(place, acts, gate_weight, up_weight, down_weight)
 
 
 def shards(rows, cotangent, labels, counts, gate_weight, up_weight, down_weight):
@@ -76,6 +130,7 @@
         ]
     )
     parts = parts.reshape(3, size_y, size_c, share_units, slots).transpose(2, 1, 0, 3, 4)
+    parts = with_layout_constraint(parts, Layout(major_to_minor=(0, 1, 2, 3, 4)))
     pair = lax.all_to_all(parts, "width_core", 0, 0, tiled=True)
     pair = pair[0] + pair[1]
     sent = lax.all_to_all(pair.astype(BF16), "width_y", 0, 0, tiled=True)
@@ -94,21 +149,20 @@
     dgate = acts[:, 1].reshape(units, slots)
     dup = acts[:, 2].reshape(units, slots)
 
-    out_part = contract(hidden, down_weight, 0, 0)
-    back_part = contract(dgate, gate_weight, 0, 1) + contract(dup, up_weight, 0, 1)
-    result = jnp.stack(
-        [out_part.reshape(size_x, block, width), back_part.reshape(size_x, block, width)],
-        axis=1,
-    )
-    sent = lax.all_to_all(result.astype(BF16), "hidden_x", 0, 0, tiled=True)
+    place_x = lax.axis_index("hidden_x")
+    sent, own = second_products(
+        place_x.reshape(1), acts, gate_weight, up_weight, down_weight, size_x
+    )
+    sent = lax.all_to_all(
+        sent.reshape(size_x, near, 8, width), "hidden_x", 0, 0, tiled=True
+    )
     grad_gate = contract(flat_rows, dgate, 0, 1)
     grad_up = contract(flat_rows, dup, 0, 1)
     grad_down = contract(hidden, flat_cot, 1, 0)
-    result = own_kept(result, sent, "hidden_x").astype(BF16)
-    result = result.reshape(2, near, per_owner, width).transpose(1, 0, 2, 3)
-    result = lax.all_to_all(
-        result.reshape(near, 2 * per_owner, width), NEAR, 0, 0, tiled=True
-    )
+    other = lax.broadcasted_iota(jnp.int32, (size_x, 1, 1, 1), 0) != place_x
+    result = jnp.sum(jnp.where(other, sent.astype(F32), 0.0), axis=0)
+    result = (own.reshape(near, 8, width) + result).astype(BF16)
+    result = lax.all_to_all(result, NEAR, 0, 0, tiled=True)
     result = jnp.sum(
         result.reshape(2, size_z, 2, CAP, mb, width).astype(F32), axis=1
     )

time: 132 us -> 130 us (0.985)
  local copies, waits for them, and re-layouts: 5.49 us -> 1.25 us
  Pallas kernels: 0 us -> 2.84 us
  matrix products: 7.2 us -> 4.38 us
    pallas_call x0 -> x1, Pallas kernels: none -> 2.84 us  [second_products(): pl.pallas_call(second_kernel, out_shape=(jax.ShapeDtypeStruct(shape, BF16...]
    dot_general x9 -> x6, matrix products: 7.2 us -> 4.38 us  [contract(): lax.dot_general(left, right, (((left_dim,), (right_dim,)), ((), ())), pre...]
    convert_element_type x3 -> x0, local copies, waits for them, and re-layouts: 1.92 us -> none  [the longest x1 0.98 us: shards(): sent = lax.all_to_all(result.astype(BF16), 'hidden_x', 0, 0, tiled=True)]
where the time goes in v3:
time: 130 us; the launch traced here: 129 us
  blocking collectives  65.3 us (50%)
  waiting for transfers between devices  33.7 us (26%)
  starting transfers between devices  16 us (12%)
  other arithmetic  4.89 us (4%)
  matrix products  4.38 us (3%)
  Pallas kernels  2.84 us (2%)
    all_to_all x1, blocking collectives, shards(): lax.all_to_all(send.reshape(near, 2 * per_owner, width), NEAR, 0, 0, tile...  29.8 us
    all_gather x1, blocking collectives, shards(): acts = lax.all_gather(share, WIDTH, axis=0, tiled=False)  16.4 us
    all_gather x1, blocking collectives, shards(): lax.all_gather(recv.reshape(2, block, width), 'hidden_x', axis=0, tiled=F...  14.4 us
    all_to_all x1, waiting for transfers between devices, shards(): lax.all_to_all(sent.reshape(size_x, near, 8, width), 'hidden_x', 0, 0, ti...  13 us
    all_to_all x1, waiting for transfers between devices, shards(): sent = lax.all_to_all(pair.astype(BF16), 'width_y', 0, 0, tiled=True)  11 us
    all_to_all x1, waiting for transfers between devices, shards(): result = lax.all_to_all(result, NEAR, 0, 0, tiled=True)  9.62 us
    all_to_all x1, starting transfers between devices, shards(): sent = lax.all_to_all(pair.astype(BF16), 'width_y', 0, 0, tiled=True)  6.19 us
    all_to_all x1, starting transfers between devices, shards(): result = lax.all_to_all(result, NEAR, 0, 0, tiled=True)  6.13 us
  transfers between devices with their start and end apart: 3, of which 3 were waited for; matrix products, arithmetic and copies ran while one was open for 3% of the time, Pallas kernels for 0%

profile of v3, /device:TPU:8, one launch (start us, length us, event | category | flops | bytes accessed | tf_op | source)
XLA Modules:
  0.0 129.1 jit_solution(11718381422040090374)
XLA Ops:
  0.6 1.0 fusion.4
  1.7 0.7 maximum_convert_fusion
  2.4 0.1 select_reduce_fusion.2
  2.6 29.8 %all_to_all.25 = bf16[24,8,512]{2,1,0:T(8,128)(2,1)S(1)} all-to-all(bf16[24,8,512]{2,1,0:T(8,128)(2,1)S(1)} %bitcast.168), channel_id=1, replica_groups=mesh['branch'=2,'hidden_x'=4,'hidden_z'=12,'width_y'=4,'width_core'=2] {..., dimensions={0} | all-to-all | bytes 393216 | tf_op jit(solution)/shard_map/all_to_all | solution.py:117
  32.4 0.2 copy.43
  32.6 14.4 %all_gather.9 = bf16[4,2,96,512]{3,2,1,0:T(8,128)(2,1)S(1)} all-gather(bf16[1,2,96,512]{3,2,1,0:T(8,128)(2,1)S(1)} %copy.44), channel_id=1, replica_groups=mesh['branch'=2,'hidden_x'=4,'hidden_z'=12,'width_y'=4,'width_core'=2] {..., dimensions={0}, use_global_device_ids=true | all-gather | bytes 983040 | tf_op jit(solution)/shard_map/all_gather | solution.py:121
  47.1 0.3 fusion.8
  47.5 0.5 copy-done.3
  48.0 0.3 fusion.10
  48.3 0.3 fusion.6
  48.7 0.1 copy_bitcast_fusion
  48.8 4.7 %all_to_all.26 = f32[2,4,3,32,384]{4,3,2,1,0:T(8,128)S(1)} all-to-all(f32[2,4,3,32,384]{4,3,2,1,0:T(8,128)S(1)} %copy_bitcast_fusion), channel_id=1, replica_groups=mesh['branch'=2,'hidden_x'=4,'hidden_z'=12,'width_y'=4,'width_core'=2] {..., dimensions={0} | all-to-all | bytes 2359296 | tf_op jit(solution)/shard_map/all_to_all | solution.py:134
  53.4 0.8 fusion.2
  54.2 6.2 %all-to-all-start.2 = ((bf16[4,3,32,384]{3,2,1,0:T(8,128)(2,1)}), bf16[4,3,32,384]{3,2,1,0:T(8,128)(2,1)S(1)}, u32[]{:S(2)}, u32[]{:S(2)}) async-start(bf16[4,3,32,384]{3,2,1,0:T(8,128)(2,1)} %fusion.2), calls=%async_computation.2 | async-start | bytes 589824 | tf_op jit(solution)/shard_map/all_to_all | solution.py:136
  60.4 11.0 %all-to-all-done.2 = bf16[4,3,32,384]{3,2,1,0:T(8,128)(2,1)S(1)} async-done(((bf16[4,3,32,384]{3,2,1,0:T(8,128)(2,1)}), bf16[4,3,32,384]{3,2,1,0:T(8,128)(2,1)S(1)}, u32[]{:S(2)}, u32[]{:S(2)}) %all-to-all-start.2) | async-done | bytes 294944 | tf_op jit(solution)/shard_map/all_to_all | solution.py:136
  71.5 0.2 select_reduce_fusion.1
  71.7 16.4 %all-gather = bf16[24,32,384]{2,1,0:T(8,128)(2,1)} all-gather(bf16[3,32,384]{2,1,0:T(8,128)(2,1)S(1)} %pad_maximum_fusion.1), channel_id=2, replica_groups=mesh['branch'=2,'hidden_x'=4,'hidden_z'=12,'width_y'=4,'width_core'=2] {..., dimensions={0}, use_global_device_ids=true | all-gather | bytes 663552 | tf_op jit(solution)/shard_map/all_gather | solution.py:147
  88.1 2.8 %second_products.1 = (bf16[48,2,8,512]{3,2,1,0:T(8,128)(2,1)}, f32[12,2,8,512]{3,2,1,0:T(8,128)}) custom-call(s32[1]{0:T(128)} %bitcast.2.place_ref, bf16[8,3,32,384]{3,2,1,0:T(8,128)(2,1)} %bitcast.157, bf16[512,256]{1,0:T(8,128)(2,1)} %bitcast.166, bf16[512,256]{1,0:T(8,128)(2,1)} %bitcast.165, bf16[256,512]{1,0:T(8,128)(2,1)} %bitcast.164), custom_call_target="tpu_custom_call" | custom-call | tf_op jit(solution)/shard_map/second_products/pallas_call | solution.py:76
  91.0 3.6 %all-to-all-start.3 = ((bf16[4,24,8,512]{3,2,1,0:T(8,128)(2,1)}), bf16[4,24,8,512]{3,2,1,0:T(8,128)(2,1)S(1)}, u32[]{:S(2)}, u32[]{:S(2)}) async-start(bf16[4,24,8,512]{3,2,1,0:T(8,128)(2,1)} %bitcast.167), calls=%async_computation.3 | async-start | bytes 1572864 | tf_op jit(solution)/shard_map/all_to_all | solution.py:156
  94.6 13.0 %all-to-all-done.3 = bf16[4,24,8,512]{3,2,1,0:T(8,128)(2,1)S(1)} async-done(((bf16[4,24,8,512]{3,2,1,0:T(8,128)(2,1)}), bf16[4,24,8,512]{3,2,1,0:T(8,128)(2,1)S(1)}, u32[]{:S(2)}, u32[]{:S(2)}) %all-to-all-start.3) | async-done | bytes 786464 | tf_op jit(solution)/shard_map/all_to_all | solution.py:156
  107.6 0.2 select_reduce_fusion
  107.9 0.7 fusion.1
  108.6 6.1 %all-to-all-start.4 = ((bf16[24,8,512]{2,1,0:T(8,128)(2,1)}), bf16[24,8,512]{2,1,0:T(8,128)(2,1)S(1)}, u32[]{:S(2)}, u32[]{:S(2)}) async-start(bf16[24,8,512]{2,1,0:T(8,128)(2,1)} %fusion.1), calls=%async_computation.4 | async-start | bytes 393216 | tf_op jit(solution)/shard_map/all_to_all | solution.py:165
  114.8 1.1 convolution_bitcast_fusion
  115.9 1.1 convolution_bitcast_fusion.2
  117.1 1.1 convolution_bitcast_fusion.1
  118.2 9.6 %all-to-all-done.4 = bf16[24,8,512]{2,1,0:T(8,128)(2,1)S(1)} async-done(((bf16[24,8,512]{2,1,0:T(8,128)(2,1)}), bf16[24,8,512]{2,1,0:T(8,128)(2,1)S(1)}, u32[]{:S(2)}, u32[]{:S(2)}) %all-to-all-start.4) | async-done | bytes 196640 | tf_op jit(solution)/shard_map/all_to_all | solution.py:165
  127.8 0.3 reshape.1007
  128.1 0.1 reduce_sum.59
  128.2 0.1 broadcast_select_fusion.4
  128.3 0.1 broadcast_select_fusion.10
  128.5 0.6 pad_maximum_fusion.2
  (23 shorter events, 0.4 us)
Async XLA Ops:
  32.6 14.5 %copy-start.2 = (bf16[1,512,256]{2,1,0:T(8,128)(2,1)S(1)}, bf16[1,512,256]{2,1,0:T(8,128)(2,1)}, u32[]{:S(2)}) copy-start(bf16[1,512,256]{2,1,0:T(8,128)(2,1)} %param.12) | copy-start | bytes 786436
  47.0 1.0 copy-start.3
  47.1 1.2 copy-start.1
  54.2 17.2 %all-to-all-start.2 = ((bf16[4,3,32,384]{3,2,1,0:T(8,128)(2,1)}), bf16[4,3,32,384]{3,2,1,0:T(8,128)(2,1)S(1)}, u32[]{:S(2)}, u32[]{:S(2)}) async-start(bf16[4,3,32,384]{3,2,1,0:T(8,128)(2,1)} %fusion.2), calls=%async_computation.2 | async-start | bytes 589824 | tf_op jit(solution)/shard_map/all_to_all | solution.py:136
  91.0 16.9 %copy-start.4 = (f32[12,2,8,512]{3,2,1,0:T(8,128)S(1)}, f32[12,2,8,512]{3,2,1,0:T(8,128)}, u32[]{:S(2)}) copy-start(f32[12,2,8,512]{3,2,1,0:T(8,128)} %get-tuple-element.7) | copy-start | bytes 1179652
  91.0 16.7 %all-to-all-start.3 = ((bf16[4,24,8,512]{3,2,1,0:T(8,128)(2,1)}), bf16[4,24,8,512]{3,2,1,0:T(8,128)(2,1)S(1)}, u32[]{:S(2)}, u32[]{:S(2)}) async-start(bf16[4,24,8,512]{3,2,1,0:T(8,128)(2,1)} %bitcast.167), calls=%async_computation.3 | async-start | bytes 1572864 | tf_op jit(solution)/shard_map/all_to_all | solution.py:156
  94.6 20.1 %copy-start = (bf16[24,32,384]{2,1,0:T(8,128)(2,1)S(1)}, bf16[24,32,384]{2,1,0:T(8,128)(2,1)}, u32[]{:S(2)}) copy-start(bf16[24,32,384]{2,1,0:T(8,128)(2,1)} %all-gather) | copy-start | bytes 1769476
  108.6 19.2 %all-to-all-start.4 = ((bf16[24,8,512]{2,1,0:T(8,128)(2,1)}), bf16[24,8,512]{2,1,0:T(8,128)(2,1)S(1)}, u32[]{:S(2)}, u32[]{:S(2)}) async-start(bf16[24,8,512]{2,1,0:T(8,128)(2,1)} %fusion.1), calls=%async_computation.4 | async-start | bytes 393216 | tf_op jit(solution)/shard_map/all_to_all | solution.py:165

commit v4 on v3

--- a/solution.py
+++ b/solution.py
@@ -88,6 +88,7 @@
         ],
         out_specs=(full(shape), full(own_shape)),
         scratch_shapes=[pltpu.VMEM(shape, F32)],
+        compiler_params=pltpu.CompilerParams(vmem_limit_bytes=12 * 1024 * 1024),
         name="second_products",
     )(place, acts, gate_weight, up_weight, down_weight)
 

time: 130 us -> 127 us (0.977)
  Pallas kernels: 2.84 us -> 1.42 us
    pallas_call x1, Pallas kernels: 2.84 us -> 1.42 us  [second_products(): pl.pallas_call(second_kernel, out_shape=(jax.ShapeDtypeStruct(shape, BF16...]
where the time goes in v4:
time: 127 us
  blocking collectives  64.5 us (51%)
  waiting for transfers between devices  33.5 us (26%)
  starting transfers between devices  15.8 us (12%)
  other arithmetic  4.89 us (4%)
  matrix products  4.36 us (3%)
  Pallas kernels  1.42 us (1%)
    all_to_all x1, blocking collectives, shards(): lax.all_to_all(send.reshape(near, 2 * per_owner, width), NEAR, 0, 0, tile...  29.8 us
    all_gather x1, blocking collectives, shards(): acts = lax.all_gather(share, WIDTH, axis=0, tiled=False)  15.7 us
    all_gather x1, blocking collectives, shards(): lax.all_gather(recv.reshape(2, block, width), 'hidden_x', axis=0, tiled=F...  14.4 us
    all_to_all x1, waiting for transfers between devices, shards(): lax.all_to_all(sent.reshape(size_x, near, 8, width), 'hidden_x', 0, 0, ti...  13 us
    all_to_all x1, waiting for transfers between devices, shards(): sent = lax.all_to_all(pair.astype(BF16), 'width_y', 0, 0, tiled=True)  11 us
    all_to_all x1, waiting for transfers between devices, shards(): result = lax.all_to_all(result, NEAR, 0, 0, tiled=True)  9.49 us
    all_to_all x1, starting transfers between devices, shards(): sent = lax.all_to_all(pair.astype(BF16), 'width_y', 0, 0, tiled=True)  6.2 us
    all_to_all x1, starting transfers between devices, shards(): result = lax.all_to_all(result, NEAR, 0, 0, tiled=True)  6.09 us
  transfers between devices with their start and end apart: 3, of which 3 were waited for; matrix products, arithmetic and copies ran while one was open for 3% of the time, Pallas kernels for 0%

profile of v4, /device:TPU:8, one launch (start us, length us, event | category | flops | bytes accessed | tf_op | source)
XLA Modules:
  0.0 126.6 jit_solution(4166930122751401533)
XLA Ops:
  0.6 1.0 fusion.4
  1.7 0.7 maximum_convert_fusion
  2.4 0.1 select_reduce_fusion.2
  2.6 29.8 %all_to_all.25 = bf16[24,8,512]{2,1,0:T(8,128)(2,1)S(1)} all-to-all(bf16[24,8,512]{2,1,0:T(8,128)(2,1)S(1)} %bitcast.167), channel_id=1, replica_groups=mesh['branch'=2,'hidden_x'=4,'hidden_z'=12,'width_y'=4,'width_core'=2] {..., dimensions={0} | all-to-all | bytes 393216 | tf_op jit(solution)/shard_map/all_to_all | solution.py:118
  32.4 0.2 copy.43
  32.6 14.4 %all_gather.9 = bf16[4,2,96,512]{3,2,1,0:T(8,128)(2,1)S(1)} all-gather(bf16[1,2,96,512]{3,2,1,0:T(8,128)(2,1)S(1)} %copy.44), channel_id=1, replica_groups=mesh['branch'=2,'hidden_x'=4,'hidden_z'=12,'width_y'=4,'width_core'=2] {..., dimensions={0}, use_global_device_ids=true | all-gather | bytes 983040 | tf_op jit(solution)/shard_map/all_gather | solution.py:122
  47.1 0.3 fusion.8
  47.5 0.5 copy-done.2
  48.0 0.3 fusion.10
  48.3 0.3 fusion.6
  48.7 0.1 copy_bitcast_fusion
  48.8 4.7 %all_to_all.26 = f32[2,4,3,32,384]{4,3,2,1,0:T(8,128)S(1)} all-to-all(f32[2,4,3,32,384]{4,3,2,1,0:T(8,128)S(1)} %copy_bitcast_fusion), channel_id=1, replica_groups=mesh['branch'=2,'hidden_x'=4,'hidden_z'=12,'width_y'=4,'width_core'=2] {..., dimensions={0} | all-to-all | bytes 2359296 | tf_op jit(solution)/shard_map/all_to_all | solution.py:135
  53.4 0.8 fusion.2
  54.2 6.2 %all-to-all-start.2 = ((bf16[4,3,32,384]{3,2,1,0:T(8,128)(2,1)}), bf16[4,3,32,384]{3,2,1,0:T(8,128)(2,1)S(1)}, u32[]{:S(2)}, u32[]{:S(2)}) async-start(bf16[4,3,32,384]{3,2,1,0:T(8,128)(2,1)} %fusion.2), calls=%async_computation.2 | async-start | bytes 589824 | tf_op jit(solution)/shard_map/all_to_all | solution.py:137
  60.4 11.0 %all-to-all-done.2 = bf16[4,3,32,384]{3,2,1,0:T(8,128)(2,1)S(1)} async-done(((bf16[4,3,32,384]{3,2,1,0:T(8,128)(2,1)}), bf16[4,3,32,384]{3,2,1,0:T(8,128)(2,1)S(1)}, u32[]{:S(2)}, u32[]{:S(2)}) %all-to-all-start.2) | async-done | bytes 294944 | tf_op jit(solution)/shard_map/all_to_all | solution.py:137
  71.5 0.2 select_reduce_fusion.1
  71.7 15.7 %all-gather = bf16[24,32,384]{2,1,0:T(8,128)(2,1)S(1)} all-gather(bf16[3,32,384]{2,1,0:T(8,128)(2,1)S(1)} %pad_maximum_fusion.1), channel_id=2, replica_groups=mesh['branch'=2,'hidden_x'=4,'hidden_z'=12,'width_y'=4,'width_core'=2] {..., dimensions={0}, use_global_device_ids=true | all-gather | bytes 663552 | tf_op jit(solution)/shard_map/all_gather | solution.py:148
  87.3 1.4 %second_products.1 = (bf16[48,2,8,512]{3,2,1,0:T(8,128)(2,1)}, f32[12,2,8,512]{3,2,1,0:T(8,128)S(1)}) custom-call(s32[1]{0:T(128)} %bitcast.2.place_ref, bf16[8,3,32,384]{3,2,1,0:T(8,128)(2,1)S(1)} %bitcast.153, bf16[512,256]{1,0:T(8,128)(2,1)S(1)} %bitcast.157, bf16[512,256]{1,0:T(8,128)(2,1)S(1)} %bitcast.156, bf16[256,512]{1,0:T(8,128)(2,1)S(1)} %bitcast.155), custom_call_target="tpu_custom_call" | custom-call | tf_op jit(solution)/shard_map/second_products/pallas_call | solution.py:76
  88.8 3.5 %all-to-all-start.3 = ((bf16[4,24,8,512]{3,2,1,0:T(8,128)(2,1)}), bf16[4,24,8,512]{3,2,1,0:T(8,128)(2,1)S(1)}, u32[]{:S(2)}, u32[]{:S(2)}) async-start(bf16[4,24,8,512]{3,2,1,0:T(8,128)(2,1)} %bitcast.24), calls=%async_computation.3 | async-start | bytes 1572864 | tf_op jit(solution)/shard_map/all_to_all | solution.py:157
  92.3 13.0 %all-to-all-done.3 = bf16[4,24,8,512]{3,2,1,0:T(8,128)(2,1)S(1)} async-done(((bf16[4,24,8,512]{3,2,1,0:T(8,128)(2,1)}), bf16[4,24,8,512]{3,2,1,0:T(8,128)(2,1)S(1)}, u32[]{:S(2)}, u32[]{:S(2)}) %all-to-all-start.3) | async-done | bytes 786464 | tf_op jit(solution)/shard_map/all_to_all | solution.py:157
  105.3 0.2 select_reduce_fusion
  105.5 0.7 fusion.1
  106.3 6.1 %all-to-all-start.4 = ((bf16[24,8,512]{2,1,0:T(8,128)(2,1)}), bf16[24,8,512]{2,1,0:T(8,128)(2,1)S(1)}, u32[]{:S(2)}, u32[]{:S(2)}) async-start(bf16[24,8,512]{2,1,0:T(8,128)(2,1)} %fusion.1), calls=%async_computation.4 | async-start | bytes 393216 | tf_op jit(solution)/shard_map/all_to_all | solution.py:166
  112.4 1.1 convolution_bitcast_fusion
  113.5 1.1 convolution_bitcast_fusion.2
  114.7 1.1 convolution_bitcast_fusion.1
  115.8 9.5 %all-to-all-done.4 = bf16[24,8,512]{2,1,0:T(8,128)(2,1)S(1)} async-done(((bf16[24,8,512]{2,1,0:T(8,128)(2,1)}), bf16[24,8,512]{2,1,0:T(8,128)(2,1)S(1)}, u32[]{:S(2)}, u32[]{:S(2)}) %all-to-all-start.4) | async-done | bytes 196640 | tf_op jit(solution)/shard_map/all_to_all | solution.py:166
  125.3 0.3 reshape.1007
  125.6 0.1 reduce_sum.59
  125.7 0.1 broadcast_select_fusion.4
  125.9 0.1 broadcast_select_fusion.16
  126.0 0.6 pad_maximum_fusion.2
  (19 shorter events, 0.4 us)
Async XLA Ops:
  32.6 14.5 %copy-start.1 = (bf16[1,512,256]{2,1,0:T(8,128)(2,1)S(1)}, bf16[1,512,256]{2,1,0:T(8,128)(2,1)}, u32[]{:S(2)}) copy-start(bf16[1,512,256]{2,1,0:T(8,128)(2,1)} %param.12) | copy-start | bytes 786436
  47.0 1.0 copy-start.2
  47.1 1.2 copy-start
  54.2 17.2 %all-to-all-start.2 = ((bf16[4,3,32,384]{3,2,1,0:T(8,128)(2,1)}), bf16[4,3,32,384]{3,2,1,0:T(8,128)(2,1)S(1)}, u32[]{:S(2)}, u32[]{:S(2)}) async-start(bf16[4,3,32,384]{3,2,1,0:T(8,128)(2,1)} %fusion.2), calls=%async_computation.2 | async-start | bytes 589824 | tf_op jit(solution)/shard_map/all_to_all | solution.py:137
  88.8 16.6 %all-to-all-start.3 = ((bf16[4,24,8,512]{3,2,1,0:T(8,128)(2,1)}), bf16[4,24,8,512]{3,2,1,0:T(8,128)(2,1)S(1)}, u32[]{:S(2)}, u32[]{:S(2)}) async-start(bf16[4,24,8,512]{3,2,1,0:T(8,128)(2,1)} %bitcast.24), calls=%async_computation.3 | async-start | bytes 1572864 | tf_op jit(solution)/shard_map/all_to_all | solution.py:157
  106.3 19.0 %all-to-all-start.4 = ((bf16[24,8,512]{2,1,0:T(8,128)(2,1)}), bf16[24,8,512]{2,1,0:T(8,128)(2,1)S(1)}, u32[]{:S(2)}, u32[]{:S(2)}) async-start(bf16[24,8,512]{2,1,0:T(8,128)(2,1)} %fusion.1), calls=%async_computation.4 | async-start | bytes 393216 | tf_op jit(solution)/shard_map/all_to_all | solution.py:166

commit v5 on v4

--- a/solution.py
+++ b/solution.py
@@ -33,12 +33,6 @@
     return lax.dot_general(
         left, right, (((left_dim,), (right_dim,)), ((), ())), preferred_element_type=F32
     )
-
-
-def own_kept(own, received, axis):
-    place = lax.broadcasted_iota(jnp.int32, own.shape, 0)
-    mine = place == lax.axis_index(axis)
-    return jnp.sum(jnp.where(mine, own, received.astype(F32)), axis=0)
 
 
 def full(shape):
@@ -103,7 +97,6 @@
     block = near * per_owner
     slots = size_x * block
     units = gate_weight.shape[1]
-    share_units = units // (size_y * size_c)
     table = slot_table(labels, counts)
 
     source = jnp.stack([rows, cotangent])
@@ -130,12 +123,18 @@
             contract(down_weight, flat_cot, 1, 1),
         ]
     )
-    parts = parts.reshape(3, size_y, size_c, share_units, slots).transpose(2, 1, 0, 3, 4)
-    parts = with_layout_constraint(parts, Layout(major_to_minor=(0, 1, 2, 3, 4)))
+    half = units // size_c
+    parts = parts.reshape(3, size_c, half, slots).transpose(1, 0, 2, 3)
+    parts = with_layout_constraint(parts, Layout(major_to_minor=(0, 1, 2, 3)))
     pair = lax.all_to_all(parts, "width_core", 0, 0, tiled=True)
     pair = pair[0] + pair[1]
-    sent = lax.all_to_all(pair.astype(BF16), "width_y", 0, 0, tiled=True)
-    gate, up_value, dhid = own_kept(pair, sent, "width_y")
+    sent = jnp.broadcast_to(pair.astype(BF16), (size_y,) + pair.shape)
+    sent = lax.all_to_all(sent, "width_y", 0, 0, tiled=True)
+    place_y = lax.axis_index("width_y")
+    other = lax.broadcasted_iota(jnp.int32, (size_y, 1, 1, 1), 0) != place_y
+    gate, up_value, dhid = pair + jnp.sum(
+        jnp.where(other, sent.astype(F32), 0.0), axis=0
+    )
     sigma = jax.nn.sigmoid(gate)
     silu = gate * sigma
     share = jnp.stack(
@@ -145,7 +144,7 @@
             (dhid * silu).astype(BF16),
         ]
     )
-    acts = lax.all_gather(share, WIDTH, axis=0, tiled=False)
+    acts = lax.all_gather(share, "width_core", axis=0, tiled=False)
     hidden = acts[:, 0].reshape(units, slots)
     dgate = acts[:, 1].reshape(units, slots)
     dup = acts[:, 2].reshape(units, slots)

time: 127 us -> 135 us (1.063)
  waiting for transfers between devices: 33.5 us -> 49.1 us
  blocking collectives: 64.5 us -> 51.1 us
  starting transfers between devices: 15.8 us -> 19.3 us
    all_to_all x1, waiting for transfers between devices: 11 us -> 27 us  [shards(): sent = lax.all_to_all(sent, 'width_y', 0, 0, tiled=True)]
    all_gather x1, blocking collectives: 15.7 us -> 2.23 us  [shards(): acts = lax.all_gather(share, 'width_core', axis=0, tiled=False)]
    all_to_all x1, starting transfers between devices: 3.49 us -> 6.49 us  [shards(): lax.all_to_all(sent.reshape(size_x, near, 8, width), 'hidden_x', 0, 0, ti...]
    reduce_sum x1, other arithmetic: 0.15 us -> 1.63 us  [shards(): jnp.sum(jnp.where(other, sent.astype(F32), 0.0), axis=0)]
where the time goes in v5:
time: 135 us; the launch traced here: 134 us
  blocking collectives  51.1 us (38%)
  waiting for transfers between devices  49.1 us (36%)
  starting transfers between devices  19.3 us (14%)
  other arithmetic  5.83 us (4%)
  matrix products  4.35 us (3%)
  local copies, waits for them, and re-layouts  2.44 us (2%)
  Pallas kernels  1.42 us (1%)
    all_to_all x1, blocking collectives, shards(): lax.all_to_all(send.reshape(near, 2 * per_owner, width), NEAR, 0, 0, tile...  29.8 us
    all_to_all x1, waiting for transfers between devices, shards(): sent = lax.all_to_all(sent, 'width_y', 0, 0, tiled=True)  27 us
    all_gather x1, blocking collectives, shards(): lax.all_gather(recv.reshape(2, block, width), 'hidden_x', axis=0, tiled=F...  14.4 us
    all_to_all x1, waiting for transfers between devices, shards(): lax.all_to_all(sent.reshape(size_x, near, 8, width), 'hidden_x', 0, 0, ti...  12.6 us
    all_to_all x1, waiting for transfers between devices, shards(): result = lax.all_to_all(result, NEAR, 0, 0, tiled=True)  9.52 us
    all_to_all x1, starting transfers between devices, shards(): result = lax.all_to_all(result, NEAR, 0, 0, tiled=True)  6.61 us
    all_to_all x1, starting transfers between devices, shards(): lax.all_to_all(sent.reshape(size_x, near, 8, width), 'hidden_x', 0, 0, ti...  6.49 us
    all_to_all x1, starting transfers between devices, shards(): sent = lax.all_to_all(sent, 'width_y', 0, 0, tiled=True)  6.2 us
  transfers between devices with their start and end apart: 3, of which 3 were waited for; matrix products, arithmetic and copies ran while one was open for 3% of the time, Pallas kernels for 0%

profile of v5, /device:TPU:8, one launch (start us, length us, event | category | flops | bytes accessed | tf_op | source)
XLA Modules:
  0.0 134.3 jit_solution(8848887192160715878)
XLA Ops:
  0.6 1.0 fusion.5
  1.7 0.7 maximum_convert_fusion
  2.4 0.1 select_reduce_fusion.2
  2.6 29.8 %all_to_all.25 = bf16[24,8,512]{2,1,0:T(8,128)(2,1)S(1)} all-to-all(bf16[24,8,512]{2,1,0:T(8,128)(2,1)S(1)} %bitcast.167), channel_id=1, replica_groups=mesh['branch'=2,'hidden_x'=4,'hidden_z'=12,'width_y'=4,'width_core'=2] {..., dimensions={0} | all-to-all | bytes 393216 | tf_op jit(solution)/shard_map/all_to_all | solution.py:111
  32.4 0.2 copy.31
  32.6 14.4 %all_gather.9 = bf16[4,2,96,512]{3,2,1,0:T(8,128)(2,1)S(1)} all-gather(bf16[1,2,96,512]{3,2,1,0:T(8,128)(2,1)S(1)} %copy.32), channel_id=1, replica_groups=mesh['branch'=2,'hidden_x'=4,'hidden_z'=12,'width_y'=4,'width_core'=2] {..., dimensions={0}, use_global_device_ids=true | all-gather | bytes 983040 | tf_op jit(solution)/shard_map/all_gather | solution.py:115
  47.1 0.3 fusion.11
  47.5 0.5 copy-done.1
  48.0 0.3 fusion.9
  48.3 0.3 fusion.7
  48.7 4.7 %all_to_all.26 = f32[2,3,128,384]{3,2,1,0:T(8,128)S(1)} all-to-all(f32[2,3,128,384]{3,2,1,0:T(8,128)S(1)} %maximum_bitcast_fusion), channel_id=1, replica_groups=mesh['branch'=2,'hidden_x'=4,'hidden_z'=12,'width_y'=4,'width_core'=2] {..., dimensions={0} | all-to-all | bytes 2359296 | tf_op jit(solution)/shard_map/all_to_all | solution.py:129
  53.5 1.2 broadcast_in_dim.225
  54.7 6.2 %all-to-all-start.2 = ((bf16[4,3,128,384]{3,2,1,0:T(8,128)(2,1)}), bf16[4,3,128,384]{3,2,1,0:T(8,128)(2,1)}, u32[]{:S(2)}, u32[]{:S(2)}) async-start(bf16[4,3,128,384]{3,2,1,0:T(8,128)(2,1)} %broadcast_in_dim.225), calls=%async_computation.2 | async-start | bytes 2359296 | tf_op jit(solution)/shard_map/all_to_all | solution.py:132
  60.9 27.0 %all-to-all-done.2 = bf16[4,3,128,384]{3,2,1,0:T(8,128)(2,1)} async-done(((bf16[4,3,128,384]{3,2,1,0:T(8,128)(2,1)}), bf16[4,3,128,384]{3,2,1,0:T(8,128)(2,1)}, u32[]{:S(2)}, u32[]{:S(2)}) %all-to-all-start.2) | async-done | bytes 1179680 | tf_op jit(solution)/shard_map/all_to_all | solution.py:132
  87.9 1.6 %select_reduce_fusion = f32[3,128,384]{2,1,0:T(8,128)S(1)} fusion(bf16[4,3,128,384]{3,2,1,0:T(8,128)(2,1)} %all-to-all-done.2, pred[4]{0:T(512)(128)(4,1)S(1)} %iota_compare_fusion.2), kind=kLoop, calls=%fused_computation | loop fusion | flops 1622016 | bytes 1769476 | tf_op jit(solution)/shard_map/reduce_sum | solution.py:135
  89.5 0.1 fusion.3
  89.6 0.1 multiply_convert_fusion.2
  89.8 2.2 %all-gather = bf16[6,128,384]{2,1,0:T(8,128)(2,1)S(1)} all-gather(bf16[3,128,384]{2,1,0:T(8,128)(2,1)S(1)} %pad_maximum_fusion), channel_id=2, replica_groups=mesh['branch'=2,'hidden_x'=4,'hidden_z'=12,'width_y'=4,'width_core'=2] {..., dimensions={0}, use_global_device_ids=true | all-gather | bytes 884736 | tf_op jit(solution)/shard_map/all_gather | solution.py:147
  92.0 1.4 %second_products.1 = (bf16[48,2,8,512]{3,2,1,0:T(8,128)(2,1)}, f32[12,2,8,512]{3,2,1,0:T(8,128)S(1)}) custom-call(s32[1]{0:T(128)} %bitcast.2.place_ref, bf16[2,3,128,384]{3,2,1,0:T(8,128)(2,1)S(1)} %bitcast.153, bf16[512,256]{1,0:T(8,128)(2,1)S(1)} %bitcast.157, bf16[512,256]{1,0:T(8,128)(2,1)S(1)} %bitcast.156, bf16[256,512]{1,0:T(8,128)(2,1)S(1)} %bitcast.155), custom_call_target="tpu_custom_call" | custom-call | tf_op jit(solution)/shard_map/second_products/pallas_call | solution.py:70
  93.5 6.5 %all-to-all-start.3 = ((bf16[4,24,8,512]{3,2,1,0:T(8,128)(2,1)}), bf16[4,24,8,512]{3,2,1,0:T(8,128)(2,1)S(1)}, u32[]{:S(2)}, u32[]{:S(2)}) async-start(bf16[4,24,8,512]{3,2,1,0:T(8,128)(2,1)} %bitcast.24), calls=%async_computation.3 | async-start | bytes 1572864 | tf_op jit(solution)/shard_map/all_to_all | solution.py:156
  100.0 12.6 %all-to-all-done.3 = bf16[4,24,8,512]{3,2,1,0:T(8,128)(2,1)S(1)} async-done(((bf16[4,24,8,512]{3,2,1,0:T(8,128)(2,1)}), bf16[4,24,8,512]{3,2,1,0:T(8,128)(2,1)S(1)}, u32[]{:S(2)}, u32[]{:S(2)}) %all-to-all-start.3) | async-done | bytes 786464 | tf_op jit(solution)/shard_map/all_to_all | solution.py:156
  112.5 0.2 select_reduce_fusion.1
  112.8 0.7 fusion.1
  113.5 6.6 %all-to-all-start.4 = ((bf16[24,8,512]{2,1,0:T(8,128)(2,1)}), bf16[24,8,512]{2,1,0:T(8,128)(2,1)S(1)}, u32[]{:S(2)}, u32[]{:S(2)}) async-start(bf16[24,8,512]{2,1,0:T(8,128)(2,1)} %fusion.1), calls=%async_computation.4 | async-start | bytes 393216 | tf_op jit(solution)/shard_map/all_to_all | solution.py:165
  120.2 1.1 convolution_bitcast_fusion
  121.3 1.1 convolution_bitcast_fusion.1
  122.4 1.1 convolution_bitcast_fusion.2
  123.5 9.5 %all-to-all-done.4 = bf16[24,8,512]{2,1,0:T(8,128)(2,1)S(1)} async-done(((bf16[24,8,512]{2,1,0:T(8,128)(2,1)}), bf16[24,8,512]{2,1,0:T(8,128)(2,1)S(1)}, u32[]{:S(2)}, u32[]{:S(2)}) %all-to-all-start.4) | async-done | bytes 196640 | tf_op jit(solution)/shard_map/all_to_all | solution.py:165
  133.1 0.3 reshape.1012
  133.3 0.1 reduce_sum.59
  133.5 0.1 broadcast_select_fusion.10
  133.7 0.6 pad_maximum_fusion.1
  (21 shorter events, 0.6 us)
Async XLA Ops:
  32.6 14.5 %copy-start.2 = (bf16[1,512,256]{2,1,0:T(8,128)(2,1)S(1)}, bf16[1,512,256]{2,1,0:T(8,128)(2,1)}, u32[]{:S(2)}) copy-start(bf16[1,512,256]{2,1,0:T(8,128)(2,1)} %param.11) | copy-start | bytes 786436
  47.0 1.0 copy-start.1
  47.1 1.2 copy-start
  54.7 33.2 %all-to-all-start.2 = ((bf16[4,3,128,384]{3,2,1,0:T(8,128)(2,1)}), bf16[4,3,128,384]{3,2,1,0:T(8,128)(2,1)}, u32[]{:S(2)}, u32[]{:S(2)}) async-start(bf16[4,3,128,384]{3,2,1,0:T(8,128)(2,1)} %broadcast_in_dim.225), calls=%async_computation.2 | async-start | bytes 2359296 | tf_op jit(solution)/shard_map/all_to_all | solution.py:132
  93.5 19.1 %all-to-all-start.3 = ((bf16[4,24,8,512]{3,2,1,0:T(8,128)(2,1)}), bf16[4,24,8,512]{3,2,1,0:T(8,128)(2,1)S(1)}, u32[]{:S(2)}, u32[]{:S(2)}) async-start(bf16[4,24,8,512]{3,2,1,0:T(8,128)(2,1)} %bitcast.24), calls=%async_computation.3 | async-start | bytes 1572864 | tf_op jit(solution)/shard_map/all_to_all | solution.py:156
  113.5 19.6 %all-to-all-start.4 = ((bf16[24,8,512]{2,1,0:T(8,128)(2,1)}), bf16[24,8,512]{2,1,0:T(8,128)(2,1)S(1)}, u32[]{:S(2)}, u32[]{:S(2)}) async-start(bf16[24,8,512]{2,1,0:T(8,128)(2,1)} %fusion.1), calls=%async_computation.4 | async-start | bytes 393216 | tf_op jit(solution)/shard_map/all_to_all | solution.py:165

commit v6 on v3

--- a/solution.py
+++ b/solution.py
@@ -2,7 +2,6 @@
 import jax.numpy as jnp
 from jax import lax
 from jax.experimental import pallas as pl
-from jax.experimental.layout import Layout, with_layout_constraint
 from jax.experimental.pallas import tpu as pltpu
 from jax.sharding import Mesh, PartitionSpec as P
 
@@ -17,16 +16,100 @@
 NEAR = ("branch", "hidden_z")
 
 
-def slot_table(labels, counts):
-    mb, row_dev = labels.shape
-    shape = (2, mb, row_dev, row_dev)
-    branch, _, here, other = (lax.broadcasted_iota(jnp.int32, shape, d) for d in range(4))
-    counted = (other < counts[None, :, :, None]) & (labels[None, :, None, :] == branch)
-    rank = jnp.sum(jnp.where(counted & (other < here), 1, 0), axis=3)
-    own = jnp.sum(jnp.where(counted & (other == here), 1, 0), axis=3)
-    rank = jnp.where(own == 1, rank, -1)
-    slot = lax.broadcasted_iota(jnp.int32, (2, CAP, mb, row_dev), 1)
-    return rank[:, None] == slot
+def slot_picks(labels_ref, counts_ref, shape):
+    row_dev = labels_ref.shape[1]
+    lower = lax.broadcasted_iota(jnp.int32, shape, 0) == 0
+    picks = [[[None] * row_dev for _ in range(CAP)] for _ in range(2)]
+    for branch in range(2):
+        slot = []
+        for m in range(2):
+            seen = jnp.int32(0)
+            places = []
+            for p in range(row_dev):
+                chosen = (p < counts_ref[0, m]) & (labels_ref[m, p] == branch)
+                places.append(jnp.where(chosen, seen, -1))
+                seen = seen + jnp.where(chosen, 1, 0)
+            slot.append(places)
+        for p in range(row_dev):
+            place = jnp.where(lower, slot[0][p], slot[1][p])
+            for s in range(CAP):
+                picks[branch][s][p] = place == s
+    return picks
+
+
+def pack_kernel(
+    labels_in, counts_in, rows_in, cot_in, send_ref,
+    labels_ref, counts_ref, rows_ref, cot_ref, scratch, sems,
+):
+    row_dev, mb, width = rows_ref.shape
+    copies = [
+        pltpu.make_async_copy(source, target, sems.at[i])
+        for i, (source, target) in enumerate(
+            (
+                (labels_in, labels_ref),
+                (counts_in, counts_ref),
+                (rows_in, rows_ref),
+                (cot_in, cot_ref),
+            )
+        )
+    ]
+    for copy in copies:
+        copy.start()
+    for copy in copies:
+        copy.wait()
+    picks = slot_picks(labels_ref, counts_ref, (mb, width))
+    sources = [
+        [ref[p].astype(F32) for p in range(row_dev)] for ref in (rows_ref, cot_ref)
+    ]
+    for branch in range(2):
+        for which in range(2):
+            for s in range(CAP):
+                value = jnp.zeros((mb, width), F32)
+                for p in range(row_dev):
+                    value = jnp.where(picks[branch][s][p], sources[which][p], value)
+                scratch[branch, pl.ds((which * CAP + s) * mb, mb), :] = value
+        tile = scratch[branch].astype(BF16)
+        for peer in range(send_ref.shape[1]):
+            send_ref[branch, peer] = tile
+
+
+def finish_kernel(labels_ref, counts_ref, recv_ref, out_ref, back_ref, scratch):
+    row_dev, mb, width = out_ref.shape
+    peers = recv_ref.shape[0] // 2
+    picks = slot_picks(labels_ref, counts_ref, (mb, width))
+    for branch in range(2):
+        total = recv_ref[branch * peers].astype(F32)
+        for peer in range(1, peers):
+            total = total + recv_ref[branch * peers + peer].astype(F32)
+        scratch[branch] = total
+    for which, ref in enumerate((out_ref, back_ref)):
+        for p in range(row_dev):
+            value = jnp.zeros((mb, width), F32)
+            for branch in range(2):
+                for s in range(CAP):
+                    value = jnp.where(
+                        picks[branch][s][p],
+                        scratch[branch, pl.ds((which * CAP + s) * mb, mb), :],
+                        value,
+                    )
+            ref[p] = value.astype(BF16)
+
+
+def first_kernel(every_ref, gate_ref, up_ref, down_ref, parts_ref):
+    size_x, _, block, width = every_ref.shape
+    size_c, size_y, _, share_units, slots = parts_ref.shape
+    rows = every_ref[:, 0].reshape(slots, width)
+    cot = every_ref[:, 1].reshape(slots, width)
+    sums = (
+        contract(gate_ref[...], rows, 0, 1),
+        contract(up_ref[...], rows, 0, 1),
+        contract(down_ref[...], cot, 1, 1),
+    )
+    for kind, total in enumerate(sums):
+        for y in range(size_y):
+            for c in range(size_c):
+                start = (y * size_c + c) * share_units
+                parts_ref[c, y, kind] = total[start : start + share_units]
 
 
 def contract(left, right, left_dim, right_dim):
@@ -68,6 +151,62 @@
     own_ref[...] = scratch[pl.ds(place_ref[0] * own_tiles, own_tiles)]
 
 
+GRANT = pltpu.CompilerParams(vmem_limit_bytes=12 * 1024 * 1024)
+SCALARS = pl.BlockSpec(memory_space=pltpu.SMEM)
+
+
+def pack(labels, counts, rows, cotangent, peers):
+    row_dev, mb, width = rows.shape
+    shape = (2, peers, 2 * CAP * mb, width)
+    return pl.pallas_call(
+        pack_kernel,
+        out_shape=jax.ShapeDtypeStruct(shape, BF16),
+        in_specs=[pl.BlockSpec(memory_space=pltpu.HBM)] * 4,
+        out_specs=full(shape),
+        scratch_shapes=[
+            pltpu.SMEM(labels.shape, jnp.int32),
+            pltpu.SMEM(counts.shape, jnp.int32),
+            pltpu.VMEM(rows.shape, BF16),
+            pltpu.VMEM(rows.shape, BF16),
+            pltpu.VMEM((2, 2 * CAP * mb, width), F32),
+            pltpu.SemaphoreType.DMA((4,)),
+        ],
+        name="pack",
+    )(labels, counts, rows, cotangent)
+
+
+def finish(labels, counts, recv, mb):
+    shape = (labels.shape[1], mb, recv.shape[2])
+    return pl.pallas_call(
+        finish_kernel,
+        out_shape=(jax.ShapeDtypeStruct(shape, BF16),) * 2,
+        in_specs=[SCALARS, SCALARS, full(recv.shape)],
+        out_specs=(full(shape),) * 2,
+        scratch_shapes=[pltpu.VMEM((2,) + recv.shape[1:], F32)],
+        compiler_params=GRANT,
+        name="finish",
+    )(labels, counts, recv)
+
+
+def first_products(every, gate_weight, up_weight, down_weight, size_c, size_y):
+    units = gate_weight.shape[1]
+    slots = every.shape[0] * every.shape[2]
+    shape = (size_c, size_y, 3, units // (size_c * size_y), slots)
+    return pl.pallas_call(
+        first_kernel,
+        out_shape=jax.ShapeDtypeStruct(shape, F32),
+        in_specs=[
+            full(every.shape),
+            full(gate_weight.shape),
+            full(up_weight.shape),
+            full(down_weight.shape),
+        ],
+        out_specs=full(shape),
+        compiler_params=GRANT,
+        name="first_products",
+    )(every, gate_weight, up_weight, down_weight)
+
+
 def second_products(place, acts, gate_weight, up_weight, down_weight, size_x):
     slots = acts.shape[3]
     width = down_weight.shape[1]
@@ -88,32 +227,26 @@
         ],
         out_specs=(full(shape), full(own_shape)),
         scratch_shapes=[pltpu.VMEM(shape, F32)],
+        compiler_params=GRANT,
         name="second_products",
     )(place, acts, gate_weight, up_weight, down_weight)
 
 
 def shards(rows, cotangent, labels, counts, gate_weight, up_weight, down_weight):
     gate_weight, up_weight, down_weight = gate_weight[0], up_weight[0], down_weight[0]
-    mb, row_dev, width = rows.shape
+    mb, _, width = rows.shape
     size_x, size_z = lax.axis_size("hidden_x"), lax.axis_size("hidden_z")
     size_y, size_c = lax.axis_size("width_y"), lax.axis_size("width_core")
     near = 2 * size_z
+    counts = counts.T
     per_owner = mb * CAP
     block = near * per_owner
     slots = size_x * block
     units = gate_weight.shape[1]
-    share_units = units // (size_y * size_c)
-    table = slot_table(labels, counts)
-
-    source = jnp.stack([rows, cotangent])
-    packed = jnp.sum(
-        jnp.where(
-            table[:, None, :, :, :, None], source[None, :, None].astype(F32), 0.0
-        ),
-        axis=4,
-    ).astype(BF16)
-    packed = packed.reshape(2, 1, 2 * per_owner, width)
-    send = jnp.broadcast_to(packed, (2, size_z, 2 * per_owner, width))
+
+    send = pack(
+        labels, counts, rows.transpose(1, 0, 2), cotangent.transpose(1, 0, 2), size_z
+    )
     recv = lax.all_to_all(
         send.reshape(near, 2 * per_owner, width), NEAR, 0, 0, tiled=True
     )
@@ -122,15 +255,7 @@
     flat_rows = every[:, 0].reshape(slots, width)
     flat_cot = every[:, 1].reshape(slots, width)
 
-    parts = jnp.stack(
-        [
-            contract(gate_weight, flat_rows, 0, 1),
-            contract(up_weight, flat_rows, 0, 1),
-            contract(down_weight, flat_cot, 1, 1),
-        ]
-    )
-    parts = parts.reshape(3, size_y, size_c, share_units, slots).transpose(2, 1, 0, 3, 4)
-    parts = with_layout_constraint(parts, Layout(major_to_minor=(0, 1, 2, 3, 4)))
+    parts = first_products(every, gate_weight, up_weight, down_weight, size_c, size_y)
     pair = lax.all_to_all(parts, "width_core", 0, 0, tiled=True)
     pair = pair[0] + pair[1]
     sent = lax.all_to_all(pair.astype(BF16), "width_y", 0, 0, tiled=True)
@@ -163,23 +288,14 @@
     result = jnp.sum(jnp.where(other, sent.astype(F32), 0.0), axis=0)
     result = (own.reshape(near, 8, width) + result).astype(BF16)
     result = lax.all_to_all(result, NEAR, 0, 0, tiled=True)
-    result = jnp.sum(
-        result.reshape(2, size_z, 2, CAP, mb, width).astype(F32), axis=1
-    )
-    result = lax.optimization_barrier(result).astype(BF16)
-    finals = []
-    for which in (0, 1):
-        per_row = []
-        for p in range(row_dev):
-            value = jnp.zeros((), BF16)
-            for branch in (0, 1):
-                for s in range(CAP):
-                    value = jnp.where(
-                        table[branch, s, :, p : p + 1], result[branch, which, s], value
-                    )
-            per_row.append(value)
-        finals.append(jnp.stack(per_row, axis=1))
-    return (finals[0], finals[1], grad_gate[None], grad_up[None], grad_down[None])
+    output, grad_rows = finish(labels, counts, result, mb)
+    return (
+        output.transpose(1, 0, 2),
+        grad_rows.transpose(1, 0, 2),
+        grad_gate[None],
+        grad_up[None],
+        grad_down[None],
+    )
 
 
 def solution(mesh):

time: 130 us -> 126 us (0.969)
  other arithmetic: 4.89 us -> 1.95 us
  Pallas kernels: 2.84 us -> 4.69 us
    pallas_call x0 -> x3, Pallas kernels: none -> 3.27 us  [the longest x1 1.47 us: pack(): pl.pallas_call(pack_kernel, out_shape=jax.ShapeDtypeStruct(shape, BF16),...]
    pallas_call x1, Pallas kernels: 2.84 us -> 1.42 us  [second_products(): pl.pallas_call(second_kernel, out_shape=(jax.ShapeDtypeStruct(shape, BF16...]
    dot_general x6 -> x3, matrix products: 4.38 us -> 3.37 us  [contract(): lax.dot_general(left, right, (((left_dim,), (right_dim,)), ((), ())), pre...]
where the time goes in v6:
time: 126 us; the launch traced here: 125 us
  blocking collectives  64.6 us (51%)
  waiting for transfers between devices  33.5 us (27%)
  starting transfers between devices  15.8 us (13%)
  Pallas kernels  4.69 us (4%)
  matrix products  3.37 us (3%)
  other arithmetic  1.95 us (2%)
    all_to_all x1, blocking collectives, shards(): lax.all_to_all(send.reshape(near, 2 * per_owner, width), NEAR, 0, 0, tile...  30 us
    all_gather x1, blocking collectives, shards(): acts = lax.all_gather(share, WIDTH, axis=0, tiled=False)  15.7 us
    all_gather x1, blocking collectives, shards(): lax.all_gather(recv.reshape(2, block, width), 'hidden_x', axis=0, tiled=F...  14.3 us
    all_to_all x1, waiting for transfers between devices, shards(): lax.all_to_all(sent.reshape(size_x, near, 8, width), 'hidden_x', 0, 0, ti...  13 us
    all_to_all x1, waiting for transfers between devices, shards(): sent = lax.all_to_all(pair.astype(BF16), 'width_y', 0, 0, tiled=True)  11 us
    all_to_all x1, waiting for transfers between devices, shards(): result = lax.all_to_all(result, NEAR, 0, 0, tiled=True)  9.51 us
    all_to_all x1, starting transfers between devices, shards(): sent = lax.all_to_all(pair.astype(BF16), 'width_y', 0, 0, tiled=True)  6.19 us
    all_to_all x1, starting transfers between devices, shards(): result = lax.all_to_all(result, NEAR, 0, 0, tiled=True)  6.09 us
  transfers between devices with their start and end apart: 3, of which 3 were waited for; matrix products, arithmetic and copies ran while one was open for 3% of the time, Pallas kernels for 0%

profile of v6, /device:TPU:8, one launch (start us, length us, event | category | flops | bytes accessed | tf_op | source)
XLA Modules:
  0.0 125.1 jit_solution(16683888444404228269)
XLA Ops:
  0.6 1.5 %pack.1 = bf16[2,12,8,512]{3,2,1,0:T(8,128)(2,1)} custom-call(s32[2,3]{1,0:T(2,128)} %labels_ref.1, s32[1,2]{1,0:T(1,128)} %bitcast.51, bf16[3,2,512]{2,1,0:T(2,128)(2,1)} %bitcast.62, bf16[3,2,512]{2,1,0:T(2,128)(2,1)} %bitcast.63), custom_call_target="tpu_custom_call" | custom-call | tf_op jit(solution)/shard_map/pack/pallas_call | solution.py:161
  2.1 30.0 %all_to_all.25 = bf16[24,8,512]{2,1,0:T(8,128)(2,1)S(1)} all-to-all(bf16[24,8,512]{2,1,0:T(8,128)(2,1)} %bitcast.58), channel_id=1, replica_groups=mesh['branch'=2,'hidden_x'=4,'hidden_z'=12,'width_y'=4,'width_core'=2] {..., dimensions={0} | all-to-all | bytes 393216 | tf_op jit(solution)/shard_map/all_to_all | solution.py:250
  32.1 0.0 copy-start
  32.1 0.0 copy-start.1
  32.1 0.1 copy.15
  32.1 0.2 copy.16
  32.4 14.3 %all_gather.9.every_ref = bf16[4,2,96,512]{3,2,1,0:T(8,128)(2,1)S(1)} all-gather(bf16[1,2,96,512]{3,2,1,0:T(8,128)(2,1)S(1)} %copy.17), channel_id=1, replica_groups=mesh['branch'=2,'hidden_x'=4,'hidden_z'=12,'width_y'=4,'width_core'=2] {..., dimensions={0}, use_global_device_ids=true | all-gather | bytes 983040 | tf_op jit(solution)/shard_map/all_gather | solution.py:254
  46.7 0.0 copy-done
  46.7 0.0 copy-done.1
  46.7 0.0 copy-done.2
  46.7 0.6 first_products.1
  47.3 4.7 %all_to_all.26 = f32[2,4,3,32,384]{4,3,2,1,0:T(8,128)S(1)} all-to-all(f32[2,4,3,32,384]{4,3,2,1,0:T(8,128)S(1)} %first_products.1), channel_id=1, replica_groups=mesh['branch'=2,'hidden_x'=4,'hidden_z'=12,'width_y'=4,'width_core'=2] {..., dimensions={0} | all-to-all | bytes 2359296 | tf_op jit(solution)/shard_map/all_to_all | solution.py:259
  52.0 0.8 fusion.2
  52.7 6.2 %all-to-all-start.2 = ((bf16[4,3,32,384]{3,2,1,0:T(8,128)(2,1)}), bf16[4,3,32,384]{3,2,1,0:T(8,128)(2,1)S(1)}, u32[]{:S(2)}, u32[]{:S(2)}) async-start(bf16[4,3,32,384]{3,2,1,0:T(8,128)(2,1)} %fusion.2), calls=%async_computation.2 | async-start | bytes 589824 | tf_op jit(solution)/shard_map/all_to_all | solution.py:261
  58.9 11.0 %all-to-all-done.2 = bf16[4,3,32,384]{3,2,1,0:T(8,128)(2,1)S(1)} async-done(((bf16[4,3,32,384]{3,2,1,0:T(8,128)(2,1)}), bf16[4,3,32,384]{3,2,1,0:T(8,128)(2,1)S(1)}, u32[]{:S(2)}, u32[]{:S(2)}) %all-to-all-start.2) | async-done | bytes 294944 | tf_op jit(solution)/shard_map/all_to_all | solution.py:261
  70.0 0.2 select_reduce_fusion.1
  70.2 15.7 %all-gather = bf16[24,32,384]{2,1,0:T(8,128)(2,1)S(1)} all-gather(bf16[3,32,384]{2,1,0:T(8,128)(2,1)S(1)} %pad_maximum_fusion), channel_id=2, replica_groups=mesh['branch'=2,'hidden_x'=4,'hidden_z'=12,'width_y'=4,'width_core'=2] {..., dimensions={0}, use_global_device_ids=true | all-gather | bytes 663552 | tf_op jit(solution)/shard_map/all_gather | solution.py:272
  85.9 1.4 %second_products.1 = (bf16[48,2,8,512]{3,2,1,0:T(8,128)(2,1)}, f32[12,2,8,512]{3,2,1,0:T(8,128)S(1)}) custom-call(s32[1]{0:T(128)} %bitcast.1.place_ref, bf16[8,3,32,384]{3,2,1,0:T(8,128)(2,1)S(1)} %bitcast.43, bf16[512,256]{1,0:T(8,128)(2,1)S(1)} %bitcast.46, bf16[512,256]{1,0:T(8,128)(2,1)S(1)} %bitcast.48, bf16[256,512]{1,0:T(8,128)(2,1)S(1)} %bitcast.50), custom_call_target="tpu_custom_call" | custom-call | tf_op jit(solution)/shard_map/second_products/pallas_call | solution.py:215
  87.3 3.5 %all-to-all-start.3 = ((bf16[4,24,8,512]{3,2,1,0:T(8,128)(2,1)}), bf16[4,24,8,512]{3,2,1,0:T(8,128)(2,1)S(1)}, u32[]{:S(2)}, u32[]{:S(2)}) async-start(bf16[4,24,8,512]{3,2,1,0:T(8,128)(2,1)} %bitcast.14), calls=%async_computation.3 | async-start | bytes 1572864 | tf_op jit(solution)/shard_map/all_to_all | solution.py:281
  90.8 0.1 fusion.4
  90.8 13.0 %all-to-all-done.3 = bf16[4,24,8,512]{3,2,1,0:T(8,128)(2,1)S(1)} async-done(((bf16[4,24,8,512]{3,2,1,0:T(8,128)(2,1)}), bf16[4,24,8,512]{3,2,1,0:T(8,128)(2,1)S(1)}, u32[]{:S(2)}, u32[]{:S(2)}) %all-to-all-start.3) | async-done | bytes 786464 | tf_op jit(solution)/shard_map/all_to_all | solution.py:281
  103.8 0.2 select_reduce_fusion
  104.1 0.7 fusion.1
  104.8 6.1 %all-to-all-start.4 = ((bf16[24,8,512]{2,1,0:T(8,128)(2,1)}), bf16[24,8,512]{2,1,0:T(8,128)(2,1)S(1)}, u32[]{:S(2)}, u32[]{:S(2)}) async-start(bf16[24,8,512]{2,1,0:T(8,128)(2,1)} %fusion.1), calls=%async_computation.4 | async-start | bytes 393216 | tf_op jit(solution)/shard_map/all_to_all | solution.py:290
  110.9 0.1 fusion.5
  111.0 1.1 convolution_bitcast_fusion
  112.1 1.1 convolution_bitcast_fusion.1
  113.2 1.1 convolution_bitcast_fusion.2
  114.3 9.5 %all-to-all-done.4.recv_ref = bf16[24,8,512]{2,1,0:T(8,128)(2,1)S(1)} async-done(((bf16[24,8,512]{2,1,0:T(8,128)(2,1)}), bf16[24,8,512]{2,1,0:T(8,128)(2,1)S(1)}, u32[]{:S(2)}, u32[]{:S(2)}) %all-to-all-start.4) | async-done | bytes 196640 | tf_op jit(solution)/shard_map/all_to_all | solution.py:290
  123.8 0.0 copy-done.3
  123.8 0.0 copy-done.4
  123.9 1.2 finish.1
  (8 shorter events, 0.1 us)
Async XLA Ops:
  32.1 14.6 %copy-start = (bf16[1,512,256]{2,1,0:T(8,128)(2,1)S(1)}, bf16[1,512,256]{2,1,0:T(8,128)(2,1)}, u32[]{:S(2)}) copy-start(bf16[1,512,256]{2,1,0:T(8,128)(2,1)} %param.11) | copy-start | bytes 786436
  32.1 14.6 %copy-start.1 = (bf16[1,512,256]{2,1,0:T(8,128)(2,1)S(1)}, bf16[1,512,256]{2,1,0:T(8,128)(2,1)}, u32[]{:S(2)}) copy-start(bf16[1,512,256]{2,1,0:T(8,128)(2,1)} %param.12) | copy-start | bytes 786436
  32.1 14.6 %copy-start.2 = (bf16[1,256,512]{2,1,0:T(8,128)(2,1)S(1)}, bf16[1,256,512]{2,1,0:T(8,128)(2,1)}, u32[]{:S(2)}) copy-start(bf16[1,256,512]{2,1,0:T(8,128)(2,1)} %param.13) | copy-start | bytes 786436
  52.7 17.2 %all-to-all-start.2 = ((bf16[4,3,32,384]{3,2,1,0:T(8,128)(2,1)}), bf16[4,3,32,384]{3,2,1,0:T(8,128)(2,1)S(1)}, u32[]{:S(2)}, u32[]{:S(2)}) async-start(bf16[4,3,32,384]{3,2,1,0:T(8,128)(2,1)} %fusion.2), calls=%async_computation.2 | async-start | bytes 589824 | tf_op jit(solution)/shard_map/all_to_all | solution.py:261
  87.3 16.6 %all-to-all-start.3 = ((bf16[4,24,8,512]{3,2,1,0:T(8,128)(2,1)}), bf16[4,24,8,512]{3,2,1,0:T(8,128)(2,1)S(1)}, u32[]{:S(2)}, u32[]{:S(2)}) async-start(bf16[4,24,8,512]{3,2,1,0:T(8,128)(2,1)} %bitcast.14), calls=%async_computation.3 | async-start | bytes 1572864 | tf_op jit(solution)/shard_map/all_to_all | solution.py:281
  104.8 19.1 %all-to-all-start.4 = ((bf16[24,8,512]{2,1,0:T(8,128)(2,1)}), bf16[24,8,512]{2,1,0:T(8,128)(2,1)S(1)}, u32[]{:S(2)}, u32[]{:S(2)}) async-start(bf16[24,8,512]{2,1,0:T(8,128)(2,1)} %fusion.1), calls=%async_computation.4 | async-start | bytes 393216 | tf_op jit(solution)/shard_map/all_to_all | solution.py:290
  112.1 11.8 %copy-start.3 = (s32[2,3]{1,0:T(2,128)S(1)}, s32[2,3]{1,0:T(2,128)}, u32[]{:S(2)}) copy-start(s32[2,3]{1,0:T(2,128)} %labels_ref.1) | copy-start | bytes 76
  112.1 11.8 %copy-start.4 = (s32[2,1]{0,1:T(1,128)S(1)}, s32[2,1]{0,1:T(1,128)}, u32[]{:S(2)}) copy-start(s32[2,1]{0,1:T(1,128)} %param.10) | copy-start | bytes 28

commit v7 on v6

--- a/solution.py
+++ b/solution.py
@@ -97,7 +97,7 @@
 
 def first_kernel(every_ref, gate_ref, up_ref, down_ref, parts_ref):
     size_x, _, block, width = every_ref.shape
-    size_c, size_y, _, share_units, slots = parts_ref.shape
+    size_c, pieces, _, piece_units, slots = parts_ref.shape
     rows = every_ref[:, 0].reshape(slots, width)
     cot = every_ref[:, 1].reshape(slots, width)
     sums = (
@@ -106,10 +106,10 @@
         contract(down_ref[...], cot, 1, 1),
     )
     for kind, total in enumerate(sums):
-        for y in range(size_y):
-            for c in range(size_c):
-                start = (y * size_c + c) * share_units
-                parts_ref[c, y, kind] = total[start : start + share_units]
+        for c in range(size_c):
+            for piece in range(pieces):
+                start = (c * pieces + piece) * piece_units
+                parts_ref[c, piece, kind] = total[start : start + piece_units]
 
 
 def contract(left, right, left_dim, right_dim):
@@ -118,23 +118,17 @@
     )
 
 
-def own_kept(own, received, axis):
-    place = lax.broadcasted_iota(jnp.int32, own.shape, 0)
-    mine = place == lax.axis_index(axis)
-    return jnp.sum(jnp.where(mine, own, received.astype(F32)), axis=0)
-
-
 def full(shape):
     return pl.BlockSpec(shape, lambda: (0,) * len(shape))
 
 
 def second_kernel(place_ref, acts_ref, gate_ref, up_ref, down_ref, sent_ref, own_ref, scratch):
-    parts, kinds, share_units, slots = acts_ref.shape
-    units = parts * share_units
+    size_c, pieces, _, piece_units, slots = acts_ref.shape
+    units = size_c * pieces * piece_units
     width = down_ref.shape[1]
-    hidden = acts_ref[:, 0].reshape(units, slots)
-    dgate = acts_ref[:, 1].reshape(units, slots)
-    dup = acts_ref[:, 2].reshape(units, slots)
+    hidden = acts_ref[:, :, 0].reshape(units, slots)
+    dgate = acts_ref[:, :, 1].reshape(units, slots)
+    dup = acts_ref[:, :, 2].reshape(units, slots)
     out = contract(hidden, down_ref[...], 0, 0)
     back = contract(dgate, gate_ref[...], 0, 1) + contract(dup, up_ref[...], 0, 1)
     tiles = slots // 8
@@ -188,10 +182,10 @@
     )(labels, counts, recv)
 
 
-def first_products(every, gate_weight, up_weight, down_weight, size_c, size_y):
+def first_products(every, gate_weight, up_weight, down_weight, size_c):
     units = gate_weight.shape[1]
     slots = every.shape[0] * every.shape[2]
-    shape = (size_c, size_y, 3, units // (size_c * size_y), slots)
+    shape = (size_c, 2, 3, units // (2 * size_c), slots)
     return pl.pallas_call(
         first_kernel,
         out_shape=jax.ShapeDtypeStruct(shape, F32),
@@ -208,7 +202,7 @@
 
 
 def second_products(place, acts, gate_weight, up_weight, down_weight, size_x):
-    slots = acts.shape[3]
+    slots = acts.shape[4]
     width = down_weight.shape[1]
     shape = (slots // 8, 2, 8, width)
     own_shape = (slots // 8 // size_x, 2, 8, width)
@@ -255,24 +249,29 @@
     flat_rows = every[:, 0].reshape(slots, width)
     flat_cot = every[:, 1].reshape(slots, width)
 
-    parts = first_products(every, gate_weight, up_weight, down_weight, size_c, size_y)
+    parts = first_products(every, gate_weight, up_weight, down_weight, size_c)
     pair = lax.all_to_all(parts, "width_core", 0, 0, tiled=True)
     pair = pair[0] + pair[1]
-    sent = lax.all_to_all(pair.astype(BF16), "width_y", 0, 0, tiled=True)
-    gate, up_value, dhid = own_kept(pair, sent, "width_y")
-    sigma = jax.nn.sigmoid(gate)
-    silu = gate * sigma
-    share = jnp.stack(
-        [
-            (silu * up_value).astype(BF16),
-            (dhid * up_value * sigma * (1.0 + gate * (1.0 - sigma))).astype(BF16),
-            (dhid * silu).astype(BF16),
+    low = [(i, i ^ 1) for i in range(size_y)]
+    high = [(i, (i + 1 if i % 2 else i - 1) % size_y) for i in range(size_y)]
+    sums = [pair[0], pair[1]]
+    for routes in ((low, high), (high, low)):
+        sums = [
+            own + lax.ppermute(own.astype(BF16), "width_y", route).astype(F32)
+            for own, route in zip(sums, routes)
         ]
-    )
-    acts = lax.all_gather(share, WIDTH, axis=0, tiled=False)
-    hidden = acts[:, 0].reshape(units, slots)
-    dgate = acts[:, 1].reshape(units, slots)
-    dup = acts[:, 2].reshape(units, slots)
+    share = []
+    for gate, up_value, dhid in sums:
+        sigma = jax.nn.sigmoid(gate)
+        silu = gate * sigma
+        share.append((silu * up_value).astype(BF16))
+        share.append((dhid * up_value * sigma * (1.0 + gate * (1.0 - sigma))).astype(BF16))
+        share.append((dhid * silu).astype(BF16))
+    share = jnp.stack(share).reshape(pair.shape)
+    acts = lax.all_gather(share, "width_core", axis=0, tiled=False)
+    hidden = acts[:, :, 0].reshape(units, slots)
+    dgate = acts[:, :, 1].reshape(units, slots)
+    dup = acts[:, :, 2].reshape(units, slots)
 
     place_x = lax.axis_index("hidden_x")
     sent, own = second_products(

time: 126 us -> 125 us (level)
  blocking collectives: 64.6 us -> 51.1 us
  starting transfers between devices: 15.8 us -> 25.3 us
  waiting for transfers between devices: 33.5 us -> 37.5 us
    ppermute x0 -> x4, starting transfers between devices: none -> 16.5 us  [shards(): lax.ppermute(own.astype(BF16), 'width_y', route).astype(F32)]
    ppermute x0 -> x4, waiting for transfers between devices: none -> 16 us  [shards(): lax.ppermute(own.astype(BF16), 'width_y', route).astype(F32)]
    all_gather x1, blocking collectives: 15.7 us -> 2.23 us  [shards(): acts = lax.all_gather(share, 'width_core', axis=0, tiled=False)]
    all_to_all x1 -> x0, waiting for transfers between devices: 11 us -> none  [shards(): sent = lax.all_to_all(pair.astype(BF16), 'width_y', 0, 0, tiled=True)]
    all_to_all x1 -> x0, starting transfers between devices: 6.19 us -> none  [shards(): sent = lax.all_to_all(pair.astype(BF16), 'width_y', 0, 0, tiled=True)]
  transfers between devices with their start and end apart: 3 -> 6, of which waited for: 3 -> 6; matrix products, arithmetic and copies ran while one was open for 3% -> 3% of each run, Pallas kernels for 0% -> 0%
where the time goes in v7:
time: 125 us
  blocking collectives  51.1 us (41%)
  waiting for transfers between devices  37.5 us (30%)
  starting transfers between devices  25.3 us (20%)
  Pallas kernels  4.72 us (4%)
  matrix products  3.37 us (3%)
  other arithmetic  1.47 us (1%)
    all_to_all x1, blocking collectives, shards(): lax.all_to_all(send.reshape(near, 2 * per_owner, width), NEAR, 0, 0, tile...  30 us
    ppermute x4, starting transfers between devices, shards(): lax.ppermute(own.astype(BF16), 'width_y', route).astype(F32)  16.5 us
    ppermute x4, waiting for transfers between devices, shards(): lax.ppermute(own.astype(BF16), 'width_y', route).astype(F32)  16 us
    all_gather x1, blocking collectives, shards(): lax.all_gather(recv.reshape(2, block, width), 'hidden_x', axis=0, tiled=F...  14.3 us
    all_to_all x1, waiting for transfers between devices, shards(): lax.all_to_all(sent.reshape(size_x, near, 8, width), 'hidden_x', 0, 0, ti...  12.8 us
    all_to_all x1, waiting for transfers between devices, shards(): result = lax.all_to_all(result, NEAR, 0, 0, tiled=True)  8.73 us
    all_to_all x1, starting transfers between devices, shards(): result = lax.all_to_all(result, NEAR, 0, 0, tiled=True)  5.34 us
    all_to_all x1, blocking collectives, shards(): pair = lax.all_to_all(parts, 'width_core', 0, 0, tiled=True)  4.68 us
  transfers between devices with their start and end apart: 6, of which 6 were waited for; matrix products, arithmetic and copies ran while one was open for 3% of the time, Pallas kernels for 0%

profile of v7, /device:TPU:8, one launch (start us, length us, event | category | flops | bytes accessed | tf_op | source)
XLA Modules:
  0.0 124.7 jit_solution(3441007577783259914)
XLA Ops:
  0.6 1.5 %pack.1 = bf16[2,12,8,512]{3,2,1,0:T(8,128)(2,1)} custom-call(s32[2,3]{1,0:T(2,128)} %labels_ref.1, s32[1,2]{1,0:T(1,128)} %bitcast.63, bf16[3,2,512]{2,1,0:T(2,128)(2,1)} %bitcast.75, bf16[3,2,512]{2,1,0:T(2,128)(2,1)} %bitcast.76), custom_call_target="tpu_custom_call" | custom-call | tf_op jit(solution)/shard_map/pack/pallas_call | solution.py:155
  2.1 30.0 %all_to_all.20 = bf16[24,8,512]{2,1,0:T(8,128)(2,1)S(1)} all-to-all(bf16[24,8,512]{2,1,0:T(8,128)(2,1)} %bitcast.70), channel_id=1, replica_groups=mesh['branch'=2,'hidden_x'=4,'hidden_z'=12,'width_y'=4,'width_core'=2] {..., dimensions={0} | all-to-all | bytes 393216 | tf_op jit(solution)/shard_map/all_to_all | solution.py:244
  32.1 0.1 copy.15
  32.1 0.2 copy.16
  32.4 14.3 %all_gather.6.every_ref = bf16[4,2,96,512]{3,2,1,0:T(8,128)(2,1)S(1)} all-gather(bf16[1,2,96,512]{3,2,1,0:T(8,128)(2,1)S(1)} %copy.17), channel_id=1, replica_groups=mesh['branch'=2,'hidden_x'=4,'hidden_z'=12,'width_y'=4,'width_core'=2] {..., dimensions={0}, use_global_device_ids=true | all-gather | bytes 983040 | tf_op jit(solution)/shard_map/all_gather | solution.py:248
  46.7 0.6 first_products.1
  47.3 4.7 %all_to_all.21 = f32[2,2,3,64,384]{4,3,2,1,0:T(8,128)S(1)} all-to-all(f32[2,2,3,64,384]{4,3,2,1,0:T(8,128)S(1)} %first_products.1), channel_id=1, replica_groups=mesh['branch'=2,'hidden_x'=4,'hidden_z'=12,'width_y'=4,'width_core'=2] {..., dimensions={0} | all-to-all | bytes 2359296 | tf_op jit(solution)/shard_map/all_to_all | solution.py:253
  52.0 0.1 slice_add_fusion
  52.1 5.3 %collective-permute-start.2 = (bf16[3,64,384]{2,1,0:T(8,128)(2,1)S(1)}, bf16[3,64,384]{2,1,0:T(8,128)(2,1)S(1)}, u32[]{:S(2)}, u32[]{:S(2)}) collective-permute-start(bf16[3,64,384]{2,1,0:T(8,128)(2,1)S(1)} %get-tuple-element.22), channel_id=1, source_target_pairs={{0,6},{2,4},{4,2},{6,0},{1,7},{3,5},{5,3},{7,1},{8,14},{10,12},{12... | collective-permute-start | bytes 442376 | tf_op jit(solution)/shard_map/ppermute | solution.py:260
  57.3 4.0 %collective-permute-start = (bf16[3,64,384]{2,1,0:T(8,128)(2,1)S(1)}, bf16[3,64,384]{2,1,0:T(8,128)(2,1)S(1)}, u32[]{:S(2)}, u32[]{:S(2)}) collective-permute-start(bf16[3,64,384]{2,1,0:T(8,128)(2,1)S(1)} %get-tuple-element.23), channel_id=1, source_target_pairs={{0,2},{2,0},{4,6},{6,4},{1,3},{3,1},{5,7},{7,5},{8,10},{10,8},{12,... | collective-permute-start | bytes 442376 | tf_op jit(solution)/shard_map/ppermute | solution.py:260
  61.4 3.7 %collective-permute-done.2 = bf16[3,64,384]{2,1,0:T(8,128)(2,1)S(1)} collective-permute-done((bf16[3,64,384]{2,1,0:T(8,128)(2,1)S(1)}, bf16[3,64,384]{2,1,0:T(8,128)(2,1)S(1)}, u32[]{:S(2)}, u32[]{:S(2)}) %collective-permute-start.2) | collective-permute-done | bytes 147488 | tf_op jit(solution)/shard_map/ppermute | solution.py:260
  65.1 3.8 %collective-permute-done = bf16[3,64,384]{2,1,0:T(8,128)(2,1)S(1)} collective-permute-done((bf16[3,64,384]{2,1,0:T(8,128)(2,1)S(1)}, bf16[3,64,384]{2,1,0:T(8,128)(2,1)S(1)}, u32[]{:S(2)}, u32[]{:S(2)}) %collective-permute-start) | collective-permute-done | bytes 147488 | tf_op jit(solution)/shard_map/ppermute | solution.py:260
  68.9 0.1 fusion.4
  69.0 4.1 %collective-permute-start.3 = (bf16[3,64,384]{2,1,0:T(8,128)(2,1)S(1)}, bf16[3,64,384]{2,1,0:T(8,128)(2,1)S(1)}, u32[]{:S(2)}, u32[]{:S(2)}) collective-permute-start(bf16[3,64,384]{2,1,0:T(8,128)(2,1)S(1)} %get-tuple-element.20), channel_id=1, source_target_pairs={{0,2},{2,0},{4,6},{6,4},{1,3},{3,1},{5,7},{7,5},{8,10},{10,8},{12,... | collective-permute-start | bytes 442376 | tf_op jit(solution)/shard_map/ppermute | solution.py:260
  73.1 3.1 %collective-permute-start.1 = (bf16[3,64,384]{2,1,0:T(8,128)(2,1)S(1)}, bf16[3,64,384]{2,1,0:T(8,128)(2,1)S(1)}, u32[]{:S(2)}, u32[]{:S(2)}) collective-permute-start(bf16[3,64,384]{2,1,0:T(8,128)(2,1)S(1)} %get-tuple-element.21), channel_id=1, source_target_pairs={{0,6},{2,4},{4,2},{6,0},{1,7},{3,5},{5,3},{7,1},{8,14},{10,12},{12... | collective-permute-start | bytes 442376 | tf_op jit(solution)/shard_map/ppermute | solution.py:260
  76.2 0.9 collective-permute-done.3
  77.1 7.6 %collective-permute-done.1 = bf16[3,64,384]{2,1,0:T(8,128)(2,1)S(1)} collective-permute-done((bf16[3,64,384]{2,1,0:T(8,128)(2,1)S(1)}, bf16[3,64,384]{2,1,0:T(8,128)(2,1)S(1)}, u32[]{:S(2)}, u32[]{:S(2)}) %collective-permute-start.1) | collective-permute-done | bytes 147488 | tf_op jit(solution)/shard_map/ppermute | solution.py:260
  84.6 0.1 convert_add_fusion
  84.8 0.1 fusion.8
  85.0 2.2 %all_gather.7.acts_ref = bf16[2,2,3,64,384]{4,3,2,1,0:T(8,128)(2,1)S(1)} all-gather(bf16[1,2,3,64,384]{4,3,2,1,0:T(8,128)(2,1)S(1)} %bitcast.74), channel_id=1, replica_groups=mesh['branch'=2,'hidden_x'=4,'hidden_z'=12,'width_y'=4,'width_core'=2] {..., dimensions={0}, use_global_device_ids=true | all-gather | bytes 884736 | tf_op jit(solution)/shard_map/all_gather | solution.py:271
  87.3 1.4 %second_products.1 = (bf16[48,2,8,512]{3,2,1,0:T(8,128)(2,1)}, f32[12,2,8,512]{3,2,1,0:T(8,128)S(1)}) custom-call(s32[1]{0:T(128)} %bitcast.1.place_ref, bf16[2,2,3,64,384]{4,3,2,1,0:T(8,128)(2,1)S(1)} %all_gather.7.acts_ref, bf16[512,256]{1,0:T(8,128)(2,1)S(1)} %bitcast.58, bf16[512,256]{1,0:T(8,128)(2,1)S(1)} %bitcast.60, bf16[256,512]{1,0:T(8,128)(2,1)S(1)} %bitcast.62), custom_call_target="tpu_custom_call" | custom-call | tf_op jit(solution)/shard_map/second_products/pallas_call | solution.py:209
  88.7 3.5 %all-to-all-start.2 = ((bf16[4,24,8,512]{3,2,1,0:T(8,128)(2,1)}), bf16[4,24,8,512]{3,2,1,0:T(8,128)(2,1)S(1)}, u32[]{:S(2)}, u32[]{:S(2)}) async-start(bf16[4,24,8,512]{3,2,1,0:T(8,128)(2,1)} %bitcast.15), calls=%async_computation.2 | async-start | bytes 1572864 | tf_op jit(solution)/shard_map/all_to_all | solution.py:280
  92.3 12.8 %all-to-all-done.2 = bf16[4,24,8,512]{3,2,1,0:T(8,128)(2,1)S(1)} async-done(((bf16[4,24,8,512]{3,2,1,0:T(8,128)(2,1)}), bf16[4,24,8,512]{3,2,1,0:T(8,128)(2,1)S(1)}, u32[]{:S(2)}, u32[]{:S(2)}) %all-to-all-start.2) | async-done | bytes 786464 | tf_op jit(solution)/shard_map/all_to_all | solution.py:280
  105.1 0.2 select_reduce_fusion
  105.3 0.7 fusion
  106.0 5.3 %all-to-all-start.3 = ((bf16[24,8,512]{2,1,0:T(8,128)(2,1)}), bf16[24,8,512]{2,1,0:T(8,128)(2,1)S(1)}, u32[]{:S(2)}, u32[]{:S(2)}) async-start(bf16[24,8,512]{2,1,0:T(8,128)(2,1)} %fusion), calls=%async_computation.3 | async-start | bytes 393216 | tf_op jit(solution)/shard_map/all_to_all | solution.py:289
  111.4 0.1 fusion.14
  111.4 1.1 convolution_bitcast_fusion
  112.5 1.1 convolution_bitcast_fusion.2
  113.7 1.1 convolution_bitcast_fusion.1
  114.8 8.7 %all-to-all-done.3.recv_ref = bf16[24,8,512]{2,1,0:T(8,128)(2,1)S(1)} async-done(((bf16[24,8,512]{2,1,0:T(8,128)(2,1)}), bf16[24,8,512]{2,1,0:T(8,128)(2,1)S(1)}, u32[]{:S(2)}, u32[]{:S(2)}) %all-to-all-start.3) | async-done | bytes 196640 | tf_op jit(solution)/shard_map/all_to_all | solution.py:289
  123.5 1.2 finish.1
  (19 shorter events, 0.4 us)
Async XLA Ops:
  32.1 14.6 %copy-start = (bf16[1,512,256]{2,1,0:T(8,128)(2,1)S(1)}, bf16[1,512,256]{2,1,0:T(8,128)(2,1)}, u32[]{:S(2)}) copy-start(bf16[1,512,256]{2,1,0:T(8,128)(2,1)} %param.11) | copy-start | bytes 786436
  32.1 14.6 %copy-start.1 = (bf16[1,512,256]{2,1,0:T(8,128)(2,1)S(1)}, bf16[1,512,256]{2,1,0:T(8,128)(2,1)}, u32[]{:S(2)}) copy-start(bf16[1,512,256]{2,1,0:T(8,128)(2,1)} %param.12) | copy-start | bytes 786436
  32.1 14.6 %copy-start.2 = (bf16[1,256,512]{2,1,0:T(8,128)(2,1)S(1)}, bf16[1,256,512]{2,1,0:T(8,128)(2,1)}, u32[]{:S(2)}) copy-start(bf16[1,256,512]{2,1,0:T(8,128)(2,1)} %param.13) | copy-start | bytes 786436
  52.1 13.1 %collective-permute-start.2 = (bf16[3,64,384]{2,1,0:T(8,128)(2,1)S(1)}, bf16[3,64,384]{2,1,0:T(8,128)(2,1)S(1)}, u32[]{:S(2)}, u32[]{:S(2)}) collective-permute-start(bf16[3,64,384]{2,1,0:T(8,128)(2,1)S(1)} %get-tuple-element.22), channel_id=1, source_target_pairs={{0,6},{2,4},{4,2},{6,0},{1,7},{3,5},{5,3},{7,1},{8,14},{10,12},{12... | collective-permute-start | bytes 442376 | tf_op jit(solution)/shard_map/ppermute | solution.py:260
  57.3 11.6 %collective-permute-start = (bf16[3,64,384]{2,1,0:T(8,128)(2,1)S(1)}, bf16[3,64,384]{2,1,0:T(8,128)(2,1)S(1)}, u32[]{:S(2)}, u32[]{:S(2)}) collective-permute-start(bf16[3,64,384]{2,1,0:T(8,128)(2,1)S(1)} %get-tuple-element.23), channel_id=1, source_target_pairs={{0,2},{2,0},{4,6},{6,4},{1,3},{3,1},{5,7},{7,5},{8,10},{10,8},{12,... | collective-permute-start | bytes 442376 | tf_op jit(solution)/shard_map/ppermute | solution.py:260
  69.0 8.1 %collective-permute-start.3 = (bf16[3,64,384]{2,1,0:T(8,128)(2,1)S(1)}, bf16[3,64,384]{2,1,0:T(8,128)(2,1)S(1)}, u32[]{:S(2)}, u32[]{:S(2)}) collective-permute-start(bf16[3,64,384]{2,1,0:T(8,128)(2,1)S(1)} %get-tuple-element.20), channel_id=1, source_target_pairs={{0,2},{2,0},{4,6},{6,4},{1,3},{3,1},{5,7},{7,5},{8,10},{10,8},{12,... | collective-permute-start | bytes 442376 | tf_op jit(solution)/shard_map/ppermute | solution.py:260
  73.1 11.6 %collective-permute-start.1 = (bf16[3,64,384]{2,1,0:T(8,128)(2,1)S(1)}, bf16[3,64,384]{2,1,0:T(8,128)(2,1)S(1)}, u32[]{:S(2)}, u32[]{:S(2)}) collective-permute-start(bf16[3,64,384]{2,1,0:T(8,128)(2,1)S(1)} %get-tuple-element.21), channel_id=1, source_target_pairs={{0,6},{2,4},{4,2},{6,0},{1,7},{3,5},{5,3},{7,1},{8,14},{10,12},{12... | collective-permute-start | bytes 442376 | tf_op jit(solution)/shard_map/ppermute | solution.py:260
  88.7 16.3 %all-to-all-start.2 = ((bf16[4,24,8,512]{3,2,1,0:T(8,128)(2,1)}), bf16[4,24,8,512]{3,2,1,0:T(8,128)(2,1)S(1)}, u32[]{:S(2)}, u32[]{:S(2)}) async-start(bf16[4,24,8,512]{3,2,1,0:T(8,128)(2,1)} %bitcast.15), calls=%async_computation.2 | async-start | bytes 1572864 | tf_op jit(solution)/shard_map/all_to_all | solution.py:280
  106.0 17.5 %all-to-all-start.3 = ((bf16[24,8,512]{2,1,0:T(8,128)(2,1)}), bf16[24,8,512]{2,1,0:T(8,128)(2,1)S(1)}, u32[]{:S(2)}, u32[]{:S(2)}) async-start(bf16[24,8,512]{2,1,0:T(8,128)(2,1)} %fusion), calls=%async_computation.3 | async-start | bytes 393216 | tf_op jit(solution)/shard_map/all_to_all | solution.py:289
  112.5 11.0 %copy-start.3 = (s32[2,3]{1,0:T(2,128)S(1)}, s32[2,3]{1,0:T(2,128)}, u32[]{:S(2)}) copy-start(s32[2,3]{1,0:T(2,128)} %labels_ref.1) | copy-start | bytes 76
  112.5 11.0 %copy-start.4 = (s32[2,1]{0,1:T(1,128)S(1)}, s32[2,1]{0,1:T(1,128)}, u32[]{:S(2)}) copy-start(s32[2,1]{0,1:T(1,128)} %param.10) | copy-start | bytes 28

commit v8 on v6

--- a/solution.py
+++ b/solution.py
@@ -95,9 +95,9 @@
             ref[p] = value.astype(BF16)
 
 
-def first_kernel(every_ref, gate_ref, up_ref, down_ref, parts_ref):
+def first_kernel(core_ref, every_ref, gate_ref, up_ref, down_ref, mine_ref, theirs_ref):
     size_x, _, block, width = every_ref.shape
-    size_c, size_y, _, share_units, slots = parts_ref.shape
+    size_y, _, share_units, slots = mine_ref.shape
     rows = every_ref[:, 0].reshape(slots, width)
     cot = every_ref[:, 1].reshape(slots, width)
     sums = (
@@ -105,11 +105,15 @@
         contract(up_ref[...], rows, 0, 1),
         contract(down_ref[...], cot, 1, 1),
     )
-    for kind, total in enumerate(sums):
-        for y in range(size_y):
-            for c in range(size_c):
-                start = (y * size_c + c) * share_units
-                parts_ref[c, y, kind] = total[start : start + share_units]
+    for core in range(2):
+
+        @pl.when(core_ref[0] == core)
+        def _():
+            for kind, total in enumerate(sums):
+                for y in range(size_y):
+                    for ref, c in ((mine_ref, core), (theirs_ref, 1 - core)):
+                        start = (y * 2 + c) * share_units
+                        ref[y, kind] = total[start : start + share_units]
 
 
 def contract(left, right, left_dim, right_dim):
@@ -118,10 +122,12 @@
     )
 
 
-def own_kept(own, received, axis):
-    place = lax.broadcasted_iota(jnp.int32, own.shape, 0)
-    mine = place == lax.axis_index(axis)
-    return jnp.sum(jnp.where(mine, own, received.astype(F32)), axis=0)
+def own_kept(own, received, other):
+    terms = jnp.where(other, received.astype(F32), own)
+    total = terms[0]
+    for i in range(1, terms.shape[0]):
+        total = total + terms[i]
+    return total
 
 
 def full(shape):
@@ -188,23 +194,24 @@
     )(labels, counts, recv)
 
 
-def first_products(every, gate_weight, up_weight, down_weight, size_c, size_y):
+def first_products(core, every, gate_weight, up_weight, down_weight, size_y):
     units = gate_weight.shape[1]
     slots = every.shape[0] * every.shape[2]
-    shape = (size_c, size_y, 3, units // (size_c * size_y), slots)
+    shape = (size_y, 3, units // (2 * size_y), slots)
     return pl.pallas_call(
         first_kernel,
-        out_shape=jax.ShapeDtypeStruct(shape, F32),
+        out_shape=(jax.ShapeDtypeStruct(shape, F32),) * 2,
         in_specs=[
+            SCALARS,
             full(every.shape),
             full(gate_weight.shape),
             full(up_weight.shape),
             full(down_weight.shape),
         ],
-        out_specs=full(shape),
+        out_specs=(full(shape),) * 2,
         compiler_params=GRANT,
         name="first_products",
-    )(every, gate_weight, up_weight, down_weight)
+    )(core, every, gate_weight, up_weight, down_weight)
 
 
 def second_products(place, acts, gate_weight, up_weight, down_weight, size_x):
@@ -255,11 +262,21 @@
     flat_rows = every[:, 0].reshape(slots, width)
     flat_cot = every[:, 1].reshape(slots, width)
 
-    parts = first_products(every, gate_weight, up_weight, down_weight, size_c, size_y)
-    pair = lax.all_to_all(parts, "width_core", 0, 0, tiled=True)
-    pair = pair[0] + pair[1]
+    place_x = lax.axis_index("hidden_x")
+    other_x = lax.broadcasted_iota(jnp.int32, (size_x, 1, 1), 0) != place_x
+    other_y = lax.broadcasted_iota(jnp.int32, (size_y, 1, 1, 1), 0) != lax.axis_index(
+        "width_y"
+    )
+    mine, theirs = first_products(
+        lax.axis_index("width_core").reshape(1),
+        every, gate_weight, up_weight, down_weight, size_y,
+    )
+    mine, theirs, other_x, other_y, place_x = lax.optimization_barrier(
+        (mine, theirs, other_x, other_y, place_x)
+    )
+    pair = mine + lax.ppermute(theirs, "width_core", [(0, 1), (1, 0)])
     sent = lax.all_to_all(pair.astype(BF16), "width_y", 0, 0, tiled=True)
-    gate, up_value, dhid = own_kept(pair, sent, "width_y")
+    gate, up_value, dhid = own_kept(pair, sent, other_y)
     sigma = jax.nn.sigmoid(gate)
     silu = gate * sigma
     share = jnp.stack(
@@ -274,7 +291,6 @@
     dgate = acts[:, 1].reshape(units, slots)
     dup = acts[:, 2].reshape(units, slots)
 
-    place_x = lax.axis_index("hidden_x")
     sent, own = second_products(
         place_x.reshape(1), acts, gate_weight, up_weight, down_weight, size_x
     )
@@ -284,9 +300,10 @@
     grad_gate = contract(flat_rows, dgate, 0, 1)
     grad_up = contract(flat_rows, dup, 0, 1)
     grad_down = contract(hidden, flat_cot, 1, 0)
-    other = lax.broadcasted_iota(jnp.int32, (size_x, 1, 1, 1), 0) != place_x
-    result = jnp.sum(jnp.where(other, sent.astype(F32), 0.0), axis=0)
-    result = (own.reshape(near, 8, width) + result).astype(BF16)
+    result = own.reshape(near, 8, width)
+    for i in range(size_x):
+        result = result + jnp.where(other_x[i], sent[i].astype(F32), 0.0)
+    result = result.astype(BF16)
     result = lax.all_to_all(result, NEAR, 0, 0, tiled=True)
     output, grad_rows = finish(labels, counts, result, mb)
     return (

time: 126 us -> 127 us (level)
  the two profiles are of different devices: /device:TPU:8 before, /device:TPU:2 now
where the time goes in v8:
time: 127 us; the launch traced here: 126 us
  blocking collectives  48.2 us (38%)
  waiting for transfers between devices  37.3 us (29%)
  starting transfers between devices  27.2 us (21%)
  Pallas kernels  4.78 us (4%)
  other arithmetic  3.73 us (3%)
  matrix products  3.37 us (3%)
    all_to_all x1, blocking collectives, shards(): sent = lax.all_to_all(pair.astype(BF16), 'width_y', 0, 0, tiled=True)  18.1 us
    all_gather x1, blocking collectives, shards(): acts = lax.all_gather(share, WIDTH, axis=0, tiled=False)  16.6 us
    all_to_all x1, starting transfers between devices, shards(): lax.all_to_all(send.reshape(near, 2 * per_owner, width), NEAR, 0, 0, tile...  16.4 us
    all_to_all x1, waiting for transfers between devices, shards(): lax.all_to_all(send.reshape(near, 2 * per_owner, width), NEAR, 0, 0, tile...  14.4 us
    all_gather x1, blocking collectives, shards(): lax.all_gather(recv.reshape(2, block, width), 'hidden_x', axis=0, tiled=F...  13.5 us
    all_to_all x1, waiting for transfers between devices, shards(): lax.all_to_all(sent.reshape(size_x, near, 8, width), 'hidden_x', 0, 0, ti...  10.8 us
    all_to_all x1, waiting for transfers between devices, shards(): result = lax.all_to_all(result, NEAR, 0, 0, tiled=True)  10.3 us
    all_to_all x1, starting transfers between devices, shards(): lax.all_to_all(sent.reshape(size_x, near, 8, width), 'hidden_x', 0, 0, ti...  4.51 us
  transfers between devices with their start and end apart: 4, of which 4 were waited for; matrix products, arithmetic and copies ran while one was open for 3% of the time, Pallas kernels for 0%

profile of v8, /device:TPU:2, one launch (start us, length us, event | category | flops | bytes accessed | tf_op | source)
XLA Modules:
  0.0 126.4 jit_solution(13220045388425141843)
XLA Ops:
  0.6 1.5 %pack.1 = bf16[2,12,8,512]{3,2,1,0:T(8,128)(2,1)} custom-call(s32[2,3]{1,0:T(2,128)} %labels_ref.1, s32[1,2]{1,0:T(1,128)} %bitcast.87, bf16[3,2,512]{2,1,0:T(2,128)(2,1)} %bitcast.98, bf16[3,2,512]{2,1,0:T(2,128)(2,1)} %bitcast.99), custom_call_target="tpu_custom_call" | custom-call | tf_op jit(solution)/shard_map/pack/pallas_call | solution.py:167
  2.1 16.4 %all-to-all-start = ((bf16[24,8,512]{2,1,0:T(8,128)(2,1)}), bf16[24,8,512]{2,1,0:T(8,128)(2,1)S(1)}, u32[]{:S(2)}, u32[]{:S(2)}) async-start(bf16[24,8,512]{2,1,0:T(8,128)(2,1)} %bitcast.92), calls=%async_computation | async-start | bytes 393216 | tf_op jit(solution)/shard_map/all_to_all | solution.py:257
  18.5 14.4 %all-to-all-done = bf16[24,8,512]{2,1,0:T(8,128)(2,1)S(1)} async-done(((bf16[24,8,512]{2,1,0:T(8,128)(2,1)}), bf16[24,8,512]{2,1,0:T(8,128)(2,1)S(1)}, u32[]{:S(2)}, u32[]{:S(2)}) %all-to-all-start) | async-done | bytes 196640 | tf_op jit(solution)/shard_map/all_to_all | solution.py:257
  32.9 0.1 copy.15
  33.0 0.2 copy.16
  33.2 0.0 copy-start
  33.2 0.0 copy-start.1
  33.2 0.0 copy-start.2
  33.2 13.5 %all_gather.9.every_ref = bf16[4,2,96,512]{3,2,1,0:T(8,128)(2,1)S(1)} all-gather(bf16[1,2,96,512]{3,2,1,0:T(8,128)(2,1)S(1)} %copy.17), channel_id=1, replica_groups=mesh['branch'=2,'hidden_x'=4,'hidden_z'=12,'width_y'=4,'width_core'=2] {..., dimensions={0}, use_global_device_ids=true | all-gather | bytes 983040 | tf_op jit(solution)/shard_map/all_gather | solution.py:261
  46.7 0.0 copy-done
  46.8 0.0 copy-done.1
  46.8 0.7 first_products.1
  47.4 1.9 %collective-permute-start = (f32[4,3,32,384]{3,2,1,0:T(8,128)S(1)}, f32[4,3,32,384]{3,2,1,0:T(8,128)S(1)}, u32[]{:S(2)}, u32[]{:S(2)}) collective-permute-start(f32[4,3,32,384]{3,2,1,0:T(8,128)S(1)} %get-tuple-element.21), channel_id=1, source_target_pairs={{0,1},{1,0},{2,3},{3,2},{4,5},{5,4},{6,7},{7,6},{8,9},{9,8},{10,11... | collective-permute-start | bytes 1769480 | tf_op jit(solution)/shard_map/ppermute | solution.py:277
  49.4 2.0 %collective-permute-done = f32[4,3,32,384]{3,2,1,0:T(8,128)S(1)} collective-permute-done((f32[4,3,32,384]{3,2,1,0:T(8,128)S(1)}, f32[4,3,32,384]{3,2,1,0:T(8,128)S(1)}, u32[]{:S(2)}, u32[]{:S(2)}) %collective-permute-start) | collective-permute-done | bytes 589856 | tf_op jit(solution)/shard_map/ppermute | solution.py:277
  51.3 0.1 fusion.2
  51.4 18.1 %all_to_all.20 = bf16[4,3,32,384]{3,2,1,0:T(8,128)(2,1)S(1)} all-to-all(bf16[4,3,32,384]{3,2,1,0:T(8,128)(2,1)S(1)} %get-tuple-element.27), channel_id=1, replica_groups=mesh['branch'=2,'hidden_x'=4,'hidden_z'=12,'width_y'=4,'width_core'=2] {..., dimensions={0} | all-to-all | bytes 589824 | tf_op jit(solution)/shard_map/all_to_all | solution.py:278
  69.6 0.1 convert_select_fusion
  69.8 16.6 %all-gather = bf16[24,32,384]{2,1,0:T(8,128)(2,1)S(1)} all-gather(bf16[3,32,384]{2,1,0:T(8,128)(2,1)S(1)} %pad_maximum_fusion), channel_id=2, replica_groups=mesh['branch'=2,'hidden_x'=4,'hidden_z'=12,'width_y'=4,'width_core'=2] {..., dimensions={0}, use_global_device_ids=true | all-gather | bytes 663552 | tf_op jit(solution)/shard_map/all_gather | solution.py:289
  86.4 1.4 %second_products.1 = (bf16[48,2,8,512]{3,2,1,0:T(8,128)(2,1)}, f32[12,2,8,512]{3,2,1,0:T(8,128)S(1)}) custom-call(s32[1]{0:T(128)} %bitcast.11.place_ref, bf16[8,3,32,384]{3,2,1,0:T(8,128)(2,1)S(1)} %bitcast.79, bf16[512,256]{1,0:T(8,128)(2,1)S(1)} %bitcast.82, bf16[512,256]{1,0:T(8,128)(2,1)S(1)} %bitcast.84, bf16[256,512]{1,0:T(8,128)(2,1)S(1)} %bitcast.86), custom_call_target="tpu_custom_call" | custom-call | tf_op jit(solution)/shard_map/second_products/pallas_call | solution.py:222
  87.8 4.5 %all-to-all-start.2 = ((bf16[4,24,8,512]{3,2,1,0:T(8,128)(2,1)}), bf16[4,24,8,512]{3,2,1,0:T(8,128)(2,1)S(1)}, u32[]{:S(2)}, u32[]{:S(2)}) async-start(bf16[4,24,8,512]{3,2,1,0:T(8,128)(2,1)} %bitcast.19), calls=%async_computation.2 | async-start | bytes 1572864 | tf_op jit(solution)/shard_map/all_to_all | solution.py:297
  92.3 0.5 fusion.5
  92.8 0.1 fusion.3
  92.9 10.8 %all-to-all-done.2 = bf16[4,24,8,512]{3,2,1,0:T(8,128)(2,1)S(1)} async-done(((bf16[4,24,8,512]{3,2,1,0:T(8,128)(2,1)}), bf16[4,24,8,512]{3,2,1,0:T(8,128)(2,1)S(1)}, u32[]{:S(2)}, u32[]{:S(2)}) %all-to-all-start.2) | async-done | bytes 786464 | tf_op jit(solution)/shard_map/all_to_all | solution.py:297
  103.7 3.4 %fusion = bf16[24,8,512]{2,1,0:T(8,128)(2,1)} fusion(f32[12,2,8,512]{3,2,1,0:T(8,128)S(1)} %get-tuple-element.22, bf16[4,24,8,512]{3,2,1,0:T(8,128)(2,1)S(1)} %all-to-all-done.2, pred[]{:T(512)} %bitcast.25, pred[]{:T(512)} %bitcast.23, pred[]{:T(512)} %bitcast.21, pred[]{:T(512)} %bitcast.18), kind=kLoop, calls=%fused_computation.5 | loop fusion | flops 1277952 | bytes 1376260 | tf_op jit(solution)/shard_map/convert_element_type | solution.py:306
  107.1 4.4 %all-to-all-start.3 = ((bf16[24,8,512]{2,1,0:T(8,128)(2,1)}), bf16[24,8,512]{2,1,0:T(8,128)(2,1)S(1)}, u32[]{:S(2)}, u32[]{:S(2)}) async-start(bf16[24,8,512]{2,1,0:T(8,128)(2,1)} %fusion), calls=%async_computation.3 | async-start | bytes 393216 | tf_op jit(solution)/shard_map/all_to_all | solution.py:307
  111.5 0.1 fusion.4
  111.5 1.1 convolution_bitcast_fusion
  112.6 1.1 convolution_bitcast_fusion.2
  113.8 1.1 convolution_bitcast_fusion.1
  114.9 10.3 %all-to-all-done.3.recv_ref = bf16[24,8,512]{2,1,0:T(8,128)(2,1)S(1)} async-done(((bf16[24,8,512]{2,1,0:T(8,128)(2,1)}), bf16[24,8,512]{2,1,0:T(8,128)(2,1)S(1)}, u32[]{:S(2)}, u32[]{:S(2)}) %all-to-all-start.3) | async-done | bytes 196640 | tf_op jit(solution)/shard_map/all_to_all | solution.py:307
  125.2 0.0 copy-done.3
  125.2 1.2 finish.1
  (10 shorter events, 0.1 us)
Async XLA Ops:
  2.1 30.8 %all-to-all-start = ((bf16[24,8,512]{2,1,0:T(8,128)(2,1)}), bf16[24,8,512]{2,1,0:T(8,128)(2,1)S(1)}, u32[]{:S(2)}, u32[]{:S(2)}) async-start(bf16[24,8,512]{2,1,0:T(8,128)(2,1)} %bitcast.92), calls=%async_computation | async-start | bytes 393216 | tf_op jit(solution)/shard_map/all_to_all | solution.py:257
  33.2 13.5 %copy-start = (bf16[1,512,256]{2,1,0:T(8,128)(2,1)S(1)}, bf16[1,512,256]{2,1,0:T(8,128)(2,1)}, u32[]{:S(2)}) copy-start(bf16[1,512,256]{2,1,0:T(8,128)(2,1)} %param.11) | copy-start | bytes 786436
  33.2 13.5 %copy-start.1 = (bf16[1,512,256]{2,1,0:T(8,128)(2,1)S(1)}, bf16[1,512,256]{2,1,0:T(8,128)(2,1)}, u32[]{:S(2)}) copy-start(bf16[1,512,256]{2,1,0:T(8,128)(2,1)} %param.12) | copy-start | bytes 786436
  33.2 13.5 %copy-start.2 = (bf16[1,256,512]{2,1,0:T(8,128)(2,1)S(1)}, bf16[1,256,512]{2,1,0:T(8,128)(2,1)}, u32[]{:S(2)}) copy-start(bf16[1,256,512]{2,1,0:T(8,128)(2,1)} %param.13) | copy-start | bytes 786436
  47.4 3.9 %collective-permute-start = (f32[4,3,32,384]{3,2,1,0:T(8,128)S(1)}, f32[4,3,32,384]{3,2,1,0:T(8,128)S(1)}, u32[]{:S(2)}, u32[]{:S(2)}) collective-permute-start(f32[4,3,32,384]{3,2,1,0:T(8,128)S(1)} %get-tuple-element.21), channel_id=1, source_target_pairs={{0,1},{1,0},{2,3},{3,2},{4,5},{5,4},{6,7},{7,6},{8,9},{9,8},{10,11... | collective-permute-start | bytes 1769480 | tf_op jit(solution)/shard_map/ppermute | solution.py:277
  87.8 15.8 %all-to-all-start.2 = ((bf16[4,24,8,512]{3,2,1,0:T(8,128)(2,1)}), bf16[4,24,8,512]{3,2,1,0:T(8,128)(2,1)S(1)}, u32[]{:S(2)}, u32[]{:S(2)}) async-start(bf16[4,24,8,512]{3,2,1,0:T(8,128)(2,1)} %bitcast.19), calls=%async_computation.2 | async-start | bytes 1572864 | tf_op jit(solution)/shard_map/all_to_all | solution.py:297
  107.1 18.1 %all-to-all-start.3 = ((bf16[24,8,512]{2,1,0:T(8,128)(2,1)}), bf16[24,8,512]{2,1,0:T(8,128)(2,1)S(1)}, u32[]{:S(2)}, u32[]{:S(2)}) async-start(bf16[24,8,512]{2,1,0:T(8,128)(2,1)} %fusion), calls=%async_computation.3 | async-start | bytes 393216 | tf_op jit(solution)/shard_map/all_to_all | solution.py:307
  113.8 11.4 %copy-start.3 = (s32[2,3]{1,0:T(2,128)S(1)}, s32[2,3]{1,0:T(2,128)}, u32[]{:S(2)}) copy-start(s32[2,3]{1,0:T(2,128)} %labels_ref.1) | copy-start | bytes 76
  113.8 11.4 %copy-start.4 = (s32[2,1]{0,1:T(1,128)S(1)}, s32[2,1]{0,1:T(1,128)}, u32[]{:S(2)}) copy-start(s32[2,1]{0,1:T(1,128)} %param.10) | copy-start | bytes 28

commit v9 on v8

--- a/solution.py
+++ b/solution.py
@@ -263,7 +263,6 @@
     flat_cot = every[:, 1].reshape(slots, width)
 
     place_x = lax.axis_index("hidden_x")
-    other_x = lax.broadcasted_iota(jnp.int32, (size_x, 1, 1), 0) != place_x
     other_y = lax.broadcasted_iota(jnp.int32, (size_y, 1, 1, 1), 0) != lax.axis_index(
         "width_y"
     )
@@ -271,8 +270,8 @@
         lax.axis_index("width_core").reshape(1),
         every, gate_weight, up_weight, down_weight, size_y,
     )
-    mine, theirs, other_x, other_y, place_x = lax.optimization_barrier(
-        (mine, theirs, other_x, other_y, place_x)
+    mine, theirs, other_y, place_x = lax.optimization_barrier(
+        (mine, theirs, other_y, place_x)
     )
     pair = mine + lax.ppermute(theirs, "width_core", [(0, 1), (1, 0)])
     sent = lax.all_to_all(pair.astype(BF16), "width_y", 0, 0, tiled=True)
@@ -300,10 +299,11 @@
     grad_gate = contract(flat_rows, dgate, 0, 1)
     grad_up = contract(flat_rows, dup, 0, 1)
     grad_down = contract(hidden, flat_cot, 1, 0)
-    result = own.reshape(near, 8, width)
-    for i in range(size_x):
-        result = result + jnp.where(other_x[i], sent[i].astype(F32), 0.0)
-    result = result.astype(BF16)
+    other = lax.broadcasted_iota(
+        jnp.int32, (size_x, 1, 1, 1), 0
+    ) != lax.axis_index("hidden_x")
+    result = jnp.sum(jnp.where(other, sent.astype(F32), 0.0), axis=0)
+    result = (own.reshape(near, 8, width) + result).astype(BF16)
     result = lax.all_to_all(result, NEAR, 0, 0, tiled=True)
     output, grad_rows = finish(labels, counts, result, mb)
     return (

time: 127 us -> 124 us (0.976)
  other arithmetic: 3.73 us -> 1.27 us
    convert_element_type x1, other arithmetic: 3.42 us -> 0.73 us  [shards(): result = (own.reshape(near, 8, width) + result).astype(BF16)]
where the time goes in v9:
time: 124 us
  blocking collectives  48.2 us (39%)
  waiting for transfers between devices  37.9 us (31%)
  starting transfers between devices  27.2 us (22%)
  Pallas kernels  4.79 us (4%)
  matrix products  3.37 us (3%)
  other arithmetic  1.27 us (1%)
    all_to_all x1, blocking collectives, shards(): sent = lax.all_to_all(pair.astype(BF16), 'width_y', 0, 0, tiled=True)  18.1 us
    all_gather x1, blocking collectives, shards(): acts = lax.all_gather(share, WIDTH, axis=0, tiled=False)  16.6 us
    all_to_all x1, starting transfers between devices, shards(): lax.all_to_all(send.reshape(near, 2 * per_owner, width), NEAR, 0, 0, tile...  16.4 us
    all_to_all x1, waiting for transfers between devices, shards(): lax.all_to_all(send.reshape(near, 2 * per_owner, width), NEAR, 0, 0, tile...  14.4 us
    all_gather x1, blocking collectives, shards(): lax.all_gather(recv.reshape(2, block, width), 'hidden_x', axis=0, tiled=F...  13.5 us
    all_to_all x1, waiting for transfers between devices, shards(): lax.all_to_all(sent.reshape(size_x, near, 8, width), 'hidden_x', 0, 0, ti...  11.3 us
    all_to_all x1, waiting for transfers between devices, shards(): result = lax.all_to_all(result, NEAR, 0, 0, tiled=True)  10.3 us
    all_to_all x1, starting transfers between devices, shards(): lax.all_to_all(sent.reshape(size_x, near, 8, width), 'hidden_x', 0, 0, ti...  4.51 us
  transfers between devices with their start and end apart: 4, of which 4 were waited for; matrix products, arithmetic and copies ran while one was open for 3% of the time, Pallas kernels for 0%

profile of v9, /device:TPU:2, one launch (start us, length us, event | category | flops | bytes accessed | tf_op | source)
XLA Modules:
  0.0 123.9 jit_solution(3904525596881475857)
XLA Ops:
  0.6 1.5 %pack.1 = bf16[2,12,8,512]{3,2,1,0:T(8,128)(2,1)} custom-call(s32[2,3]{1,0:T(2,128)} %labels_ref.1, s32[1,2]{1,0:T(1,128)} %bitcast.69, bf16[3,2,512]{2,1,0:T(2,128)(2,1)} %bitcast.80, bf16[3,2,512]{2,1,0:T(2,128)(2,1)} %bitcast.81), custom_call_target="tpu_custom_call" | custom-call | tf_op jit(solution)/shard_map/pack/pallas_call | solution.py:167
  2.1 16.4 %all-to-all-start = ((bf16[24,8,512]{2,1,0:T(8,128)(2,1)}), bf16[24,8,512]{2,1,0:T(8,128)(2,1)S(1)}, u32[]{:S(2)}, u32[]{:S(2)}) async-start(bf16[24,8,512]{2,1,0:T(8,128)(2,1)} %bitcast.74), calls=%async_computation | async-start | bytes 393216 | tf_op jit(solution)/shard_map/all_to_all | solution.py:257
  18.5 14.4 %all-to-all-done = bf16[24,8,512]{2,1,0:T(8,128)(2,1)S(1)} async-done(((bf16[24,8,512]{2,1,0:T(8,128)(2,1)}), bf16[24,8,512]{2,1,0:T(8,128)(2,1)S(1)}, u32[]{:S(2)}, u32[]{:S(2)}) %all-to-all-start) | async-done | bytes 196640 | tf_op jit(solution)/shard_map/all_to_all | solution.py:257
  32.9 0.1 copy.15
  33.0 0.2 copy.16
  33.2 0.0 copy-start
  33.2 0.0 copy-start.1
  33.2 0.0 copy-start.2
  33.2 13.5 %all_gather.9.every_ref = bf16[4,2,96,512]{3,2,1,0:T(8,128)(2,1)S(1)} all-gather(bf16[1,2,96,512]{3,2,1,0:T(8,128)(2,1)S(1)} %copy.17), channel_id=1, replica_groups=mesh['branch'=2,'hidden_x'=4,'hidden_z'=12,'width_y'=4,'width_core'=2] {..., dimensions={0}, use_global_device_ids=true | all-gather | bytes 983040 | tf_op jit(solution)/shard_map/all_gather | solution.py:261
  46.7 0.0 copy-done
  46.8 0.0 copy-done.1
  46.8 0.7 first_products.1
  47.4 1.9 %collective-permute-start = (f32[4,3,32,384]{3,2,1,0:T(8,128)S(1)}, f32[4,3,32,384]{3,2,1,0:T(8,128)S(1)}, u32[]{:S(2)}, u32[]{:S(2)}) collective-permute-start(f32[4,3,32,384]{3,2,1,0:T(8,128)S(1)} %get-tuple-element.20), channel_id=1, source_target_pairs={{0,1},{1,0},{2,3},{3,2},{4,5},{5,4},{6,7},{7,6},{8,9},{9,8},{10,11... | collective-permute-start | bytes 1769480 | tf_op jit(solution)/shard_map/ppermute | solution.py:276
  49.4 2.0 %collective-permute-done = f32[4,3,32,384]{3,2,1,0:T(8,128)S(1)} collective-permute-done((f32[4,3,32,384]{3,2,1,0:T(8,128)S(1)}, f32[4,3,32,384]{3,2,1,0:T(8,128)S(1)}, u32[]{:S(2)}, u32[]{:S(2)}) %collective-permute-start) | collective-permute-done | bytes 589856 | tf_op jit(solution)/shard_map/ppermute | solution.py:276
  51.3 0.1 fusion.2
  51.4 18.1 %all_to_all.20 = bf16[4,3,32,384]{3,2,1,0:T(8,128)(2,1)S(1)} all-to-all(bf16[4,3,32,384]{3,2,1,0:T(8,128)(2,1)S(1)} %get-tuple-element.25), channel_id=1, replica_groups=mesh['branch'=2,'hidden_x'=4,'hidden_z'=12,'width_y'=4,'width_core'=2] {..., dimensions={0} | all-to-all | bytes 589824 | tf_op jit(solution)/shard_map/all_to_all | solution.py:277
  69.6 0.1 convert_select_fusion
  69.8 16.6 %all-gather = bf16[24,32,384]{2,1,0:T(8,128)(2,1)S(1)} all-gather(bf16[3,32,384]{2,1,0:T(8,128)(2,1)S(1)} %pad_maximum_fusion), channel_id=2, replica_groups=mesh['branch'=2,'hidden_x'=4,'hidden_z'=12,'width_y'=4,'width_core'=2] {..., dimensions={0}, use_global_device_ids=true | all-gather | bytes 663552 | tf_op jit(solution)/shard_map/all_gather | solution.py:288
  86.4 1.4 %second_products.1 = (bf16[48,2,8,512]{3,2,1,0:T(8,128)(2,1)}, f32[12,2,8,512]{3,2,1,0:T(8,128)S(1)}) custom-call(s32[1]{0:T(128)} %bitcast.11.place_ref, bf16[8,3,32,384]{3,2,1,0:T(8,128)(2,1)S(1)} %bitcast.61, bf16[512,256]{1,0:T(8,128)(2,1)S(1)} %bitcast.64, bf16[512,256]{1,0:T(8,128)(2,1)S(1)} %bitcast.66, bf16[256,512]{1,0:T(8,128)(2,1)S(1)} %bitcast.68), custom_call_target="tpu_custom_call" | custom-call | tf_op jit(solution)/shard_map/second_products/pallas_call | solution.py:222
  87.8 4.5 %all-to-all-start.2 = ((bf16[4,24,8,512]{3,2,1,0:T(8,128)(2,1)}), bf16[4,24,8,512]{3,2,1,0:T(8,128)(2,1)S(1)}, u32[]{:S(2)}, u32[]{:S(2)}) async-start(bf16[4,24,8,512]{3,2,1,0:T(8,128)(2,1)} %bitcast.18), calls=%async_computation.2 | async-start | bytes 1572864 | tf_op jit(solution)/shard_map/all_to_all | solution.py:296
  92.3 0.1 fusion.3
  92.4 11.3 %all-to-all-done.2 = bf16[4,24,8,512]{3,2,1,0:T(8,128)(2,1)S(1)} async-done(((bf16[4,24,8,512]{3,2,1,0:T(8,128)(2,1)}), bf16[4,24,8,512]{3,2,1,0:T(8,128)(2,1)S(1)}, u32[]{:S(2)}, u32[]{:S(2)}) %all-to-all-start.2) | async-done | bytes 786464 | tf_op jit(solution)/shard_map/all_to_all | solution.py:296
  103.7 0.2 select_reduce_fusion
  103.9 0.7 fusion
  104.6 4.4 %all-to-all-start.3 = ((bf16[24,8,512]{2,1,0:T(8,128)(2,1)}), bf16[24,8,512]{2,1,0:T(8,128)(2,1)S(1)}, u32[]{:S(2)}, u32[]{:S(2)}) async-start(bf16[24,8,512]{2,1,0:T(8,128)(2,1)} %fusion), calls=%async_computation.3 | async-start | bytes 393216 | tf_op jit(solution)/shard_map/all_to_all | solution.py:307
  109.0 0.1 fusion.4
  109.1 1.1 convolution_bitcast_fusion
  110.2 1.1 convolution_bitcast_fusion.2
  111.3 1.1 convolution_bitcast_fusion.1
  112.5 10.3 %all-to-all-done.3.recv_ref = bf16[24,8,512]{2,1,0:T(8,128)(2,1)S(1)} async-done(((bf16[24,8,512]{2,1,0:T(8,128)(2,1)}), bf16[24,8,512]{2,1,0:T(8,128)(2,1)S(1)}, u32[]{:S(2)}, u32[]{:S(2)}) %all-to-all-start.3) | async-done | bytes 196640 | tf_op jit(solution)/shard_map/all_to_all | solution.py:307
  122.7 0.0 copy-done.3
  122.7 1.2 finish.1
  (10 shorter events, 0.1 us)
Async XLA Ops:
  2.1 30.8 %all-to-all-start = ((bf16[24,8,512]{2,1,0:T(8,128)(2,1)}), bf16[24,8,512]{2,1,0:T(8,128)(2,1)S(1)}, u32[]{:S(2)}, u32[]{:S(2)}) async-start(bf16[24,8,512]{2,1,0:T(8,128)(2,1)} %bitcast.74), calls=%async_computation | async-start | bytes 393216 | tf_op jit(solution)/shard_map/all_to_all | solution.py:257
  33.2 13.6 %copy-start = (bf16[1,512,256]{2,1,0:T(8,128)(2,1)S(1)}, bf16[1,512,256]{2,1,0:T(8,128)(2,1)}, u32[]{:S(2)}) copy-start(bf16[1,512,256]{2,1,0:T(8,128)(2,1)} %param.11) | copy-start | bytes 786436
  33.2 13.6 %copy-start.1 = (bf16[1,512,256]{2,1,0:T(8,128)(2,1)S(1)}, bf16[1,512,256]{2,1,0:T(8,128)(2,1)}, u32[]{:S(2)}) copy-start(bf16[1,512,256]{2,1,0:T(8,128)(2,1)} %param.12) | copy-start | bytes 786436
  33.2 13.6 %copy-start.2 = (bf16[1,256,512]{2,1,0:T(8,128)(2,1)S(1)}, bf16[1,256,512]{2,1,0:T(8,128)(2,1)}, u32[]{:S(2)}) copy-start(bf16[1,256,512]{2,1,0:T(8,128)(2,1)} %param.13) | copy-start | bytes 786436
  47.4 3.9 %collective-permute-start = (f32[4,3,32,384]{3,2,1,0:T(8,128)S(1)}, f32[4,3,32,384]{3,2,1,0:T(8,128)S(1)}, u32[]{:S(2)}, u32[]{:S(2)}) collective-permute-start(f32[4,3,32,384]{3,2,1,0:T(8,128)S(1)} %get-tuple-element.20), channel_id=1, source_target_pairs={{0,1},{1,0},{2,3},{3,2},{4,5},{5,4},{6,7},{7,6},{8,9},{9,8},{10,11... | collective-permute-start | bytes 1769480 | tf_op jit(solution)/shard_map/ppermute | solution.py:276
  87.8 15.8 %all-to-all-start.2 = ((bf16[4,24,8,512]{3,2,1,0:T(8,128)(2,1)}), bf16[4,24,8,512]{3,2,1,0:T(8,128)(2,1)S(1)}, u32[]{:S(2)}, u32[]{:S(2)}) async-start(bf16[4,24,8,512]{3,2,1,0:T(8,128)(2,1)} %bitcast.18), calls=%async_computation.2 | async-start | bytes 1572864 | tf_op jit(solution)/shard_map/all_to_all | solution.py:296
  104.6 18.1 %all-to-all-start.3 = ((bf16[24,8,512]{2,1,0:T(8,128)(2,1)}), bf16[24,8,512]{2,1,0:T(8,128)(2,1)S(1)}, u32[]{:S(2)}, u32[]{:S(2)}) async-start(bf16[24,8,512]{2,1,0:T(8,128)(2,1)} %fusion), calls=%async_computation.3 | async-start | bytes 393216 | tf_op jit(solution)/shard_map/all_to_all | solution.py:307
  111.3 11.4 %copy-start.3 = (s32[2,3]{1,0:T(2,128)S(1)}, s32[2,3]{1,0:T(2,128)}, u32[]{:S(2)}) copy-start(s32[2,3]{1,0:T(2,128)} %labels_ref.1) | copy-start | bytes 76
  111.3 11.4 %copy-start.4 = (s32[2,1]{0,1:T(1,128)S(1)}, s32[2,1]{0,1:T(1,128)}, u32[]{:S(2)}) copy-start(s32[2,1]{0,1:T(1,128)} %param.10) | copy-start | bytes 28

commit v10 on v7

--- a/solution.py
+++ b/solution.py
@@ -95,9 +95,9 @@
             ref[p] = value.astype(BF16)
 
 
-def first_kernel(every_ref, gate_ref, up_ref, down_ref, parts_ref):
+def first_kernel(core_ref, every_ref, gate_ref, up_ref, down_ref, mine_ref, theirs_ref):
     size_x, _, block, width = every_ref.shape
-    size_c, pieces, _, piece_units, slots = parts_ref.shape
+    pieces, _, piece_units, slots = mine_ref.shape
     rows = every_ref[:, 0].reshape(slots, width)
     cot = every_ref[:, 1].reshape(slots, width)
     sums = (
@@ -105,11 +105,15 @@
         contract(up_ref[...], rows, 0, 1),
         contract(down_ref[...], cot, 1, 1),
     )
-    for kind, total in enumerate(sums):
-        for c in range(size_c):
-            for piece in range(pieces):
-                start = (c * pieces + piece) * piece_units
-                parts_ref[c, piece, kind] = total[start : start + piece_units]
+    for core in range(2):
+
+        @pl.when(core_ref[0] == core)
+        def _():
+            for kind, total in enumerate(sums):
+                for piece in range(pieces):
+                    for ref, c in ((mine_ref, core), (theirs_ref, 1 - core)):
+                        start = (c * pieces + piece) * piece_units
+                        ref[piece, kind] = total[start : start + piece_units]
 
 
 def contract(left, right, left_dim, right_dim):
@@ -182,23 +186,24 @@
     )(labels, counts, recv)
 
 
-def first_products(every, gate_weight, up_weight, down_weight, size_c):
+def first_products(core, every, gate_weight, up_weight, down_weight):
     units = gate_weight.shape[1]
     slots = every.shape[0] * every.shape[2]
-    shape = (size_c, 2, 3, units // (2 * size_c), slots)
+    shape = (2, 3, units // 4, slots)
     return pl.pallas_call(
         first_kernel,
-        out_shape=jax.ShapeDtypeStruct(shape, F32),
+        out_shape=(jax.ShapeDtypeStruct(shape, F32),) * 2,
         in_specs=[
+            SCALARS,
             full(every.shape),
             full(gate_weight.shape),
             full(up_weight.shape),
             full(down_weight.shape),
         ],
-        out_specs=full(shape),
+        out_specs=(full(shape),) * 2,
         compiler_params=GRANT,
         name="first_products",
-    )(every, gate_weight, up_weight, down_weight)
+    )(core, every, gate_weight, up_weight, down_weight)
 
 
 def second_products(place, acts, gate_weight, up_weight, down_weight, size_x):
@@ -249,9 +254,11 @@
     flat_rows = every[:, 0].reshape(slots, width)
     flat_cot = every[:, 1].reshape(slots, width)
 
-    parts = first_products(every, gate_weight, up_weight, down_weight, size_c)
-    pair = lax.all_to_all(parts, "width_core", 0, 0, tiled=True)
-    pair = pair[0] + pair[1]
+    mine, theirs = first_products(
+        lax.axis_index("width_core").reshape(1),
+        every, gate_weight, up_weight, down_weight,
+    )
+    pair = mine + lax.ppermute(theirs, "width_core", [(0, 1), (1, 0)])
     low = [(i, i ^ 1) for i in range(size_y)]
     high = [(i, (i + 1 if i % 2 else i - 1) % size_y) for i in range(size_y)]
     sums = [pair[0], pair[1]]

time: 125 us -> 125 us (level)
  blocking collectives: 51.1 us -> 16.6 us
  starting transfers between devices: 25.3 us -> 43.9 us
  waiting for transfers between devices: 37.5 us -> 52.7 us
    all_to_all x2 -> x0, blocking collectives: 34.6 us -> none  [the longest x1 30 us: shards(): lax.all_to_all(send.reshape(near, 2 * per_owner, width), NEAR, 0, 0, tile...]
    all_to_all x0 -> x1, starting transfers between devices: none -> 16.7 us  [shards(): lax.all_to_all(send.reshape(near, 2 * per_owner, width), NEAR, 0, 0, tile...]
    all_to_all x0 -> x1, waiting for transfers between devices: none -> 13.3 us  [shards(): lax.all_to_all(send.reshape(near, 2 * per_owner, width), NEAR, 0, 0, tile...]
    ppermute x0 -> x1, waiting for transfers between devices: none -> 1.97 us  [shards(): pair = mine + lax.ppermute(theirs, 'width_core', [(0, 1), (1, 0)])]
    ppermute x0 -> x1, starting transfers between devices: none -> 1.92 us  [shards(): pair = mine + lax.ppermute(theirs, 'width_core', [(0, 1), (1, 0)])]
  transfers between devices with their start and end apart: 6 -> 8, of which waited for: 6 -> 8; matrix products, arithmetic and copies ran while one was open for 3% -> 3% of each run, Pallas kernels for 0% -> 0%
where the time goes in v10:
time: 125 us; the launch traced here: 124 us
  waiting for transfers between devices  52.7 us (42%)
  starting transfers between devices  43.9 us (35%)
  blocking collectives  16.6 us (13%)
  Pallas kernels  4.76 us (4%)
  matrix products  3.37 us (3%)
  other arithmetic  1.46 us (1%)
    all_to_all x1, starting transfers between devices, shards(): lax.all_to_all(send.reshape(near, 2 * per_owner, width), NEAR, 0, 0, tile...  16.7 us
    ppermute x4, starting transfers between devices, shards(): lax.ppermute(own.astype(BF16), 'width_y', route).astype(F32)  16.5 us
    ppermute x4, waiting for transfers between devices, shards(): lax.ppermute(own.astype(BF16), 'width_y', route).astype(F32)  16 us
    all_gather x1, blocking collectives, shards(): lax.all_gather(recv.reshape(2, block, width), 'hidden_x', axis=0, tiled=F...  14.4 us
    all_to_all x1, waiting for transfers between devices, shards(): lax.all_to_all(send.reshape(near, 2 * per_owner, width), NEAR, 0, 0, tile...  13.3 us
    all_to_all x1, waiting for transfers between devices, shards(): lax.all_to_all(sent.reshape(size_x, near, 8, width), 'hidden_x', 0, 0, ti...  12.8 us
    all_to_all x1, waiting for transfers between devices, shards(): result = lax.all_to_all(result, NEAR, 0, 0, tiled=True)  8.75 us
    all_to_all x1, starting transfers between devices, shards(): result = lax.all_to_all(result, NEAR, 0, 0, tiled=True)  5.35 us
  transfers between devices with their start and end apart: 8, of which 8 were waited for; matrix products, arithmetic and copies ran while one was open for 3% of the time, Pallas kernels for 0%

profile of v10, /device:TPU:8, one launch (start us, length us, event | category | flops | bytes accessed | tf_op | source)
XLA Modules:
  0.0 124.2 jit_solution(2294391650198426442)
XLA Ops:
  0.6 1.5 %pack.1 = bf16[2,12,8,512]{3,2,1,0:T(8,128)(2,1)} custom-call(s32[2,3]{1,0:T(2,128)} %labels_ref.1, s32[1,2]{1,0:T(1,128)} %bitcast.64, bf16[3,2,512]{2,1,0:T(2,128)(2,1)} %bitcast.76, bf16[3,2,512]{2,1,0:T(2,128)(2,1)} %bitcast.77), custom_call_target="tpu_custom_call" | custom-call | tf_op jit(solution)/shard_map/pack/pallas_call | solution.py:159
  2.1 16.7 %all-to-all-start = ((bf16[24,8,512]{2,1,0:T(8,128)(2,1)}), bf16[24,8,512]{2,1,0:T(8,128)(2,1)S(1)}, u32[]{:S(2)}, u32[]{:S(2)}) async-start(bf16[24,8,512]{2,1,0:T(8,128)(2,1)} %bitcast.69), calls=%async_computation | async-start | bytes 393216 | tf_op jit(solution)/shard_map/all_to_all | solution.py:249
  18.8 13.3 %all-to-all-done = bf16[24,8,512]{2,1,0:T(8,128)(2,1)S(1)} async-done(((bf16[24,8,512]{2,1,0:T(8,128)(2,1)}), bf16[24,8,512]{2,1,0:T(8,128)(2,1)S(1)}, u32[]{:S(2)}, u32[]{:S(2)}) %all-to-all-start) | async-done | bytes 196640 | tf_op jit(solution)/shard_map/all_to_all | solution.py:249
  32.2 0.2 copy.16
  32.4 14.4 %all_gather.6.every_ref = bf16[4,2,96,512]{3,2,1,0:T(8,128)(2,1)S(1)} all-gather(bf16[1,2,96,512]{3,2,1,0:T(8,128)(2,1)S(1)} %copy.17), channel_id=1, replica_groups=mesh['branch'=2,'hidden_x'=4,'hidden_z'=12,'width_y'=4,'width_core'=2] {..., dimensions={0}, use_global_device_ids=true | all-gather | bytes 983040 | tf_op jit(solution)/shard_map/all_gather | solution.py:253
  46.9 0.7 first_products.1
  47.5 1.9 %collective-permute-start = (f32[2,3,64,384]{3,2,1,0:T(8,128)S(1)}, f32[2,3,64,384]{3,2,1,0:T(8,128)S(1)}, u32[]{:S(2)}, u32[]{:S(2)}) collective-permute-start(f32[2,3,64,384]{3,2,1,0:T(8,128)S(1)} %get-tuple-element.12), channel_id=1, source_target_pairs={{0,1},{1,0},{2,3},{3,2},{4,5},{5,4},{6,7},{7,6},{8,9},{9,8},{10,11... | collective-permute-start | bytes 1769480 | tf_op jit(solution)/shard_map/ppermute | solution.py:261
  49.5 2.0 %collective-permute-done = f32[2,3,64,384]{3,2,1,0:T(8,128)S(1)} collective-permute-done((f32[2,3,64,384]{3,2,1,0:T(8,128)S(1)}, f32[2,3,64,384]{3,2,1,0:T(8,128)S(1)}, u32[]{:S(2)}, u32[]{:S(2)}) %collective-permute-start) | collective-permute-done | bytes 589856 | tf_op jit(solution)/shard_map/ppermute | solution.py:261
  51.4 0.1 add.38
  51.5 5.3 %collective-permute-start.3 = (bf16[3,64,384]{2,1,0:T(8,128)(2,1)S(1)}, bf16[3,64,384]{2,1,0:T(8,128)(2,1)S(1)}, u32[]{:S(2)}, u32[]{:S(2)}) collective-permute-start(bf16[3,64,384]{2,1,0:T(8,128)(2,1)S(1)} %get-tuple-element.26), channel_id=1, source_target_pairs={{0,6},{2,4},{4,2},{6,0},{1,7},{3,5},{5,3},{7,1},{8,14},{10,12},{12... | collective-permute-start | bytes 442376 | tf_op jit(solution)/shard_map/ppermute | solution.py:267
  56.8 4.0 %collective-permute-start.1 = (bf16[3,64,384]{2,1,0:T(8,128)(2,1)S(1)}, bf16[3,64,384]{2,1,0:T(8,128)(2,1)S(1)}, u32[]{:S(2)}, u32[]{:S(2)}) collective-permute-start(bf16[3,64,384]{2,1,0:T(8,128)(2,1)S(1)} %get-tuple-element.27), channel_id=1, source_target_pairs={{0,2},{2,0},{4,6},{6,4},{1,3},{3,1},{5,7},{7,5},{8,10},{10,8},{12,... | collective-permute-start | bytes 442376 | tf_op jit(solution)/shard_map/ppermute | solution.py:267
  60.9 3.7 %collective-permute-done.3 = bf16[3,64,384]{2,1,0:T(8,128)(2,1)S(1)} collective-permute-done((bf16[3,64,384]{2,1,0:T(8,128)(2,1)S(1)}, bf16[3,64,384]{2,1,0:T(8,128)(2,1)S(1)}, u32[]{:S(2)}, u32[]{:S(2)}) %collective-permute-start.3) | collective-permute-done | bytes 147488 | tf_op jit(solution)/shard_map/ppermute | solution.py:267
  64.6 3.8 %collective-permute-done.1 = bf16[3,64,384]{2,1,0:T(8,128)(2,1)S(1)} collective-permute-done((bf16[3,64,384]{2,1,0:T(8,128)(2,1)S(1)}, bf16[3,64,384]{2,1,0:T(8,128)(2,1)S(1)}, u32[]{:S(2)}, u32[]{:S(2)}) %collective-permute-start.1) | collective-permute-done | bytes 147488 | tf_op jit(solution)/shard_map/ppermute | solution.py:267
  68.4 0.1 fusion.4
  68.4 4.1 %collective-permute-start.4 = (bf16[3,64,384]{2,1,0:T(8,128)(2,1)S(1)}, bf16[3,64,384]{2,1,0:T(8,128)(2,1)S(1)}, u32[]{:S(2)}, u32[]{:S(2)}) collective-permute-start(bf16[3,64,384]{2,1,0:T(8,128)(2,1)S(1)} %get-tuple-element.24), channel_id=1, source_target_pairs={{0,2},{2,0},{4,6},{6,4},{1,3},{3,1},{5,7},{7,5},{8,10},{10,8},{12,... | collective-permute-start | bytes 442376 | tf_op jit(solution)/shard_map/ppermute | solution.py:267
  72.5 3.1 %collective-permute-start.2 = (bf16[3,64,384]{2,1,0:T(8,128)(2,1)S(1)}, bf16[3,64,384]{2,1,0:T(8,128)(2,1)S(1)}, u32[]{:S(2)}, u32[]{:S(2)}) collective-permute-start(bf16[3,64,384]{2,1,0:T(8,128)(2,1)S(1)} %get-tuple-element.25), channel_id=1, source_target_pairs={{0,6},{2,4},{4,2},{6,0},{1,7},{3,5},{5,3},{7,1},{8,14},{10,12},{12... | collective-permute-start | bytes 442376 | tf_op jit(solution)/shard_map/ppermute | solution.py:267
  75.6 0.9 collective-permute-done.4
  76.5 7.6 %collective-permute-done.2 = bf16[3,64,384]{2,1,0:T(8,128)(2,1)S(1)} collective-permute-done((bf16[3,64,384]{2,1,0:T(8,128)(2,1)S(1)}, bf16[3,64,384]{2,1,0:T(8,128)(2,1)S(1)}, u32[]{:S(2)}, u32[]{:S(2)}) %collective-permute-start.2) | collective-permute-done | bytes 147488 | tf_op jit(solution)/shard_map/ppermute | solution.py:267
  84.1 0.1 convert_add_fusion
  84.5 2.2 %all_gather.7.acts_ref = bf16[2,2,3,64,384]{4,3,2,1,0:T(8,128)(2,1)S(1)} all-gather(bf16[1,2,3,64,384]{4,3,2,1,0:T(8,128)(2,1)S(1)} %bitcast.75), channel_id=1, replica_groups=mesh['branch'=2,'hidden_x'=4,'hidden_z'=12,'width_y'=4,'width_core'=2] {..., dimensions={0}, use_global_device_ids=true | all-gather | bytes 884736 | tf_op jit(solution)/shard_map/all_gather | solution.py:278
  86.7 1.4 %second_products.1 = (bf16[48,2,8,512]{3,2,1,0:T(8,128)(2,1)}, f32[12,2,8,512]{3,2,1,0:T(8,128)S(1)}) custom-call(s32[1]{0:T(128)} %bitcast.1.place_ref, bf16[2,2,3,64,384]{4,3,2,1,0:T(8,128)(2,1)S(1)} %all_gather.7.acts_ref, bf16[512,256]{1,0:T(8,128)(2,1)S(1)} %bitcast.59, bf16[512,256]{1,0:T(8,128)(2,1)S(1)} %bitcast.61, bf16[256,512]{1,0:T(8,128)(2,1)S(1)} %bitcast.63), custom_call_target="tpu_custom_call" | custom-call | tf_op jit(solution)/shard_map/second_products/pallas_call | solution.py:214
  88.2 3.5 %all-to-all-start.1 = ((bf16[4,24,8,512]{3,2,1,0:T(8,128)(2,1)}), bf16[4,24,8,512]{3,2,1,0:T(8,128)(2,1)S(1)}, u32[]{:S(2)}, u32[]{:S(2)}) async-start(bf16[4,24,8,512]{3,2,1,0:T(8,128)(2,1)} %bitcast.16), calls=%async_computation.1 | async-start | bytes 1572864 | tf_op jit(solution)/shard_map/all_to_all | solution.py:287
  91.7 12.8 %all-to-all-done.1 = bf16[4,24,8,512]{3,2,1,0:T(8,128)(2,1)S(1)} async-done(((bf16[4,24,8,512]{3,2,1,0:T(8,128)(2,1)}), bf16[4,24,8,512]{3,2,1,0:T(8,128)(2,1)S(1)}, u32[]{:S(2)}, u32[]{:S(2)}) %all-to-all-start.1) | async-done | bytes 786464 | tf_op jit(solution)/shard_map/all_to_all | solution.py:287
  104.5 0.2 select_reduce_fusion
  104.7 0.7 fusion
  105.5 5.3 %all-to-all-start.2 = ((bf16[24,8,512]{2,1,0:T(8,128)(2,1)}), bf16[24,8,512]{2,1,0:T(8,128)(2,1)S(1)}, u32[]{:S(2)}, u32[]{:S(2)}) async-start(bf16[24,8,512]{2,1,0:T(8,128)(2,1)} %fusion), calls=%async_computation.2 | async-start | bytes 393216 | tf_op jit(solution)/shard_map/all_to_all | solution.py:296
  110.8 0.1 fusion.14
  110.9 1.1 convolution_bitcast_fusion
  112.0 1.1 convolution_bitcast_fusion.2
  113.1 1.1 convolution_bitcast_fusion.1
  114.3 8.7 %all-to-all-done.2.recv_ref = bf16[24,8,512]{2,1,0:T(8,128)(2,1)S(1)} async-done(((bf16[24,8,512]{2,1,0:T(8,128)(2,1)}), bf16[24,8,512]{2,1,0:T(8,128)(2,1)S(1)}, u32[]{:S(2)}, u32[]{:S(2)}) %all-to-all-start.2) | async-done | bytes 196640 | tf_op jit(solution)/shard_map/all_to_all | solution.py:296
  123.0 1.2 finish.1
  (21 shorter events, 0.5 us)
Async XLA Ops:
  2.1 30.0 %all-to-all-start = ((bf16[24,8,512]{2,1,0:T(8,128)(2,1)}), bf16[24,8,512]{2,1,0:T(8,128)(2,1)S(1)}, u32[]{:S(2)}, u32[]{:S(2)}) async-start(bf16[24,8,512]{2,1,0:T(8,128)(2,1)} %bitcast.69), calls=%async_computation | async-start | bytes 393216 | tf_op jit(solution)/shard_map/all_to_all | solution.py:249
  32.4 14.5 %copy-start = (bf16[1,512,256]{2,1,0:T(8,128)(2,1)S(1)}, bf16[1,512,256]{2,1,0:T(8,128)(2,1)}, u32[]{:S(2)}) copy-start(bf16[1,512,256]{2,1,0:T(8,128)(2,1)} %param.11) | copy-start | bytes 786436
  32.4 14.5 %copy-start.1 = (bf16[1,512,256]{2,1,0:T(8,128)(2,1)S(1)}, bf16[1,512,256]{2,1,0:T(8,128)(2,1)}, u32[]{:S(2)}) copy-start(bf16[1,512,256]{2,1,0:T(8,128)(2,1)} %param.12) | copy-start | bytes 786436
  32.4 14.4 %copy-start.2 = (bf16[1,256,512]{2,1,0:T(8,128)(2,1)S(1)}, bf16[1,256,512]{2,1,0:T(8,128)(2,1)}, u32[]{:S(2)}) copy-start(bf16[1,256,512]{2,1,0:T(8,128)(2,1)} %param.13) | copy-start | bytes 786436
  47.5 3.9 %collective-permute-start = (f32[2,3,64,384]{3,2,1,0:T(8,128)S(1)}, f32[2,3,64,384]{3,2,1,0:T(8,128)S(1)}, u32[]{:S(2)}, u32[]{:S(2)}) collective-permute-start(f32[2,3,64,384]{3,2,1,0:T(8,128)S(1)} %get-tuple-element.12), channel_id=1, source_target_pairs={{0,1},{1,0},{2,3},{3,2},{4,5},{5,4},{6,7},{7,6},{8,9},{9,8},{10,11... | collective-permute-start | bytes 1769480 | tf_op jit(solution)/shard_map/ppermute | solution.py:261
  51.5 13.1 %collective-permute-start.3 = (bf16[3,64,384]{2,1,0:T(8,128)(2,1)S(1)}, bf16[3,64,384]{2,1,0:T(8,128)(2,1)S(1)}, u32[]{:S(2)}, u32[]{:S(2)}) collective-permute-start(bf16[3,64,384]{2,1,0:T(8,128)(2,1)S(1)} %get-tuple-element.26), channel_id=1, source_target_pairs={{0,6},{2,4},{4,2},{6,0},{1,7},{3,5},{5,3},{7,1},{8,14},{10,12},{12... | collective-permute-start | bytes 442376 | tf_op jit(solution)/shard_map/ppermute | solution.py:267
  56.8 11.6 %collective-permute-start.1 = (bf16[3,64,384]{2,1,0:T(8,128)(2,1)S(1)}, bf16[3,64,384]{2,1,0:T(8,128)(2,1)S(1)}, u32[]{:S(2)}, u32[]{:S(2)}) collective-permute-start(bf16[3,64,384]{2,1,0:T(8,128)(2,1)S(1)} %get-tuple-element.27), channel_id=1, source_target_pairs={{0,2},{2,0},{4,6},{6,4},{1,3},{3,1},{5,7},{7,5},{8,10},{10,8},{12,... | collective-permute-start | bytes 442376 | tf_op jit(solution)/shard_map/ppermute | solution.py:267
  68.4 8.1 %collective-permute-start.4 = (bf16[3,64,384]{2,1,0:T(8,128)(2,1)S(1)}, bf16[3,64,384]{2,1,0:T(8,128)(2,1)S(1)}, u32[]{:S(2)}, u32[]{:S(2)}) collective-permute-start(bf16[3,64,384]{2,1,0:T(8,128)(2,1)S(1)} %get-tuple-element.24), channel_id=1, source_target_pairs={{0,2},{2,0},{4,6},{6,4},{1,3},{3,1},{5,7},{7,5},{8,10},{10,8},{12,... | collective-permute-start | bytes 442376 | tf_op jit(solution)/shard_map/ppermute | solution.py:267
  72.5 11.6 %collective-permute-start.2 = (bf16[3,64,384]{2,1,0:T(8,128)(2,1)S(1)}, bf16[3,64,384]{2,1,0:T(8,128)(2,1)S(1)}, u32[]{:S(2)}, u32[]{:S(2)}) collective-permute-start(bf16[3,64,384]{2,1,0:T(8,128)(2,1)S(1)} %get-tuple-element.25), channel_id=1, source_target_pairs={{0,6},{2,4},{4,2},{6,0},{1,7},{3,5},{5,3},{7,1},{8,14},{10,12},{12... | collective-permute-start | bytes 442376 | tf_op jit(solution)/shard_map/ppermute | solution.py:267
  88.2 16.3 %all-to-all-start.1 = ((bf16[4,24,8,512]{3,2,1,0:T(8,128)(2,1)}), bf16[4,24,8,512]{3,2,1,0:T(8,128)(2,1)S(1)}, u32[]{:S(2)}, u32[]{:S(2)}) async-start(bf16[4,24,8,512]{3,2,1,0:T(8,128)(2,1)} %bitcast.16), calls=%async_computation.1 | async-start | bytes 1572864 | tf_op jit(solution)/shard_map/all_to_all | solution.py:287
  105.5 17.5 %all-to-all-start.2 = ((bf16[24,8,512]{2,1,0:T(8,128)(2,1)}), bf16[24,8,512]{2,1,0:T(8,128)(2,1)S(1)}, u32[]{:S(2)}, u32[]{:S(2)}) async-start(bf16[24,8,512]{2,1,0:T(8,128)(2,1)} %fusion), calls=%async_computation.2 | async-start | bytes 393216 | tf_op jit(solution)/shard_map/all_to_all | solution.py:296
  113.1 9.9 %copy-start.3 = (s32[2,3]{1,0:T(2,128)S(1)}, s32[2,3]{1,0:T(2,128)}, u32[]{:S(2)}) copy-start(s32[2,3]{1,0:T(2,128)} %labels_ref.1) | copy-start | bytes 76
  113.1 9.9 %copy-start.4 = (s32[2,1]{0,1:T(1,128)S(1)}, s32[2,1]{0,1:T(1,128)}, u32[]{:S(2)}) copy-start(s32[2,1]{0,1:T(1,128)} %param.10) | copy-start | bytes 28
